TPU v7x, 256 devices: a whole 4x4x8 slice. The times are simulated.
256 devices in a mesh: row: 16 (over x_hi, z), col: 16 (over x_lo, y, core).
Axes of the slice: x: 4 (x_hi: 2, x_lo: 2; x = x_hi * 2 + x_lo), y: 4, z: 8, core: 2. Of those that a mesh axis runs over, the one named last changes fastest.
Arguments:
- tokens: bfloat16 [6016, 8192], P('row', 'col'), may hold values from -6 to 6
- weight: bfloat16 [8192, 26624], P('row', 'col'), may hold values from -0.0625 to 0.0625
Outputs:
- activated: bfloat16 [6016, 26624], P('row', 'col')
All inputs are finite; a program needn't handle non-finite values.
Results may differ from a plain program's by a relative error of at most 0.001.
Values may be sent and summed in bfloat16 or wider, within the bound.
No kernel may reach another device: no remote copies, remote signals or barrier semaphores. Data moves between devices by JAX's collectives and lax.ppermute only.
A program may use at most 128 MiB of HBM per device.

v0:
```python
import jax
import jax.numpy as jnp
from jax import lax
from jax.sharding import PartitionSpec as P


def on_device(tokens, weight):
    whole_weight = lax.all_gather(weight, "row", axis=0, tiled=True)
    preact = jnp.dot(
        lax.all_gather(tokens, "col", axis=1, tiled=True),
        whole_weight,
        preferred_element_type=jnp.float32,
    )
    return jax.nn.silu(preact).astype(jnp.bfloat16)


def solution(mesh):
    placed = (P("row", "col"), P("row", "col"))
    return jax.shard_map(
        on_device, mesh=mesh, in_specs=placed, out_specs=P("row", "col"), check_vma=False
    )
```

profile of v0, /device:TPU:1, one launch (start us, length us, event | category | flops | bytes accessed | tf_op | source)
XLA Modules:
  0.0 428.8 jit_solution(3382763551147418032)
XLA Ops:
  6.5 0.0 all-gather.3.cloned.1.call-start
  6.5 0.7 all-gather.3.cloned.1.call-update
  7.3 0.0 all-gather.5.cloned.1.call-start
  7.3 0.7 all-gather.5.cloned.1.call-update
  8.0 49.8 %all-gather.3.cloned.1.call-done = bf16[376,8192]{1,0:T(8,128)(2,1)} async-done(((bf16[376,512]{1,0:T(8,128)(2,1)}), bf16[376,8192]{1,0:T(8,128)(2,1)}) %all-gather.3.cloned.1.call-update) | async-done | bytes 6160400 | tf_op jit(solution)/shard_map/all_gather | solution.py:10
  57.8 345.2 %all-gather.5.cloned.1.call-done = bf16[8192,1664]{1,0:T(8,128)(2,1)} async-done(((bf16[512,1664]{1,0:T(8,128)(2,1)}), bf16[8192,1664]{1,0:T(8,128)(2,1)}) %all-gather.5.cloned.1.call-update) | async-done | bytes 27262992 | tf_op jit(solution)/shard_map/all_gather | solution.py:8
  403.0 19.0 %multiply_convert_fusion = bf16[376,1664]{1,0:T(8,128)(2,1)} fusion(bf16[376,8192]{1,0:T(8,128)(2,1)} %all-gather.3.cloned.1.call-done, bf16[8192,1664]{1,0:T(8,128)(2,1)} %all-gather.5.cloned.1.call-done), kind=kOutput, calls=%fused_computation | convolution fusion | flops 10254007296 | bytes 34674688 | tf_op jit(solution)/shard_map/dot_general | solution.py:9
Async XLA Ops:
  6.5 51.2 %all-gather.3.cloned.1.call-start = ((), (), s32[]{:S(2)}) async-start(), calls=%async_computation | async-start | bytes 6545408 | tf_op jit(solution)/shard_map/all_gather | solution.py:10
  7.3 395.7 %all-gather.5.cloned.1.call-start = ((), (), s32[]{:S(2)}) async-start(), calls=%async_computation.1 | async-start | bytes 28966912 | tf_op jit(solution)/shard_map/all_gather | solution.py:8
Sparse Core Ops, SparseCore 0:
  9.2 48.5 all-gather.2
  60.4 342.5 all-gather.4
where the time goes:
time: 429 us
  waiting for transfers between devices  396 us (92%)
  matrix products  19 us (4%)
  between operations  13.4 us (3%)
    all_gather x1, waiting for transfers between devices, on_device(): whole_weight = lax.all_gather(weight, 'row', axis=0, tiled=True)  345 us
    all_gather x1, waiting for transfers between devices, on_device(): lax.all_gather(tokens, 'col', axis=1, tiled=True)  49.8 us
    dot_general x1, matrix products, on_device(): jnp.dot(lax.all_gather(tokens, 'col', axis=1, tiled=True), whole_weight,...  19 us
  transfers between devices with their start and end apart: 2, of which 2 were waited for; matrix products, arithmetic and copies ran while one was open for 0% of the time, Pallas kernels for 0%

commit v1 on v0

v1 whole, which is shorter than its diff:
```python
import jax
import jax.numpy as jnp
from jax import lax
from jax.sharding import Mesh, PartitionSpec as P

AXES = ("xh", "z", "xl", "y", "core")
SIZES = (2, 8, 2, 4, 2)
WIDTHS = (256, 640, 512, 256)


def exchange(value, axis, flip, size):
    return lax.ppermute(value, axis, [(i, i ^ flip) for i in range(size)])


def swap_if(flag, first, second):
    return jnp.where(flag, second, first), jnp.where(flag, first, second)


def gather_tokens(tokens):
    xh, xl, y, core = (lax.axis_index(name) for name in ("xh", "xl", "y", "core"))
    rows, features = tokens.shape
    half = features // 2
    mine, other = swap_if(core == 1, tokens[:, :half], tokens[:, half:])
    received = exchange(other, "core", 1, 2)
    block = jnp.concatenate(swap_if(core == 1, mine, received), axis=1)
    here = block
    beside = exchange(block, ("xh", "xl"), 1, 4)
    across = exchange(block, ("xh", "xl"), 2, 4)
    corner = exchange(block, ("xh", "xl"), 3, 4)
    flip_l = xl != core
    low = swap_if(flip_l, here, beside)
    high = swap_if(flip_l, across, corner)
    flip_h = xh != core
    firsts = swap_if(flip_h, low[0], high[0])
    seconds = swap_if(flip_h, low[1], high[1])
    pieces = []
    for first, second in zip(firsts, seconds):
        pieces.append(
            jnp.concatenate(
                [first[:, :half], second[:, :half], first[:, half:], second[:, half:]], axis=1
            )
        )
    piece = jnp.concatenate(pieces, axis=0)
    width = piece.shape[1]
    out = [jnp.zeros((rows, 4 * width), tokens.dtype) for _ in range(2)]
    for d in range(4):
        arrived = piece if d == 0 else exchange(piece, "y", d, 4)
        for e in range(2):
            out[e] = lax.dynamic_update_slice(
                out[e], arrived[e * rows : (e + 1) * rows], (0, (y ^ d) * width)
            )
    return out


TURN = [(h * 2 + c, c * 2 + h) for h in range(2) for c in range(2)]
CROSS = [(h * 2 + c, c * 2 + 1 - h) for h in range(2) for c in range(2)]


def on_device(tokens, weight):
    xh = lax.axis_index("xh")
    half = weight.shape[0] // 2
    keep, give = gather_tokens(tokens)
    at = 0
    mines = []
    for width in WIDTHS:
        part = weight[:, at : at + width]
        at += width
        if mines:
            part, mines[-1] = lax.optimization_barrier((part, mines[-1]))
        first, second = swap_if(xh == 1, part[:half], part[half:])
        mines.append(
            jnp.concatenate(
                [
                    lax.ppermute(first, ("xh", "core"), TURN),
                    lax.ppermute(second, ("xh", "core"), CROSS),
                ]
            )
        )
    outs = []
    out = None
    for mine in mines:
        whole = lax.all_gather(mine, "z", axis=0, tiled=True)
        if out is not None:
            whole, out = lax.optimization_barrier((whole, out))
            outs.append(lax.ppermute(out, ("xh", "core"), TURN))
        given = jnp.dot(give, whole, preferred_element_type=jnp.float32)
        kept = jnp.dot(keep, whole, preferred_element_type=jnp.float32)
        total = kept + exchange(given, "core", 1, 2)
        out = jax.nn.silu(total).astype(jnp.bfloat16)
    outs.append(lax.ppermute(out, ("xh", "core"), TURN))
    return jnp.concatenate(outs, axis=1)


def solution(mesh):
    fine = Mesh(mesh.devices.reshape(SIZES), AXES)
    placed = P(("xh", "z"), ("xl", "y", "core"))
    return jax.shard_map(
        on_device, mesh=fine, in_specs=(placed, placed), out_specs=placed, check_vma=False
    )
```

time: 429 us -> 259 us (0.60)
  waiting for transfers between devices: 396 us -> 134 us
  starting transfers between devices: 0.04 us -> 51.4 us
  other arithmetic: 0 us -> 18 us
  matrix products: 19 us -> 30.2 us
  local copies, waits for them, and re-layouts: 0 us -> 10.7 us
    all_gather x2 -> x4, waiting for transfers between devices: 395 us -> 31.3 us  [on_device(): whole = lax.all_gather(mine, 'z', axis=0, tiled=True)]
    ppermute x0 -> x23, waiting for transfers between devices: none -> 103 us  [the longest x11 80.4 us: exchange(): return lax.ppermute(value, axis, [(i, i ^ flip) for i in range(size)])]
    ppermute x0 -> x23, starting transfers between devices: none -> 51.2 us  [the longest x11 19.4 us: exchange(): return lax.ppermute(value, axis, [(i, i ^ flip) for i in range(size)])]
    concatenate x0 -> x7, other arithmetic: none -> 14.7 us  [the longest x1 10.3 us: gather_tokens(): piece = jnp.concatenate(pieces, axis=0)]
    dot_general x1 -> x8, matrix products: 19 us -> 30.2 us  [the longest x4 19.3 us: on_device(): given = jnp.dot(give, whole, preferred_element_type=jnp.float32)]
    dynamic_update_slice x0 -> x3, local copies, waits for them, and re-layouts: none -> 7.38 us  [gather_tokens(): lax.dynamic_update_slice(out[e], arrived[e * rows:(e + 1) * rows], (0, (y...]
  transfers between devices with their start and end apart: 2 -> 27, of which waited for: 2 -> 18; matrix products, arithmetic and copies ran while one was open for 0% -> 20% of each run, Pallas kernels for 0% -> 0%
where the time goes in v1:
time: 259 us; the launch traced here: 258 us
  waiting for transfers between devices  134 us (52%)
  starting transfers between devices  51.4 us (20%)
  matrix products  30.2 us (12%)
  other arithmetic  18 us (7%)
  between operations  13.5 us (5%)
  local copies, waits for them, and re-layouts  10.7 us (4%)
    ppermute x11, waiting for transfers between devices, exchange(): return lax.ppermute(value, axis, [(i, i ^ flip) for i in range(size)])  80.4 us
    all_gather x4, waiting for transfers between devices, on_device(): whole = lax.all_gather(mine, 'z', axis=0, tiled=True)  31.3 us
    ppermute x11, starting transfers between devices, exchange(): return lax.ppermute(value, axis, [(i, i ^ flip) for i in range(size)])  19.4 us
    dot_general x4, matrix products, on_device(): given = jnp.dot(give, whole, preferred_element_type=jnp.float32)  19.3 us
    ppermute x4, starting transfers between devices, on_device(): lax.ppermute(first, ('xh', 'core'), TURN)  16.4 us
    ppermute x4, starting transfers between devices, on_device(): outs.append(lax.ppermute(out, ('xh', 'core'), TURN))  14.1 us
    ppermute x4, waiting for transfers between devices, on_device(): lax.ppermute(first, ('xh', 'core'), TURN)  12.8 us
    dot_general x4, matrix products, on_device(): kept = jnp.dot(keep, whole, preferred_element_type=jnp.float32)  10.9 us
  transfers between devices with their start and end apart: 27, of which 18 were waited for; matrix products, arithmetic and copies ran while one was open for 20% of the time, Pallas kernels for 0%

profile of v1, /device:TPU:1, one launch (start us, length us, event | category | flops | bytes accessed | tf_op | source)
XLA Modules:
  0.0 258.1 jit_solution(8508668689851486958)
XLA Ops:
  7.6 6.0 %collective-permute-start = (bf16[256,256]{1,0:T(8,128)(2,1)S(1)}, bf16[256,256]{1,0:T(8,128)(2,1)S(1)}, u32[]{:S(2)}, u32[]{:S(2)}) collective-permute-start(bf16[256,256]{1,0:T(8,128)(2,1)S(1)} %get-tuple-element.29), channel_id=1, source_target_pairs={{0,0},{1,128},{128,1},{129,129},{2,2},{3,130},{130,3},{131,131},{4... | collective-permute-start | bytes 393224 | tf_op jit(solution)/shard_map/ppermute | solution.py:74
  17.8 4.5 %collective-permute-start.2 = (bf16[256,640]{1,0:T(8,128)(2,1)S(1)}, bf16[256,640]{1,0:T(8,128)(2,1)S(1)}, u32[]{:S(2)}, u32[]{:S(2)}) collective-permute-start(bf16[256,640]{1,0:T(8,128)(2,1)S(1)} %get-tuple-element.41), channel_id=1, source_target_pairs={{0,0},{1,128},{128,1},{129,129},{2,2},{3,130},{130,3},{131,131},{4... | collective-permute-start | bytes 983048 | tf_op jit(solution)/shard_map/ppermute | solution.py:74
  22.5 5.3 %collective-permute-done.2 = bf16[256,640]{1,0:T(8,128)(2,1)S(1)} collective-permute-done((bf16[256,640]{1,0:T(8,128)(2,1)S(1)}, bf16[256,640]{1,0:T(8,128)(2,1)S(1)}, u32[]{:S(2)}, u32[]{:S(2)}) %collective-permute-start.2) | collective-permute-done | bytes 327712 | tf_op jit(solution)/shard_map/ppermute | solution.py:74
  30.9 3.1 %collective-permute-start.13 = (bf16[256,512]{1,0:T(8,128)(2,1)S(1)}, bf16[256,512]{1,0:T(8,128)(2,1)S(1)}, u32[]{:S(2)}, u32[]{:S(2)}) collective-permute-start(bf16[256,512]{1,0:T(8,128)(2,1)S(1)} %get-tuple-element.45), channel_id=1, source_target_pairs={{0,0},{1,128},{128,1},{129,129},{2,2},{3,130},{130,3},{131,131},{4... | collective-permute-start | bytes 786440 | tf_op jit(solution)/shard_map/ppermute | solution.py:74
  35.1 5.0 %collective-permute-done.13 = bf16[256,512]{1,0:T(8,128)(2,1)S(1)} collective-permute-done((bf16[256,512]{1,0:T(8,128)(2,1)S(1)}, bf16[256,512]{1,0:T(8,128)(2,1)S(1)}, u32[]{:S(2)}, u32[]{:S(2)}) %collective-permute-start.13) | collective-permute-done | bytes 262176 | tf_op jit(solution)/shard_map/ppermute | solution.py:74
  41.1 3.5 %collective-permute-start.4 = (bf16[376,256]{1,0:T(8,128)(2,1)S(1)}, bf16[376,256]{1,0:T(8,128)(2,1)S(1)}, u32[]{:S(2)}, u32[]{:S(2)}) collective-permute-start(bf16[376,256]{1,0:T(8,128)(2,1)S(1)} %broadcast_select_fusion.15), channel_id=1, source_target_pairs={{0,1},{1,0},{2,3},{3,2},{4,5},{5,4},{6,7},{7,6},{8,9},{9,8},{10,11... | collective-permute-start | bytes 577544 | tf_op jit(solution)/shard_map/ppermute | solution.py:12
  49.1 16.5 %collective-permute-done.5 = bf16[376,512]{1,0:T(8,128)(2,1)S(1)} collective-permute-done((bf16[376,512]{1,0:T(8,128)(2,1)S(1)}, bf16[376,512]{1,0:T(8,128)(2,1)S(1)}, u32[]{:S(2)}, u32[]{:S(2)}) %collective-permute-start.5) | collective-permute-done | bytes 385056 | tf_op jit(solution)/shard_map/ppermute | solution.py:12
  66.4 10.3 %maximum_maximum_fusion = bf16[752,1024]{1,0:T(8,128)(2,1)} fusion(bf16[376,256]{1,0:T(8,128)(2,1)S(1)} %get-tuple-element.59, bf16[376,256]{1,0:T(8,128)(2,1)S(1)} %get-tuple-element.52, bf16[376,256]{1,0:T(8,128)(2,1)S(1)} %get-tuple-element.60, bf16[376,256]{1,0:T(8,128)(2,1)S(1)} %get-tuple-element.51, bf16[376,256]{1,0:T(8,128)(2,1)S(1)} %get-tuple-element.57, ...), kind=kLoop, calls=%fused_computation | loop fusion | flops 12320768 | bytes 3080192 | tf_op jit(solution)/shard_map/concatenate | solution.py:43
  77.9 2.6 %collective-permute-start.9 = (bf16[752,1024]{1,0:T(8,128)(2,1)}, bf16[752,1024]{1,0:T(8,128)(2,1)}, u32[]{:S(2)}, u32[]{:S(2)}) collective-permute-start(bf16[752,1024]{1,0:T(8,128)(2,1)} %maximum_maximum_fusion), channel_id=1, source_target_pairs={{0,4},{2,6},{4,0},{6,2},{1,5},{3,7},{5,1},{7,3},{8,12},{10,14},{12... | collective-permute-start | bytes 4620296 | tf_op jit(solution)/shard_map/ppermute | solution.py:12
  84.8 25.9 %collective-permute-done.8 = bf16[752,1024]{1,0:T(8,128)(2,1)} collective-permute-done((bf16[752,1024]{1,0:T(8,128)(2,1)}, bf16[752,1024]{1,0:T(8,128)(2,1)}, u32[]{:S(2)}, u32[]{:S(2)}) %collective-permute-start.8) | collective-permute-done | bytes 1540128 | tf_op jit(solution)/shard_map/ppermute | solution.py:12
  113.1 33.0 %collective-permute-done.9 = bf16[752,1024]{1,0:T(8,128)(2,1)} collective-permute-done((bf16[752,1024]{1,0:T(8,128)(2,1)}, bf16[752,1024]{1,0:T(8,128)(2,1)}, u32[]{:S(2)}, u32[]{:S(2)}) %collective-permute-start.9) | collective-permute-done | bytes 1540128 | tf_op jit(solution)/shard_map/ppermute | solution.py:12
  151.1 3.7 %fusion.4 = f32[376,256]{1,0:T(8,128)S(1)} fusion(bf16[376,4096]{1,0:T(8,128)(2,1)} %get-tuple-element.32, bf16[4096,256]{1,0:T(8,128)(2,1)} %all-gather.7.cloned.1.call-done), kind=kOutput, calls=%fused_computation.47 | convolution fusion | flops 788529152 | bytes 5562368 | tf_op jit(solution)/shard_map/dot_general | solution.py:86
  154.8 2.6 %collective-permute-start.11 = (f32[376,256]{1,0:T(8,128)S(1)}, f32[376,256]{1,0:T(8,128)S(1)}, u32[]{:S(2)}, u32[]{:S(2)}) collective-permute-start(f32[376,256]{1,0:T(8,128)S(1)} %fusion.4), channel_id=1, source_target_pairs={{0,1},{1,0},{2,3},{3,2},{4,5},{5,4},{6,7},{7,6},{8,9},{9,8},{10,11... | collective-permute-start | bytes 1155080 | tf_op jit(solution)/shard_map/ppermute | solution.py:12
  158.1 2.8 %collective-permute-start.17 = (bf16[256,256]{1,0:T(8,128)(2,1)}, bf16[256,256]{1,0:T(8,128)(2,1)S(1)}, u32[]{:S(2)}, u32[]{:S(2)}) collective-permute-start(bf16[256,256]{1,0:T(8,128)(2,1)} %get-tuple-element.55), channel_id=1, source_target_pairs={{0,0},{1,128},{128,1},{129,129},{2,2},{3,130},{130,3},{131,131},{4... | collective-permute-start | bytes 393224 | tf_op jit(solution)/shard_map/ppermute | solution.py:74
  162.8 7.0 %fusion.5 = f32[376,640]{1,0:T(8,128)} fusion(bf16[376,4096]{1,0:T(8,128)(2,1)} %get-tuple-element.32, bf16[4096,640]{1,0:T(8,128)(2,1)} %all-gather.5.cloned.1.call-done), kind=kOutput, calls=%fused_computation.48 | convolution fusion | flops 1971322880 | bytes 9285632 | tf_op jit(solution)/shard_map/dot_general | solution.py:86
  172.7 6.2 %multiply_convert_fusion = bf16[376,640]{1,0:T(8,128)(2,1)} fusion(f32[376,640]{1,0:T(8,128)} %collective-permute-done.15, bf16[376,4096]{1,0:T(8,128)(2,1)S(1)} %get-tuple-element.31, bf16[4096,640]{1,0:T(8,128)(2,1)} %all-gather.5.cloned.1.call-done), kind=kOutput, calls=%fused_computation.6 | convolution fusion | flops 1972766720 | bytes 9766912 | tf_op jit(solution)/shard_map/dot_general | solution.py:87
  178.9 3.4 %all-gather.9.cloned.1.call-done = bf16[4096,512]{1,0:T(8,128)(2,1)} async-done(((bf16[512,512]{1,0:T(8,128)(2,1)}), bf16[4096,512]{1,0:T(8,128)(2,1)}) %all-gather.9.cloned.1.call-update) | async-done | bytes 4194320 | tf_op jit(solution)/shard_map/all_gather | solution.py:82
  182.4 5.0 %fusion.6 = f32[376,512]{1,0:T(8,128)S(1)} fusion(bf16[376,4096]{1,0:T(8,128)(2,1)} %get-tuple-element.32, bf16[4096,512]{1,0:T(8,128)(2,1)} %all-gather.9.cloned.1.call-done), kind=kOutput, calls=%fused_computation.49 | convolution fusion | flops 1577058304 | bytes 8044544 | tf_op jit(solution)/shard_map/dot_general | solution.py:86
  192.1 27.9 %all-gather.11.cloned.1.call-done = bf16[4096,256]{1,0:T(8,128)(2,1)} async-done(((bf16[512,256]{1,0:T(8,128)(2,1)}), bf16[4096,256]{1,0:T(8,128)(2,1)}) %all-gather.11.cloned.1.call-update) | async-done | bytes 2097168 | tf_op jit(solution)/shard_map/all_gather | solution.py:82
  220.1 3.6 %fusion.7 = f32[376,256]{1,0:T(8,128)S(1)} fusion(bf16[376,4096]{1,0:T(8,128)(2,1)} %get-tuple-element.32, bf16[4096,256]{1,0:T(8,128)(2,1)} %all-gather.11.cloned.1.call-done), kind=kOutput, calls=%fused_computation.50 | convolution fusion | flops 788529152 | bytes 5562368 | tf_op jit(solution)/shard_map/dot_general | solution.py:86
  223.7 4.5 %collective-permute-start.21 = (f32[376,256]{1,0:T(8,128)S(1)}, f32[376,256]{1,0:T(8,128)S(1)}, u32[]{:S(2)}, u32[]{:S(2)}) collective-permute-start(f32[376,256]{1,0:T(8,128)S(1)} %fusion.7), channel_id=1, source_target_pairs={{0,1},{1,0},{2,3},{3,2},{4,5},{5,4},{6,7},{7,6},{8,9},{9,8},{10,11... | collective-permute-start | bytes 1155080 | tf_op jit(solution)/shard_map/ppermute | solution.py:12
  228.2 4.5 %collective-permute-start.12 = (bf16[376,256]{1,0:T(8,128)(2,1)S(1)}, bf16[376,256]{1,0:T(8,128)(2,1)S(1)}, u32[]{:S(2)}, u32[]{:S(2)}) collective-permute-start(bf16[376,256]{1,0:T(8,128)(2,1)S(1)} %copy-done.9), channel_id=1, source_target_pairs={{0,0},{1,128},{128,1},{129,129},{2,2},{3,130},{130,3},{131,131},{4... | collective-permute-start | bytes 577544 | tf_op jit(solution)/shard_map/ppermute | solution.py:85
  235.3 4.5 %collective-permute-start.20 = (bf16[376,512]{1,0:T(8,128)(2,1)S(1)}, bf16[376,512]{1,0:T(8,128)(2,1)S(1)}, u32[]{:S(2)}, u32[]{:S(2)}) collective-permute-start(bf16[376,512]{1,0:T(8,128)(2,1)S(1)} %multiply_convert_fusion.1), channel_id=1, source_target_pairs={{0,0},{1,128},{128,1},{129,129},{2,2},{3,130},{130,3},{131,131},{4... | collective-permute-start | bytes 1155080 | tf_op jit(solution)/shard_map/ppermute | solution.py:85
  244.3 4.1 %collective-permute-done.20 = bf16[376,512]{1,0:T(8,128)(2,1)S(1)} collective-permute-done((bf16[376,512]{1,0:T(8,128)(2,1)S(1)}, bf16[376,512]{1,0:T(8,128)(2,1)S(1)}, u32[]{:S(2)}, u32[]{:S(2)}) %collective-permute-start.20) | collective-permute-done | bytes 385056 | tf_op jit(solution)/shard_map/ppermute | solution.py:85
  (91 shorter events, 48.9 us)
Async XLA Ops:
  6.5 144.6 %all-gather.7.cloned.1.call-start = ((), (), s32[]{:S(2)}) async-start(), calls=%async_computation.1 | async-start | bytes 2359296 | tf_op jit(solution)/shard_map/all_gather | solution.py:82
  7.6 8.7 %collective-permute-start = (bf16[256,256]{1,0:T(8,128)(2,1)S(1)}, bf16[256,256]{1,0:T(8,128)(2,1)S(1)}, u32[]{:S(2)}, u32[]{:S(2)}) collective-permute-start(bf16[256,256]{1,0:T(8,128)(2,1)S(1)} %get-tuple-element.29), channel_id=1, source_target_pairs={{0,0},{1,128},{128,1},{129,129},{2,2},{3,130},{130,3},{131,131},{4... | collective-permute-start | bytes 393224 | tf_op jit(solution)/shard_map/ppermute | solution.py:74
  17.7 145.0 %all-gather.5.cloned.1.call-start = ((), (), s32[]{:S(2)}) async-start(), calls=%async_computation | async-start | bytes 5898240 | tf_op jit(solution)/shard_map/all_gather | solution.py:82
  17.8 9.9 %collective-permute-start.2 = (bf16[256,640]{1,0:T(8,128)(2,1)S(1)}, bf16[256,640]{1,0:T(8,128)(2,1)S(1)}, u32[]{:S(2)}, u32[]{:S(2)}) collective-permute-start(bf16[256,640]{1,0:T(8,128)(2,1)S(1)} %get-tuple-element.41), channel_id=1, source_target_pairs={{0,0},{1,128},{128,1},{129,129},{2,2},{3,130},{130,3},{131,131},{4... | collective-permute-start | bytes 983048 | tf_op jit(solution)/shard_map/ppermute | solution.py:74
  22.4 7.5 %collective-permute-start.3 = (bf16[256,640]{1,0:T(8,128)(2,1)S(1)}, bf16[256,640]{1,0:T(8,128)(2,1)S(1)}, u32[]{:S(2)}, u32[]{:S(2)}) collective-permute-start(bf16[256,640]{1,0:T(8,128)(2,1)S(1)} %get-tuple-element.42), channel_id=1, source_target_pairs={{0,1},{1,129},{128,0},{129,128},{2,3},{3,131},{130,2},{131,130},{4... | collective-permute-start | bytes 983048 | tf_op jit(solution)/shard_map/ppermute | solution.py:75
  30.8 151.6 %all-gather.9.cloned.1.call-start = ((), (), s32[]{:S(2)}) async-start(), calls=%async_computation.2 | async-start | bytes 4718592 | tf_op jit(solution)/shard_map/all_gather | solution.py:82
  30.9 9.2 %collective-permute-start.13 = (bf16[256,512]{1,0:T(8,128)(2,1)S(1)}, bf16[256,512]{1,0:T(8,128)(2,1)S(1)}, u32[]{:S(2)}, u32[]{:S(2)}) collective-permute-start(bf16[256,512]{1,0:T(8,128)(2,1)S(1)} %get-tuple-element.45), channel_id=1, source_target_pairs={{0,0},{1,128},{128,1},{129,129},{2,2},{3,130},{130,3},{131,131},{4... | collective-permute-start | bytes 786440 | tf_op jit(solution)/shard_map/ppermute | solution.py:74
  34.0 6.1 %collective-permute-start.14 = (bf16[256,512]{1,0:T(8,128)(2,1)S(1)}, bf16[256,512]{1,0:T(8,128)(2,1)S(1)}, u32[]{:S(2)}, u32[]{:S(2)}) collective-permute-start(bf16[256,512]{1,0:T(8,128)(2,1)S(1)} %get-tuple-element.46), channel_id=1, source_target_pairs={{0,1},{1,129},{128,0},{129,128},{2,3},{3,131},{130,2},{131,130},{4... | collective-permute-start | bytes 786440 | tf_op jit(solution)/shard_map/ppermute | solution.py:75
  41.0 179.0 %all-gather.11.cloned.1.call-start = ((), (), s32[]{:S(2)}) async-start(), calls=%async_computation.3 | async-start | bytes 2359296 | tf_op jit(solution)/shard_map/all_gather | solution.py:82
  41.1 4.6 %collective-permute-start.4 = (bf16[376,256]{1,0:T(8,128)(2,1)S(1)}, bf16[376,256]{1,0:T(8,128)(2,1)S(1)}, u32[]{:S(2)}, u32[]{:S(2)}) collective-permute-start(bf16[376,256]{1,0:T(8,128)(2,1)S(1)} %broadcast_select_fusion.15), channel_id=1, source_target_pairs={{0,1},{1,0},{2,3},{3,2},{4,5},{5,4},{6,7},{7,6},{8,9},{9,8},{10,11... | collective-permute-start | bytes 577544 | tf_op jit(solution)/shard_map/ppermute | solution.py:12
  45.8 19.9 %collective-permute-start.5 = (bf16[376,512]{1,0:T(8,128)(2,1)S(1)}, bf16[376,512]{1,0:T(8,128)(2,1)S(1)}, u32[]{:S(2)}, u32[]{:S(2)}) collective-permute-start(bf16[376,512]{1,0:T(8,128)(2,1)S(1)} %pad_maximum_fusion.3), channel_id=1, source_target_pairs={{0,136},{8,128},{128,8},{136,0},{1,137},{9,129},{129,9},{137,1},{2... | collective-permute-start | bytes 1155080 | tf_op jit(solution)/shard_map/ppermute | solution.py:12
  46.1 19.5 %collective-permute-start.6 = (bf16[376,512]{1,0:T(8,128)(2,1)S(1)}, bf16[376,512]{1,0:T(8,128)(2,1)S(1)}, u32[]{:S(2)}, u32[]{:S(2)}) collective-permute-start(bf16[376,512]{1,0:T(8,128)(2,1)S(1)} %pad_maximum_fusion.3), channel_id=1, source_target_pairs={{0,128},{8,136},{128,0},{136,8},{1,129},{9,137},{129,1},{137,9},{2... | collective-permute-start | bytes 1155080 | tf_op jit(solution)/shard_map/ppermute | solution.py:12
  48.0 17.9 %collective-permute-start.7 = (bf16[376,512]{1,0:T(8,128)(2,1)S(1)}, bf16[376,512]{1,0:T(8,128)(2,1)S(1)}, u32[]{:S(2)}, u32[]{:S(2)}) collective-permute-start(bf16[376,512]{1,0:T(8,128)(2,1)S(1)} %pad_maximum_fusion.3), channel_id=1, source_target_pairs={{0,8},{8,0},{128,136},{136,128},{1,9},{9,1},{129,137},{137,129},{2... | collective-permute-start | bytes 1155080 | tf_op jit(solution)/shard_map/ppermute | solution.py:12
  76.6 34.0 %collective-permute-start.8 = (bf16[752,1024]{1,0:T(8,128)(2,1)}, bf16[752,1024]{1,0:T(8,128)(2,1)}, u32[]{:S(2)}, u32[]{:S(2)}) collective-permute-start(bf16[752,1024]{1,0:T(8,128)(2,1)} %maximum_maximum_fusion), channel_id=1, source_target_pairs={{0,2},{2,0},{4,6},{6,4},{1,3},{3,1},{5,7},{7,5},{8,10},{10,8},{12,... | collective-permute-start | bytes 4620296 | tf_op jit(solution)/shard_map/ppermute | solution.py:12
  77.9 68.2 %collective-permute-start.9 = (bf16[752,1024]{1,0:T(8,128)(2,1)}, bf16[752,1024]{1,0:T(8,128)(2,1)}, u32[]{:S(2)}, u32[]{:S(2)}) collective-permute-start(bf16[752,1024]{1,0:T(8,128)(2,1)} %maximum_maximum_fusion), channel_id=1, source_target_pairs={{0,4},{2,6},{4,0},{6,2},{1,5},{3,7},{5,1},{7,3},{8,12},{10,14},{12... | collective-permute-start | bytes 4620296 | tf_op jit(solution)/shard_map/ppermute | solution.py:12
  80.5 68.1 %collective-permute-start.10 = (bf16[752,1024]{1,0:T(8,128)(2,1)}, bf16[752,1024]{1,0:T(8,128)(2,1)}, u32[]{:S(2)}, u32[]{:S(2)}) collective-permute-start(bf16[752,1024]{1,0:T(8,128)(2,1)} %maximum_maximum_fusion), channel_id=1, source_target_pairs={{0,6},{2,4},{4,2},{6,0},{1,7},{3,5},{5,3},{7,1},{8,14},{10,12},{12... | collective-permute-start | bytes 4620296 | tf_op jit(solution)/shard_map/ppermute | solution.py:12
  154.8 6.2 %collective-permute-start.11 = (f32[376,256]{1,0:T(8,128)S(1)}, f32[376,256]{1,0:T(8,128)S(1)}, u32[]{:S(2)}, u32[]{:S(2)}) collective-permute-start(f32[376,256]{1,0:T(8,128)S(1)} %fusion.4), channel_id=1, source_target_pairs={{0,1},{1,0},{2,3},{3,2},{4,5},{5,4},{6,7},{7,6},{8,9},{9,8},{10,11... | collective-permute-start | bytes 1155080 | tf_op jit(solution)/shard_map/ppermute | solution.py:12
  158.1 12.1 %collective-permute-start.17 = (bf16[256,256]{1,0:T(8,128)(2,1)}, bf16[256,256]{1,0:T(8,128)(2,1)S(1)}, u32[]{:S(2)}, u32[]{:S(2)}) collective-permute-start(bf16[256,256]{1,0:T(8,128)(2,1)} %get-tuple-element.55), channel_id=1, source_target_pairs={{0,0},{1,128},{128,1},{129,129},{2,2},{3,130},{130,3},{131,131},{4... | collective-permute-start | bytes 393224 | tf_op jit(solution)/shard_map/ppermute | solution.py:74
  160.9 9.3 %collective-permute-start.18 = (bf16[256,256]{1,0:T(8,128)(2,1)S(1)}, bf16[256,256]{1,0:T(8,128)(2,1)S(1)}, u32[]{:S(2)}, u32[]{:S(2)}) collective-permute-start(bf16[256,256]{1,0:T(8,128)(2,1)S(1)} %get-tuple-element.56), channel_id=1, source_target_pairs={{0,1},{1,129},{128,0},{129,128},{2,3},{3,131},{130,2},{131,130},{4... | collective-permute-start | bytes 393224 | tf_op jit(solution)/shard_map/ppermute | solution.py:75
  223.7 16.1 %collective-permute-start.21 = (f32[376,256]{1,0:T(8,128)S(1)}, f32[376,256]{1,0:T(8,128)S(1)}, u32[]{:S(2)}, u32[]{:S(2)}) collective-permute-start(f32[376,256]{1,0:T(8,128)S(1)} %fusion.7), channel_id=1, source_target_pairs={{0,1},{1,0},{2,3},{3,2},{4,5},{5,4},{6,7},{7,6},{8,9},{9,8},{10,11... | collective-permute-start | bytes 1155080 | tf_op jit(solution)/shard_map/ppermute | solution.py:12
  228.2 15.2 %collective-permute-start.12 = (bf16[376,256]{1,0:T(8,128)(2,1)S(1)}, bf16[376,256]{1,0:T(8,128)(2,1)S(1)}, u32[]{:S(2)}, u32[]{:S(2)}) collective-permute-start(bf16[376,256]{1,0:T(8,128)(2,1)S(1)} %copy-done.9), channel_id=1, source_target_pairs={{0,0},{1,128},{128,1},{129,129},{2,2},{3,130},{130,3},{131,131},{4... | collective-permute-start | bytes 577544 | tf_op jit(solution)/shard_map/ppermute | solution.py:85
  232.7 11.5 %collective-permute-start.16 = (bf16[376,640]{1,0:T(8,128)(2,1)S(1)}, bf16[376,640]{1,0:T(8,128)(2,1)S(1)}, u32[]{:S(2)}, u32[]{:S(2)}) collective-permute-start(bf16[376,640]{1,0:T(8,128)(2,1)S(1)} %copy-done.8), channel_id=1, source_target_pairs={{0,0},{1,128},{128,1},{129,129},{2,2},{3,130},{130,3},{131,131},{4... | collective-permute-start | bytes 1443848 | tf_op jit(solution)/shard_map/ppermute | solution.py:85
  235.3 13.1 %collective-permute-start.20 = (bf16[376,512]{1,0:T(8,128)(2,1)S(1)}, bf16[376,512]{1,0:T(8,128)(2,1)S(1)}, u32[]{:S(2)}, u32[]{:S(2)}) collective-permute-start(bf16[376,512]{1,0:T(8,128)(2,1)S(1)} %multiply_convert_fusion.1), channel_id=1, source_target_pairs={{0,0},{1,128},{128,1},{129,129},{2,2},{3,130},{130,3},{131,131},{4... | collective-permute-start | bytes 1155080 | tf_op jit(solution)/shard_map/ppermute | solution.py:85
  240.9 9.6 %collective-permute-start.22 = (bf16[376,256]{1,0:T(8,128)(2,1)S(1)}, bf16[376,256]{1,0:T(8,128)(2,1)S(1)}, u32[]{:S(2)}, u32[]{:S(2)}) collective-permute-start(bf16[376,256]{1,0:T(8,128)(2,1)S(1)} %multiply_convert_fusion.2), channel_id=1, source_target_pairs={{0,0},{1,128},{128,1},{129,129},{2,2},{3,130},{130,3},{131,131},{4... | collective-permute-start | bytes 577544 | tf_op jit(solution)/shard_map/ppermute | solution.py:90
  (16 other events, 155.5 us)
Sparse Core Ops, SparseCore 0:
  17.8 40.5 all-gather.6
  60.2 66.8 all-gather.4
  128.9 53.4 all-gather.8
  184.0 35.9 all-gather.10

commit v2 on v0

v2 whole, which is shorter than its diff:
```python
import jax
import jax.numpy as jnp
from jax import lax
from jax.sharding import Mesh, PartitionSpec as P

AXES = ("xh", "z", "xl", "y", "core")
SIZES = (2, 8, 2, 4, 2)
WIDTHS = (896, 768)

TURN = [(h * 2 + c, c * 2 + h) for h in range(2) for c in range(2)]
CROSS = [(h * 2 + c, c * 2 + 1 - h) for h in range(2) for c in range(2)]
HOME = [(h * 2 + c, (h ^ c) * 2 + h) for h in range(2) for c in range(2)]


def exchange(value, axis, flip, size):
    return lax.ppermute(value, axis, [(i, i ^ flip) for i in range(size)])


def swap_if(flag, first, second):
    return jnp.where(flag, second, first), jnp.where(flag, first, second)


def together(*values):
    return lax.optimization_barrier(values)


def gather_tokens(tokens):
    z, y, core = (lax.axis_index(name) for name in ("z", "y", "core"))
    rows, features = tokens.shape
    half = features // 2
    mine, other = swap_if(core == 1, tokens[:, :half], tokens[:, half:])
    received = exchange(other, "core", 1, 2)
    near = swap_if(core == 1, mine, received)
    pair = jnp.concatenate(near, axis=1)
    far = exchange(pair, "xl", 1, 2)
    piece = jnp.concatenate([near[0], far[:, :half], near[1], far[:, half:]], axis=1)
    piece = jnp.concatenate([piece, exchange(piece, "xh", 1, 2)], axis=0)
    out = jnp.zeros((2 * rows, 8 * features), tokens.dtype)
    for d in range(4):
        arrived = piece if d == 0 else exchange(piece, "y", d, 4)
        for c in range(2):
            block = (z - (2 * (y ^ d) + c)) % 8
            out = lax.dynamic_update_slice(
                out, arrived[:, c * features : (c + 1) * features], (0, block * features)
            )
    return out


def along_z(value, shift):
    return lax.ppermute(value, "z", [(i, (i + shift) % 8) for i in range(8)])


def step_along_z(step, up, down):
    if step == 4:
        half = up.shape[0] // 2
        up, down = up[:half], down[half:]
    return along_z(up, 1), along_z(down, -1)


def product(gathered, blocks, half):
    total = 0
    for block, piece in blocks:
        features = gathered[:, block * half : block * half + piece.shape[0]]
        total += jnp.dot(features, piece, preferred_element_type=jnp.float32)
    return total


def swapped(part):
    xh, xl, core = (lax.axis_index(name) for name in ("xh", "xl", "core"))
    half = part.shape[0] // 2
    first, second = swap_if(xh == 1, part[:half], part[half:])
    turned = lax.ppermute(first, ("xh", "core"), TURN)
    crossed = lax.ppermute(second, ("xh", "core"), CROSS)
    return jnp.concatenate(swap_if(xl != core, turned, crossed))


def activate(total):
    rows = total.shape[0] // 2
    core = lax.axis_index("core")
    kept, given = swap_if(core == 1, total[:rows], total[rows:])
    total = kept + exchange(given, "core", 1, 2)
    return lax.ppermute(jax.nn.silu(total).astype(jnp.bfloat16), ("xh", "core"), HOME)


def on_device(tokens, weight):
    half = weight.shape[0] // 2
    parts = [weight[:, : WIDTHS[0]], weight[:, WIDTHS[0] :]]
    gathered = gather_tokens(tokens)
    mine = swapped(parts[0])
    mine, parts[1] = together(mine, parts[1])
    mine = [mine, swapped(parts[1])]
    front = [(value, value) for value in mine]
    blocks = [[(0, value)] for value in mine]
    totals = [None, None]
    for step in range(1, 5):
        for chunk in range(2):
            if step == 4:
                totals[chunk] = product(gathered, blocks[chunk][:5], half)
                *front[chunk], totals[chunk] = together(*front[chunk], totals[chunk])
            up, down = together(*step_along_z(step, *front[chunk]))
            front[chunk] = (up, down)
            if step == 4:
                blocks[chunk] += [(8, up), (9, down)]
            else:
                blocks[chunk] += [(2 * step, up), (2 * (8 - step), down)]
    outs = [
        activate(totals[chunk] + product(gathered, blocks[chunk][5:], half)) for chunk in range(2)
    ]
    return jnp.concatenate(outs, axis=1)


def solution(mesh):
    fine = Mesh(mesh.devices.reshape(SIZES), AXES)
    placed = P(("xh", "z"), ("xl", "y", "core"))
    return jax.shard_map(
        on_device, mesh=fine, in_specs=(placed, placed), out_specs=placed, check_vma=False
    )
```

time: 429 us -> 220 us (0.51)
  waiting for transfers between devices: 396 us -> 129 us
  starting transfers between devices: 0.04 us -> 47.1 us
  between operations: 13.4 us -> 0.48 us
  other arithmetic: 0 us -> 8.79 us
  local copies, waits for them, and re-layouts: 0 us -> 8.11 us
  matrix products: 19 us -> 24.7 us
    all_gather x2 -> x0, waiting for transfers between devices: 395 us -> none  [the longest x1 345 us: on_device(): whole_weight = lax.all_gather(weight, 'row', axis=0, tiled=True)]
    ppermute x0 -> x30, waiting for transfers between devices: none -> 129 us  [the longest x8 49.6 us: exchange(): return lax.ppermute(value, axis, [(i, i ^ flip) for i in range(size)])]
    ppermute x0 -> x30, starting transfers between devices: none -> 47.1 us  [the longest x16 21.5 us: along_z(): return lax.ppermute(value, 'z', [(i, (i + shift) % 8) for i in range(8)])]
    dot_general x1 -> x18, matrix products: 19 us -> 24.7 us  [product(): total += jnp.dot(features, piece, preferred_element_type=jnp.float32)]
    dynamic_update_slice x0 -> x8, local copies, waits for them, and re-layouts: none -> 5.24 us  [gather_tokens(): lax.dynamic_update_slice(out, arrived[:, c * features:(c + 1) * features]...]
  transfers between devices with their start and end apart: 2 -> 30, of which waited for: 2 -> 15; matrix products, arithmetic and copies ran while one was open for 0% -> 16% of each run, Pallas kernels for 0% -> 0%
where the time goes in v2:
time: 220 us; the launch traced here: 218 us
  waiting for transfers between devices  129 us (59%)
  starting transfers between devices  47.1 us (21%)
  matrix products  24.7 us (11%)
  other arithmetic  8.79 us (4%)
  local copies, waits for them, and re-layouts  8.11 us (4%)
    ppermute x8, waiting for transfers between devices, exchange(): return lax.ppermute(value, axis, [(i, i ^ flip) for i in range(size)])  49.6 us
    ppermute x16, waiting for transfers between devices, along_z(): return lax.ppermute(value, 'z', [(i, (i + shift) % 8) for i in range(8)])  41.3 us
    dot_general x18, matrix products, product(): total += jnp.dot(features, piece, preferred_element_type=jnp.float32)  24.7 us
    ppermute x16, starting transfers between devices, along_z(): return lax.ppermute(value, 'z', [(i, (i + shift) % 8) for i in range(8)])  21.5 us
    ppermute x2, waiting for transfers between devices, swapped(): turned = lax.ppermute(first, ('xh', 'core'), TURN)  18.2 us
    ppermute x2, waiting for transfers between devices, activate(): lax.ppermute(jax.nn.silu(total).astype(jnp.bfloat16), ('xh', 'core'), HOME)  14.9 us
    ppermute x8, starting transfers between devices, exchange(): return lax.ppermute(value, axis, [(i, i ^ flip) for i in range(size)])  11.5 us
    ppermute x2, starting transfers between devices, swapped(): turned = lax.ppermute(first, ('xh', 'core'), TURN)  9.07 us
  transfers between devices with their start and end apart: 30, of which 15 were waited for; matrix products, arithmetic and copies ran while one was open for 16% of the time, Pallas kernels for 0%

profile of v2, /device:TPU:1, one launch (start us, length us, event | category | flops | bytes accessed | tf_op | source)
XLA Modules:
  0.0 218.5 jit_solution(17224191565773793029)
XLA Ops:
  1.1 3.3 %collective-permute-start.8 = (bf16[376,256]{1,0:T(8,128)(2,1)S(1)}, bf16[376,256]{1,0:T(8,128)(2,1)S(1)}, u32[]{:S(2)}, u32[]{:S(2)}) collective-permute-start(bf16[376,256]{1,0:T(8,128)(2,1)S(1)} %broadcast_select_fusion.11), channel_id=1, source_target_pairs={{0,1},{1,0},{2,3},{3,2},{4,5},{5,4},{6,7},{7,6},{8,9},{9,8},{10,11... | collective-permute-start | bytes 577544 | tf_op jit(solution)/shard_map/ppermute | solution.py:16
  6.8 4.0 %collective-permute-start.1 = (bf16[256,896]{1,0:T(8,128)(2,1)S(1)}, bf16[256,896]{1,0:T(8,128)(2,1)S(1)}, u32[]{:S(2)}, u32[]{:S(2)}) collective-permute-start(bf16[256,896]{1,0:T(8,128)(2,1)S(1)} %get-tuple-element.54), channel_id=1, source_target_pairs={{0,0},{1,128},{128,1},{129,129},{2,2},{3,130},{130,3},{131,131},{4... | collective-permute-start | bytes 1376264 | tf_op jit(solution)/shard_map/ppermute | solution.py:72
  11.0 5.3 %collective-permute-done = bf16[256,896]{1,0:T(8,128)(2,1)S(1)} collective-permute-done((bf16[256,896]{1,0:T(8,128)(2,1)S(1)}, bf16[256,896]{1,0:T(8,128)(2,1)S(1)}, u32[]{:S(2)}, u32[]{:S(2)}) %collective-permute-start) | collective-permute-done | bytes 458784 | tf_op jit(solution)/shard_map/ppermute | solution.py:73
  16.3 7.2 %collective-permute-done.1 = bf16[256,896]{1,0:T(8,128)(2,1)S(1)} collective-permute-done((bf16[256,896]{1,0:T(8,128)(2,1)S(1)}, bf16[256,896]{1,0:T(8,128)(2,1)S(1)}, u32[]{:S(2)}, u32[]{:S(2)}) %collective-permute-start.1) | collective-permute-done | bytes 458784 | tf_op jit(solution)/shard_map/ppermute | solution.py:72
  24.3 4.0 %collective-permute-start.3 = (bf16[512,896]{1,0:T(8,128)(2,1)S(1)}, bf16[512,896]{1,0:T(8,128)(2,1)}, u32[]{:S(2)}, u32[]{:S(2)}) collective-permute-start(bf16[512,896]{1,0:T(8,128)(2,1)S(1)} %pad_maximum_fusion.2), channel_id=1, source_target_pairs={{0,112},{16,0},{32,16},{48,32},{64,48},{80,64},{96,80},{112,96},{1... | collective-permute-start | bytes 2752520 | tf_op jit(solution)/shard_map/ppermute | solution.py:50
  28.5 5.0 %collective-permute-start.19 = (bf16[256,768]{1,0:T(8,128)(2,1)S(1)}, bf16[256,768]{1,0:T(8,128)(2,1)S(1)}, u32[]{:S(2)}, u32[]{:S(2)}) collective-permute-start(bf16[256,768]{1,0:T(8,128)(2,1)S(1)} %get-tuple-element.60), channel_id=1, source_target_pairs={{0,0},{1,128},{128,1},{129,129},{2,2},{3,130},{130,3},{131,131},{4... | collective-permute-start | bytes 1179656 | tf_op jit(solution)/shard_map/ppermute | solution.py:72
  33.8 11.0 %collective-permute-done.19 = bf16[256,768]{1,0:T(8,128)(2,1)S(1)} collective-permute-done((bf16[256,768]{1,0:T(8,128)(2,1)S(1)}, bf16[256,768]{1,0:T(8,128)(2,1)S(1)}, u32[]{:S(2)}, u32[]{:S(2)}) %collective-permute-start.19) | collective-permute-done | bytes 393248 | tf_op jit(solution)/shard_map/ppermute | solution.py:72
  45.0 2.7 %collective-permute-start.21 = (bf16[512,768]{1,0:T(8,128)(2,1)S(1)}, bf16[512,768]{1,0:T(8,128)(2,1)}, u32[]{:S(2)}, u32[]{:S(2)}) collective-permute-start(bf16[512,768]{1,0:T(8,128)(2,1)S(1)} %pad_maximum_fusion.3), channel_id=1, source_target_pairs={{0,112},{16,0},{32,16},{48,32},{64,48},{80,64},{96,80},{112,96},{1... | collective-permute-start | bytes 2359304 | tf_op jit(solution)/shard_map/ppermute | solution.py:50
  47.7 6.9 %collective-permute-done.10 = bf16[376,1024]{1,0:T(8,128)(2,1)S(1)} collective-permute-done((bf16[376,1024]{1,0:T(8,128)(2,1)S(1)}, bf16[376,1024]{1,0:T(8,128)(2,1)S(1)}, u32[]{:S(2)}, u32[]{:S(2)}) %collective-permute-start.10) | collective-permute-done | bytes 770080 | tf_op jit(solution)/shard_map/ppermute | solution.py:16
  57.9 7.9 %collective-permute-done.20 = bf16[512,768]{1,0:T(8,128)(2,1)} collective-permute-done((bf16[512,768]{1,0:T(8,128)(2,1)S(1)}, bf16[512,768]{1,0:T(8,128)(2,1)}, u32[]{:S(2)}, u32[]{:S(2)}) %collective-permute-start.20) | collective-permute-done | bytes 786464 | tf_op jit(solution)/shard_map/ppermute | solution.py:50
  65.8 2.9 %collective-permute-start.12 = (bf16[752,1024]{1,0:T(8,128)(2,1)S(1)}, bf16[752,1024]{1,0:T(8,128)(2,1)}, u32[]{:S(2)}, u32[]{:S(2)}) collective-permute-start(bf16[752,1024]{1,0:T(8,128)(2,1)S(1)} %pad_maximum_fusion), channel_id=1, source_target_pairs={{0,4},{2,6},{4,0},{6,2},{1,5},{3,7},{5,1},{7,3},{8,12},{10,14},{12... | collective-permute-start | bytes 4620296 | tf_op jit(solution)/shard_map/ppermute | solution.py:16
  68.7 16.8 %collective-permute-done.4 = bf16[512,896]{1,0:T(8,128)(2,1)S(1)} collective-permute-done((bf16[512,896]{1,0:T(8,128)(2,1)S(1)}, bf16[512,896]{1,0:T(8,128)(2,1)S(1)}, u32[]{:S(2)}, u32[]{:S(2)}) %collective-permute-start.4) | collective-permute-done | bytes 917536 | tf_op jit(solution)/shard_map/ppermute | solution.py:50
  87.6 2.7 %collective-permute-start.13 = (bf16[752,1024]{1,0:T(8,128)(2,1)S(1)}, bf16[752,1024]{1,0:T(8,128)(2,1)S(1)}, u32[]{:S(2)}, u32[]{:S(2)}) collective-permute-start(bf16[752,1024]{1,0:T(8,128)(2,1)S(1)} %pad_maximum_fusion), channel_id=1, source_target_pairs={{0,6},{2,4},{4,2},{6,0},{1,7},{3,5},{5,3},{7,1},{8,14},{10,12},{12... | collective-permute-start | bytes 4620296 | tf_op jit(solution)/shard_map/ppermute | solution.py:16
  91.3 6.9 %collective-permute-done.22 = bf16[512,768]{1,0:T(8,128)(2,1)} collective-permute-done((bf16[512,768]{1,0:T(8,128)(2,1)}, bf16[512,768]{1,0:T(8,128)(2,1)}, u32[]{:S(2)}, u32[]{:S(2)}) %collective-permute-start.22) | collective-permute-done | bytes 786464 | tf_op jit(solution)/shard_map/ppermute | solution.py:50
  99.3 3.0 %collective-permute-start.7 = (bf16[512,896]{1,0:T(8,128)(2,1)}, bf16[512,896]{1,0:T(8,128)(2,1)S(1)}, u32[]{:S(2)}, u32[]{:S(2)}) collective-permute-start(bf16[512,896]{1,0:T(8,128)(2,1)} %collective-permute-done.5), channel_id=1, source_target_pairs={{0,112},{16,0},{32,16},{48,32},{64,48},{80,64},{96,80},{112,96},{1... | collective-permute-start | bytes 2752520 | tf_op jit(solution)/shard_map/ppermute | solution.py:50
  104.8 17.2 %collective-permute-done.12 = bf16[752,1024]{1,0:T(8,128)(2,1)} collective-permute-done((bf16[752,1024]{1,0:T(8,128)(2,1)S(1)}, bf16[752,1024]{1,0:T(8,128)(2,1)}, u32[]{:S(2)}, u32[]{:S(2)}) %collective-permute-start.12) | collective-permute-done | bytes 1540128 | tf_op jit(solution)/shard_map/ppermute | solution.py:16
  126.1 25.3 %collective-permute-done.13 = bf16[752,1024]{1,0:T(8,128)(2,1)S(1)} collective-permute-done((bf16[752,1024]{1,0:T(8,128)(2,1)S(1)}, bf16[752,1024]{1,0:T(8,128)(2,1)S(1)}, u32[]{:S(2)}, u32[]{:S(2)}) %collective-permute-start.13) | collective-permute-done | bytes 1540128 | tf_op jit(solution)/shard_map/ppermute | solution.py:16
  162.5 2.6 %add_add_fusion.1 = f32[752,896]{1,0:T(8,128)S(1)} fusion(f32[752,896]{1,0:T(8,128)S(1)} %fusion.18, f32[752,896]{1,0:T(8,128)S(1)} %fusion.22, f32[752,896]{1,0:T(8,128)S(1)} %fusion.30, f32[752,896]{1,0:T(8,128)S(1)} %fusion.26, bf16[512,896]{1,0:T(8,128)(2,1)} %collective-permute-done.5, bf16[752,4096]{1,0:T(8,128)(2,1)S(1)} %slice_dynamic-update-slice_fusion), kind=kOutput, calls=%fused_computation.1 | convolution fusion | flops 692658176 | bytes 15163392 | tf_op jit(solution)/shard_map/dot_general | solution.py:64
  168.3 3.6 %collective-permute-start.27 = (bf16[256,768]{1,0:T(8,128)(2,1)S(1)}, bf16[256,768]{1,0:T(8,128)(2,1)S(1)}, u32[]{:S(2)}, u32[]{:S(2)}) collective-permute-start(bf16[256,768]{1,0:T(8,128)(2,1)S(1)} %slice.145), channel_id=1, source_target_pairs={{0,112},{16,0},{32,16},{48,32},{64,48},{80,64},{96,80},{112,96},{1... | collective-permute-start | bytes 1179656 | tf_op jit(solution)/shard_map/ppermute | solution.py:50
  174.6 2.7 %collective-permute-start.15 = (bf16[256,896]{1,0:T(8,128)(2,1)S(1)}, bf16[256,896]{1,0:T(8,128)(2,1)S(1)}, u32[]{:S(2)}, u32[]{:S(2)}) collective-permute-start(bf16[256,896]{1,0:T(8,128)(2,1)S(1)} %slice.138), channel_id=1, source_target_pairs={{0,112},{16,0},{32,16},{48,32},{64,48},{80,64},{96,80},{112,96},{1... | collective-permute-start | bytes 1376264 | tf_op jit(solution)/shard_map/ppermute | solution.py:50
  178.3 3.0 %collective-permute-done.26 = bf16[256,768]{1,0:T(8,128)(2,1)S(1)} collective-permute-done((bf16[256,768]{1,0:T(8,128)(2,1)S(1)}, bf16[256,768]{1,0:T(8,128)(2,1)S(1)}, u32[]{:S(2)}, u32[]{:S(2)}) %collective-permute-start.26) | collective-permute-done | bytes 393248 | tf_op jit(solution)/shard_map/ppermute | solution.py:50
  185.1 4.2 %collective-permute-done.14 = bf16[256,896]{1,0:T(8,128)(2,1)S(1)} collective-permute-done((bf16[256,896]{1,0:T(8,128)(2,1)S(1)}, bf16[256,896]{1,0:T(8,128)(2,1)S(1)}, u32[]{:S(2)}, u32[]{:S(2)}) %collective-permute-start.14) | collective-permute-done | bytes 458784 | tf_op jit(solution)/shard_map/ppermute | solution.py:50
  194.5 2.6 %add_add_fusion.2 = f32[752,768]{1,0:T(8,128)S(1)} fusion(f32[752,768]{1,0:T(8,128)S(1)} %add_add_fusion.3, f32[752,768]{1,0:T(8,128)} %fusion.32, f32[752,768]{1,0:T(8,128)S(1)} %copy-done, f32[752,768]{1,0:T(8,128)S(1)} %fusion.4, f32[752,768]{1,0:T(8,128)S(1)} %fusion), kind=kLoop, calls=%fused_computation.2 | loop fusion | flops 2310144 | bytes 13860864 | tf_op jit(solution)/shard_map/add | solution.py:107
  202.4 14.9 %collective-permute-done.29 = bf16[376,768]{1,0:T(8,128)(2,1)S(1)} collective-permute-done((bf16[376,768]{1,0:T(8,128)(2,1)S(1)}, bf16[376,768]{1,0:T(8,128)(2,1)S(1)}, u32[]{:S(2)}, u32[]{:S(2)}) %collective-permute-start.29) | collective-permute-done | bytes 577568 | tf_op jit(solution)/shard_map/ppermute | solution.py:82
  (100 shorter events, 52.0 us)
Async XLA Ops:
  6.8 16.7 %collective-permute-start.1 = (bf16[256,896]{1,0:T(8,128)(2,1)S(1)}, bf16[256,896]{1,0:T(8,128)(2,1)S(1)}, u32[]{:S(2)}, u32[]{:S(2)}) collective-permute-start(bf16[256,896]{1,0:T(8,128)(2,1)S(1)} %get-tuple-element.54), channel_id=1, source_target_pairs={{0,0},{1,128},{128,1},{129,129},{2,2},{3,130},{130,3},{131,131},{4... | collective-permute-start | bytes 1376264 | tf_op jit(solution)/shard_map/ppermute | solution.py:72
  10.9 22.6 %collective-permute-start.9 = (bf16[376,512]{1,0:T(8,128)(2,1)S(1)}, bf16[376,512]{1,0:T(8,128)(2,1)S(1)}, u32[]{:S(2)}, u32[]{:S(2)}) collective-permute-start(bf16[376,512]{1,0:T(8,128)(2,1)S(1)} %pad_maximum_fusion.5), channel_id=1, source_target_pairs={{0,8},{8,0},{1,9},{9,1},{2,10},{10,2},{3,11},{11,3},{4,12},{12,4},... | collective-permute-start | bytes 1155080 | tf_op jit(solution)/shard_map/ppermute | solution.py:16
  23.7 24.0 %collective-permute-start.2 = (bf16[512,896]{1,0:T(8,128)(2,1)S(1)}, bf16[512,896]{1,0:T(8,128)(2,1)S(1)}, u32[]{:S(2)}, u32[]{:S(2)}) collective-permute-start(bf16[512,896]{1,0:T(8,128)(2,1)S(1)} %pad_maximum_fusion.2), channel_id=1, source_target_pairs={{0,16},{16,32},{32,48},{48,64},{64,80},{80,96},{96,112},{112,0},{1... | collective-permute-start | bytes 2752520 | tf_op jit(solution)/shard_map/ppermute | solution.py:50
  24.3 23.4 %collective-permute-start.3 = (bf16[512,896]{1,0:T(8,128)(2,1)S(1)}, bf16[512,896]{1,0:T(8,128)(2,1)}, u32[]{:S(2)}, u32[]{:S(2)}) collective-permute-start(bf16[512,896]{1,0:T(8,128)(2,1)S(1)} %pad_maximum_fusion.2), channel_id=1, source_target_pairs={{0,112},{16,0},{32,16},{48,32},{64,48},{80,64},{96,80},{112,96},{1... | collective-permute-start | bytes 2752520 | tf_op jit(solution)/shard_map/ppermute | solution.py:50
  28.5 16.3 %collective-permute-start.19 = (bf16[256,768]{1,0:T(8,128)(2,1)S(1)}, bf16[256,768]{1,0:T(8,128)(2,1)S(1)}, u32[]{:S(2)}, u32[]{:S(2)}) collective-permute-start(bf16[256,768]{1,0:T(8,128)(2,1)S(1)} %get-tuple-element.60), channel_id=1, source_target_pairs={{0,0},{1,128},{128,1},{129,129},{2,2},{3,130},{130,3},{131,131},{4... | collective-permute-start | bytes 1179656 | tf_op jit(solution)/shard_map/ppermute | solution.py:72
  33.6 21.1 %collective-permute-start.10 = (bf16[376,1024]{1,0:T(8,128)(2,1)S(1)}, bf16[376,1024]{1,0:T(8,128)(2,1)S(1)}, u32[]{:S(2)}, u32[]{:S(2)}) collective-permute-start(bf16[376,1024]{1,0:T(8,128)(2,1)S(1)} %pad_maximum_fusion.4), channel_id=1, source_target_pairs={{0,128},{128,0},{1,129},{129,1},{2,130},{130,2},{3,131},{131,3},{4... | collective-permute-start | bytes 2310152 | tf_op jit(solution)/shard_map/ppermute | solution.py:16
  44.9 20.9 %collective-permute-start.20 = (bf16[512,768]{1,0:T(8,128)(2,1)S(1)}, bf16[512,768]{1,0:T(8,128)(2,1)}, u32[]{:S(2)}, u32[]{:S(2)}) collective-permute-start(bf16[512,768]{1,0:T(8,128)(2,1)S(1)} %pad_maximum_fusion.3), channel_id=1, source_target_pairs={{0,16},{16,32},{32,48},{48,64},{64,80},{80,96},{96,112},{112,0},{1... | collective-permute-start | bytes 2359304 | tf_op jit(solution)/shard_map/ppermute | solution.py:50
  45.0 23.7 %collective-permute-start.21 = (bf16[512,768]{1,0:T(8,128)(2,1)S(1)}, bf16[512,768]{1,0:T(8,128)(2,1)}, u32[]{:S(2)}, u32[]{:S(2)}) collective-permute-start(bf16[512,768]{1,0:T(8,128)(2,1)S(1)} %pad_maximum_fusion.3), channel_id=1, source_target_pairs={{0,112},{16,0},{32,16},{48,32},{64,48},{80,64},{96,80},{112,96},{1... | collective-permute-start | bytes 2359304 | tf_op jit(solution)/shard_map/ppermute | solution.py:50
  47.7 37.9 %collective-permute-start.4 = (bf16[512,896]{1,0:T(8,128)(2,1)S(1)}, bf16[512,896]{1,0:T(8,128)(2,1)S(1)}, u32[]{:S(2)}, u32[]{:S(2)}) collective-permute-start(bf16[512,896]{1,0:T(8,128)(2,1)S(1)} %collective-permute-done.2), channel_id=1, source_target_pairs={{0,16},{16,32},{32,48},{48,64},{64,80},{80,96},{96,112},{112,0},{1... | collective-permute-start | bytes 2752520 | tf_op jit(solution)/shard_map/ppermute | solution.py:50
  54.9 47.5 %collective-permute-start.11 = (bf16[752,1024]{1,0:T(8,128)(2,1)S(1)}, bf16[752,1024]{1,0:T(8,128)(2,1)}, u32[]{:S(2)}, u32[]{:S(2)}) collective-permute-start(bf16[752,1024]{1,0:T(8,128)(2,1)S(1)} %pad_maximum_fusion), channel_id=1, source_target_pairs={{0,2},{2,0},{4,6},{6,4},{1,3},{3,1},{5,7},{7,5},{8,10},{10,8},{12,... | collective-permute-start | bytes 4620296 | tf_op jit(solution)/shard_map/ppermute | solution.py:16
  56.2 31.4 %collective-permute-start.5 = (bf16[512,896]{1,0:T(8,128)(2,1)}, bf16[512,896]{1,0:T(8,128)(2,1)}, u32[]{:S(2)}, u32[]{:S(2)}) collective-permute-start(bf16[512,896]{1,0:T(8,128)(2,1)} %collective-permute-done.3), channel_id=1, source_target_pairs={{0,112},{16,0},{32,16},{48,32},{64,48},{80,64},{96,80},{112,96},{1... | collective-permute-start | bytes 2752520 | tf_op jit(solution)/shard_map/ppermute | solution.py:50
  65.8 56.2 %collective-permute-start.12 = (bf16[752,1024]{1,0:T(8,128)(2,1)S(1)}, bf16[752,1024]{1,0:T(8,128)(2,1)}, u32[]{:S(2)}, u32[]{:S(2)}) collective-permute-start(bf16[752,1024]{1,0:T(8,128)(2,1)S(1)} %pad_maximum_fusion), channel_id=1, source_target_pairs={{0,4},{2,6},{4,0},{6,2},{1,5},{3,7},{5,1},{7,3},{8,12},{10,14},{12... | collective-permute-start | bytes 4620296 | tf_op jit(solution)/shard_map/ppermute | solution.py:16
  68.7 29.5 %collective-permute-start.22 = (bf16[512,768]{1,0:T(8,128)(2,1)}, bf16[512,768]{1,0:T(8,128)(2,1)}, u32[]{:S(2)}, u32[]{:S(2)}) collective-permute-start(bf16[512,768]{1,0:T(8,128)(2,1)} %collective-permute-done.20), channel_id=1, source_target_pairs={{0,16},{16,32},{32,48},{48,64},{64,80},{80,96},{96,112},{112,0},{1... | collective-permute-start | bytes 2359304 | tf_op jit(solution)/shard_map/ppermute | solution.py:50
  87.6 63.8 %collective-permute-start.13 = (bf16[752,1024]{1,0:T(8,128)(2,1)S(1)}, bf16[752,1024]{1,0:T(8,128)(2,1)S(1)}, u32[]{:S(2)}, u32[]{:S(2)}) collective-permute-start(bf16[752,1024]{1,0:T(8,128)(2,1)S(1)} %pad_maximum_fusion), channel_id=1, source_target_pairs={{0,6},{2,4},{4,2},{6,0},{1,7},{3,5},{5,3},{7,1},{8,14},{10,12},{12... | collective-permute-start | bytes 4620296 | tf_op jit(solution)/shard_map/ppermute | solution.py:16
  98.2 75.3 %collective-permute-start.6 = (bf16[512,896]{1,0:T(8,128)(2,1)S(1)}, bf16[512,896]{1,0:T(8,128)(2,1)S(1)}, u32[]{:S(2)}, u32[]{:S(2)}) collective-permute-start(bf16[512,896]{1,0:T(8,128)(2,1)S(1)} %copy-done.5), channel_id=1, source_target_pairs={{0,16},{16,32},{32,48},{48,64},{64,80},{80,96},{96,112},{112,0},{1... | collective-permute-start | bytes 2752520 | tf_op jit(solution)/shard_map/ppermute | solution.py:50
  99.3 74.2 %collective-permute-start.7 = (bf16[512,896]{1,0:T(8,128)(2,1)}, bf16[512,896]{1,0:T(8,128)(2,1)S(1)}, u32[]{:S(2)}, u32[]{:S(2)}) collective-permute-start(bf16[512,896]{1,0:T(8,128)(2,1)} %collective-permute-done.5), channel_id=1, source_target_pairs={{0,112},{16,0},{32,16},{48,32},{64,48},{80,64},{96,80},{112,96},{1... | collective-permute-start | bytes 2752520 | tf_op jit(solution)/shard_map/ppermute | solution.py:50
  102.3 65.7 %collective-permute-start.24 = (bf16[512,768]{1,0:T(8,128)(2,1)}, bf16[512,768]{1,0:T(8,128)(2,1)S(1)}, u32[]{:S(2)}, u32[]{:S(2)}) collective-permute-start(bf16[512,768]{1,0:T(8,128)(2,1)} %collective-permute-done.22), channel_id=1, source_target_pairs={{0,16},{16,32},{32,48},{48,64},{64,80},{80,96},{96,112},{112,0},{1... | collective-permute-start | bytes 2359304 | tf_op jit(solution)/shard_map/ppermute | solution.py:50
  122.0 46.1 %collective-permute-start.25 = (bf16[512,768]{1,0:T(8,128)(2,1)}, bf16[512,768]{1,0:T(8,128)(2,1)S(1)}, u32[]{:S(2)}, u32[]{:S(2)}) collective-permute-start(bf16[512,768]{1,0:T(8,128)(2,1)} %collective-permute-done.23), channel_id=1, source_target_pairs={{0,112},{16,0},{32,16},{48,32},{64,48},{80,64},{96,80},{112,96},{1... | collective-permute-start | bytes 2359304 | tf_op jit(solution)/shard_map/ppermute | solution.py:50
  168.1 13.2 %collective-permute-start.26 = (bf16[256,768]{1,0:T(8,128)(2,1)S(1)}, bf16[256,768]{1,0:T(8,128)(2,1)S(1)}, u32[]{:S(2)}, u32[]{:S(2)}) collective-permute-start(bf16[256,768]{1,0:T(8,128)(2,1)S(1)} %slice.144), channel_id=1, source_target_pairs={{0,16},{16,32},{32,48},{48,64},{64,80},{80,96},{96,112},{112,0},{1... | collective-permute-start | bytes 1179656 | tf_op jit(solution)/shard_map/ppermute | solution.py:50
  168.3 13.0 %collective-permute-start.27 = (bf16[256,768]{1,0:T(8,128)(2,1)S(1)}, bf16[256,768]{1,0:T(8,128)(2,1)S(1)}, u32[]{:S(2)}, u32[]{:S(2)}) collective-permute-start(bf16[256,768]{1,0:T(8,128)(2,1)S(1)} %slice.145), channel_id=1, source_target_pairs={{0,112},{16,0},{32,16},{48,32},{64,48},{80,64},{96,80},{112,96},{1... | collective-permute-start | bytes 1179656 | tf_op jit(solution)/shard_map/ppermute | solution.py:50
  174.5 14.8 %collective-permute-start.14 = (bf16[256,896]{1,0:T(8,128)(2,1)S(1)}, bf16[256,896]{1,0:T(8,128)(2,1)S(1)}, u32[]{:S(2)}, u32[]{:S(2)}) collective-permute-start(bf16[256,896]{1,0:T(8,128)(2,1)S(1)} %slice.137), channel_id=1, source_target_pairs={{0,16},{16,32},{32,48},{48,64},{64,80},{80,96},{96,112},{112,0},{1... | collective-permute-start | bytes 1376264 | tf_op jit(solution)/shard_map/ppermute | solution.py:50
  174.6 16.0 %collective-permute-start.15 = (bf16[256,896]{1,0:T(8,128)(2,1)S(1)}, bf16[256,896]{1,0:T(8,128)(2,1)S(1)}, u32[]{:S(2)}, u32[]{:S(2)}) collective-permute-start(bf16[256,896]{1,0:T(8,128)(2,1)S(1)} %slice.138), channel_id=1, source_target_pairs={{0,112},{16,0},{32,16},{48,32},{64,48},{80,64},{96,80},{112,96},{1... | collective-permute-start | bytes 1376264 | tf_op jit(solution)/shard_map/ppermute | solution.py:50
  198.1 19.2 %collective-permute-start.17 = (bf16[376,896]{1,0:T(8,128)(2,1)S(1)}, bf16[376,896]{1,0:T(8,128)(2,1)S(1)}, u32[]{:S(2)}, u32[]{:S(2)}) collective-permute-start(bf16[376,896]{1,0:T(8,128)(2,1)S(1)} %multiply_convert_fusion), channel_id=1, source_target_pairs={{0,0},{1,128},{128,129},{129,1},{2,2},{3,130},{130,131},{131,3},{4... | collective-permute-start | bytes 2021384 | tf_op jit(solution)/shard_map/ppermute | solution.py:82
  200.5 16.9 %collective-permute-start.29 = (bf16[376,768]{1,0:T(8,128)(2,1)S(1)}, bf16[376,768]{1,0:T(8,128)(2,1)S(1)}, u32[]{:S(2)}, u32[]{:S(2)}) collective-permute-start(bf16[376,768]{1,0:T(8,128)(2,1)S(1)} %multiply_convert_fusion.1), channel_id=1, source_target_pairs={{0,0},{1,128},{128,129},{129,1},{2,2},{3,130},{130,131},{131,3},{4... | collective-permute-start | bytes 1732616 | tf_op jit(solution)/shard_map/ppermute | solution.py:82
  (13 other events, 96.7 us)

commit v3 on v2

--- a/solution.py
+++ b/solution.py
@@ -1,11 +1,13 @@
 import jax
 import jax.numpy as jnp
 from jax import lax
+from jax.experimental import pallas as pl
+from jax.experimental.pallas import tpu as pltpu
 from jax.sharding import Mesh, PartitionSpec as P
 
 AXES = ("xh", "z", "xl", "y", "core")
 SIZES = (2, 8, 2, 4, 2)
-WIDTHS = (896, 768)
+WIDTHS = (768, 896)
 
 TURN = [(h * 2 + c, c * 2 + h) for h in range(2) for c in range(2)]
 CROSS = [(h * 2 + c, c * 2 + 1 - h) for h in range(2) for c in range(2)]
@@ -24,26 +26,43 @@
     return lax.optimization_barrier(values)
 
 
-def gather_tokens(tokens):
-    z, y, core = (lax.axis_index(name) for name in ("z", "y", "core"))
-    rows, features = tokens.shape
-    half = features // 2
+def order_blocks(place, plane, out):
+    half = plane.shape[2] // 2
+    at = lax.rem(place[2] + 8 - pl.program_id(0), 8)
+    y, core = lax.div(at, 2), lax.rem(at, 2)
+    for e in range(2):
+        for b in range(2):
+            device = (lax.rem(place[0] + e, 2) * 2 + lax.rem(place[1] + b, 2)) * 4 + y
+            columns = pl.ds(pl.multiple_of(core * half, half), half)
+            out[e, :, b * half : (b + 1) * half] = plane[device, :, columns]
+
+
+def tokens_of_core(tokens):
+    core = lax.axis_index("core")
+    half = tokens.shape[1] // 2
     mine, other = swap_if(core == 1, tokens[:, :half], tokens[:, half:])
     received = exchange(other, "core", 1, 2)
-    near = swap_if(core == 1, mine, received)
-    pair = jnp.concatenate(near, axis=1)
-    far = exchange(pair, "xl", 1, 2)
-    piece = jnp.concatenate([near[0], far[:, :half], near[1], far[:, half:]], axis=1)
-    piece = jnp.concatenate([piece, exchange(piece, "xh", 1, 2)], axis=0)
-    out = jnp.zeros((2 * rows, 8 * features), tokens.dtype)
-    for d in range(4):
-        arrived = piece if d == 0 else exchange(piece, "y", d, 4)
-        for c in range(2):
-            block = (z - (2 * (y ^ d) + c)) % 8
-            out = lax.dynamic_update_slice(
-                out, arrived[:, c * features : (c + 1) * features], (0, block * features)
-            )
-    return out
+    return jnp.concatenate(swap_if(core == 1, mine, received), axis=1)
+
+
+def order_tokens(plane, rows):
+    place = jnp.stack([lax.axis_index(name) for name in ("xh", "xl", "z")])
+    features = plane.shape[2]
+    ordered = pl.pallas_call(
+        order_blocks,
+        grid=(8,),
+        in_specs=[
+            pl.BlockSpec(memory_space=pltpu.SMEM),
+            pl.BlockSpec(plane.shape, lambda r: (0, 0, 0)),
+        ],
+        out_specs=pl.BlockSpec((2, rows, features), lambda r: (0, 0, r)),
+        out_shape=jax.ShapeDtypeStruct((2, rows, 8 * features), plane.dtype),
+        compiler_params=pltpu.CompilerParams(vmem_limit_bytes=32 * 2**20),
+        cost_estimate=pl.CostEstimate(
+            flops=0, transcendentals=0, bytes_accessed=4 * 16 * rows * features
+        ),
+    )(place, plane)
+    return ordered.reshape(2 * rows, 8 * features)
 
 
 def along_z(value, shift):
@@ -79,24 +98,36 @@
     core = lax.axis_index("core")
     kept, given = swap_if(core == 1, total[:rows], total[rows:])
     total = kept + exchange(given, "core", 1, 2)
-    return lax.ppermute(jax.nn.silu(total).astype(jnp.bfloat16), ("xh", "core"), HOME)
+    return jax.nn.silu(total).astype(jnp.bfloat16)
+
+
+def home(out):
+    return lax.ppermute(out, ("xh", "core"), HOME)
 
 
 def on_device(tokens, weight):
+    rows = tokens.shape[0]
     half = weight.shape[0] // 2
     parts = [weight[:, : WIDTHS[0]], weight[:, WIDTHS[0] :]]
-    gathered = gather_tokens(tokens)
+    near = tokens_of_core(tokens)
+    near, parts[0] = together(near, parts[0])
+    plane = lax.all_gather(near[None], ("xh", "xl", "y"), axis=0, tiled=True)
     mine = swapped(parts[0])
     mine, parts[1] = together(mine, parts[1])
     mine = [mine, swapped(parts[1])]
     front = [(value, value) for value in mine]
     blocks = [[(0, value)] for value in mine]
-    totals = [None, None]
+    totals = [0, 0]
+    gathered = None
     for step in range(1, 5):
         for chunk in range(2):
-            if step == 4:
-                totals[chunk] = product(gathered, blocks[chunk][:5], half)
+            if step == 2 and chunk:
+                gathered, *front[1] = together(order_tokens(plane, rows), *front[1])
+            if step > 2:
+                totals[chunk] += product(gathered, blocks[chunk][:-2], half)
+                blocks[chunk] = blocks[chunk][-2:]
                 *front[chunk], totals[chunk] = together(*front[chunk], totals[chunk])
+                blocks[chunk] = [(blocks[chunk][i][0], front[chunk][i]) for i in range(2)]
             up, down = together(*step_along_z(step, *front[chunk]))
             front[chunk] = (up, down)
             if step == 4:
@@ -104,7 +135,7 @@
             else:
                 blocks[chunk] += [(2 * step, up), (2 * (8 - step), down)]
     outs = [
-        activate(totals[chunk] + product(gathered, blocks[chunk][5:], half)) for chunk in range(2)
+        home(activate(totals[chunk] + product(gathered, blocks[chunk], half))) for chunk in range(2)
     ]
     return jnp.concatenate(outs, axis=1)
 

time: 220 us -> 214 us (0.973)
  between operations: 0.48 us -> 13.7 us
  waiting for transfers between devices: 129 us -> 123 us
  local copies, waits for them, and re-layouts: 8.11 us -> 2.89 us
  other arithmetic: 8.79 us -> 4.66 us
  matrix products: 24.7 us -> 20.7 us
    ppermute x8 -> x3, waiting for transfers between devices: 49.6 us -> 2.91 us  [exchange(): return lax.ppermute(value, axis, [(i, i ^ flip) for i in range(size)])]
    ppermute x16, waiting for transfers between devices: 41.3 us -> 87.8 us  [along_z(): return lax.ppermute(value, 'z', [(i, (i + shift) % 8) for i in range(8)])]
    ppermute x16, starting transfers between devices: 21.5 us -> 29.8 us  [along_z(): return lax.ppermute(value, 'z', [(i, (i + shift) % 8) for i in range(8)])]
    ppermute x8 -> x3, starting transfers between devices: 11.5 us -> 4.38 us  [exchange(): return lax.ppermute(value, axis, [(i, i ^ flip) for i in range(size)])]
    dynamic_update_slice x8 -> x0, local copies, waits for them, and re-layouts: 5.24 us -> none  [gather_tokens(): lax.dynamic_update_slice(out, arrived[:, c * features:(c + 1) * features]...]
    dot_general x18, matrix products: 24.7 us -> 20.7 us  [product(): total += jnp.dot(features, piece, preferred_element_type=jnp.float32)]
    ppermute x2, waiting for transfers between devices: 5.28 us -> 1.55 us  [swapped(): crossed = lax.ppermute(second, ('xh', 'core'), CROSS)]
    add x2 -> x0, other arithmetic: 3.6 us -> none  [on_device(): totals[chunk] + product(gathered, blocks[chunk][5:], half)]
  transfers between devices with their start and end apart: 30 -> 26, of which waited for: 15 -> 18; matrix products, arithmetic and copies ran while one was open for 16% -> 7% of each run, Pallas kernels for 0% -> 0%
where the time goes in v3:
time: 214 us
  waiting for transfers between devices  123 us (57%)
  starting transfers between devices  47.3 us (22%)
  matrix products  20.7 us (10%)
  between operations  13.7 us (6%)
  other arithmetic  4.66 us (2%)
  local copies, waits for them, and re-layouts  2.89 us (1%)
    ppermute x16, waiting for transfers between devices, along_z(): return lax.ppermute(value, 'z', [(i, (i + shift) % 8) for i in range(8)])  87.8 us
    ppermute x16, starting transfers between devices, along_z(): return lax.ppermute(value, 'z', [(i, (i + shift) % 8) for i in range(8)])  29.8 us
    dot_general x18, matrix products, product(): total += jnp.dot(features, piece, preferred_element_type=jnp.float32)  20.7 us
    ppermute x2, waiting for transfers between devices, swapped(): turned = lax.ppermute(first, ('xh', 'core'), TURN)  16 us
    ppermute x2, waiting for transfers between devices, home(): return lax.ppermute(out, ('xh', 'core'), HOME)  14.4 us
    ppermute x2, starting transfers between devices, swapped(): turned = lax.ppermute(first, ('xh', 'core'), TURN)  7.49 us
    ppermute x2, starting transfers between devices, home(): return lax.ppermute(out, ('xh', 'core'), HOME)  4.42 us
    ppermute x3, starting transfers between devices, exchange(): return lax.ppermute(value, axis, [(i, i ^ flip) for i in range(size)])  4.38 us
  transfers between devices with their start and end apart: 26, of which 18 were waited for; matrix products, arithmetic and copies ran while one was open for 7% of the time, Pallas kernels for 0%

profile of v3, /device:TPU:1, one launch (start us, length us, event | category | flops | bytes accessed | tf_op | source)
XLA Modules:
  0.0 213.7 jit_solution(13075203015885604709)
XLA Ops:
  7.7 3.3 %collective-permute-start = (bf16[376,256]{1,0:T(8,128)(2,1)S(1)}, bf16[376,256]{1,0:T(8,128)(2,1)S(1)}, u32[]{:S(2)}, u32[]{:S(2)}) collective-permute-start(bf16[376,256]{1,0:T(8,128)(2,1)S(1)} %broadcast_select_fusion.11), channel_id=1, source_target_pairs={{0,1},{1,0},{2,3},{3,2},{4,5},{5,4},{6,7},{7,6},{8,9},{9,8},{10,11... | collective-permute-start | bytes 577544 | tf_op jit(solution)/shard_map/ppermute | solution.py:18
  14.1 4.5 %collective-permute-start.2 = (bf16[256,768]{1,0:T(8,128)(2,1)S(1)}, bf16[256,768]{1,0:T(8,128)(2,1)S(1)}, u32[]{:S(2)}, u32[]{:S(2)}) collective-permute-start(bf16[256,768]{1,0:T(8,128)(2,1)S(1)} %get-tuple-element.82), channel_id=1, source_target_pairs={{0,0},{1,128},{128,1},{129,129},{2,2},{3,130},{130,3},{131,131},{4... | collective-permute-start | bytes 1179656 | tf_op jit(solution)/shard_map/ppermute | solution.py:91
  18.8 7.4 %collective-permute-done.2 = bf16[256,768]{1,0:T(8,128)(2,1)S(1)} collective-permute-done((bf16[256,768]{1,0:T(8,128)(2,1)S(1)}, bf16[256,768]{1,0:T(8,128)(2,1)S(1)}, u32[]{:S(2)}, u32[]{:S(2)}) %collective-permute-start.2) | collective-permute-done | bytes 393248 | tf_op jit(solution)/shard_map/ppermute | solution.py:91
  26.6 3.0 %collective-permute-start.8 = (bf16[256,896]{1,0:T(8,128)(2,1)S(1)}, bf16[256,896]{1,0:T(8,128)(2,1)S(1)}, u32[]{:S(2)}, u32[]{:S(2)}) collective-permute-start(bf16[256,896]{1,0:T(8,128)(2,1)S(1)} %get-tuple-element.78), channel_id=1, source_target_pairs={{0,0},{1,128},{128,1},{129,129},{2,2},{3,130},{130,3},{131,131},{4... | collective-permute-start | bytes 1376264 | tf_op jit(solution)/shard_map/ppermute | solution.py:91
  31.0 4.0 %collective-permute-start.4 = (bf16[512,768]{1,0:T(8,128)(2,1)S(1)}, bf16[512,768]{1,0:T(8,128)(2,1)}, u32[]{:S(2)}, u32[]{:S(2)}) collective-permute-start(bf16[512,768]{1,0:T(8,128)(2,1)S(1)} %pad_maximum_fusion.2), channel_id=1, source_target_pairs={{0,112},{16,0},{32,16},{48,32},{64,48},{80,64},{96,80},{112,96},{1... | collective-permute-start | bytes 2359304 | tf_op jit(solution)/shard_map/ppermute | solution.py:69
  36.4 8.5 %collective-permute-done.8 = bf16[256,896]{1,0:T(8,128)(2,1)S(1)} collective-permute-done((bf16[256,896]{1,0:T(8,128)(2,1)S(1)}, bf16[256,896]{1,0:T(8,128)(2,1)S(1)}, u32[]{:S(2)}, u32[]{:S(2)}) %collective-permute-start.8) | collective-permute-done | bytes 458784 | tf_op jit(solution)/shard_map/ppermute | solution.py:91
  45.1 5.0 %collective-permute-start.10 = (bf16[512,896]{1,0:T(8,128)(2,1)S(1)}, bf16[512,896]{1,0:T(8,128)(2,1)}, u32[]{:S(2)}, u32[]{:S(2)}) collective-permute-start(bf16[512,896]{1,0:T(8,128)(2,1)S(1)} %pad_maximum_fusion.1), channel_id=1, source_target_pairs={{0,112},{16,0},{32,16},{48,32},{64,48},{80,64},{96,80},{112,96},{1... | collective-permute-start | bytes 2752520 | tf_op jit(solution)/shard_map/ppermute | solution.py:69
  50.1 2.3 %collective-permute-done.4 = bf16[512,768]{1,0:T(8,128)(2,1)} collective-permute-done((bf16[512,768]{1,0:T(8,128)(2,1)S(1)}, bf16[512,768]{1,0:T(8,128)(2,1)}, u32[]{:S(2)}, u32[]{:S(2)}) %collective-permute-start.4) | collective-permute-done | bytes 786464 | tf_op jit(solution)/shard_map/ppermute | solution.py:69
  52.5 3.4 %collective-permute-start.6 = (bf16[512,768]{1,0:T(8,128)(2,1)}, bf16[512,768]{1,0:T(8,128)(2,1)}, u32[]{:S(2)}, u32[]{:S(2)}) collective-permute-start(bf16[512,768]{1,0:T(8,128)(2,1)} %collective-permute-done.4), channel_id=1, source_target_pairs={{0,112},{16,0},{32,16},{48,32},{64,48},{80,64},{96,80},{112,96},{1... | collective-permute-start | bytes 2359304 | tf_op jit(solution)/shard_map/ppermute | solution.py:69
  56.0 16.1 %collective-permute-done.10 = bf16[512,896]{1,0:T(8,128)(2,1)} collective-permute-done((bf16[512,896]{1,0:T(8,128)(2,1)S(1)}, bf16[512,896]{1,0:T(8,128)(2,1)}, u32[]{:S(2)}, u32[]{:S(2)}) %collective-permute-start.10) | collective-permute-done | bytes 917536 | tf_op jit(solution)/shard_map/ppermute | solution.py:69
  73.8 12.8 %collective-permute-done.5 = bf16[512,768]{1,0:T(8,128)(2,1)} collective-permute-done((bf16[512,768]{1,0:T(8,128)(2,1)}, bf16[512,768]{1,0:T(8,128)(2,1)}, u32[]{:S(2)}, u32[]{:S(2)}) %collective-permute-start.5) | collective-permute-done | bytes 786464 | tf_op jit(solution)/shard_map/ppermute | solution.py:69
  86.6 2.7 %copy-done = bf16[6016,512]{1,0:T(8,128)(2,1)S(1)} copy-done((bf16[6016,512]{1,0:T(8,128)(2,1)S(1)}, bf16[6016,512]{1,0:T(8,128)(2,1)}, u32[]{:S(2)}) %copy-start) | copy-done | bytes 6160408
  97.7 3.2 %collective-permute-start.12 = (bf16[512,768]{1,0:T(8,128)(2,1)}, bf16[512,768]{1,0:T(8,128)(2,1)S(1)}, u32[]{:S(2)}, u32[]{:S(2)}) collective-permute-start(bf16[512,768]{1,0:T(8,128)(2,1)} %collective-permute-done.6), channel_id=1, source_target_pairs={{0,112},{16,0},{32,16},{48,32},{64,48},{80,64},{96,80},{112,96},{1... | collective-permute-start | bytes 2359304 | tf_op jit(solution)/shard_map/ppermute | solution.py:69
  100.9 2.7 %collective-permute-start.18 = (bf16[512,896]{1,0:T(8,128)(2,1)}, bf16[512,896]{1,0:T(8,128)(2,1)S(1)}, u32[]{:S(2)}, u32[]{:S(2)}) collective-permute-start(bf16[512,896]{1,0:T(8,128)(2,1)} %collective-permute-done.10), channel_id=1, source_target_pairs={{0,112},{16,0},{32,16},{48,32},{64,48},{80,64},{96,80},{112,96},{1... | collective-permute-start | bytes 2752520 | tf_op jit(solution)/shard_map/ppermute | solution.py:69
  103.6 2.2 %add_add_fusion.2 = f32[752,896]{1,0:T(8,128)S(1)} fusion(f32[752,896]{1,0:T(8,128)S(1)} %fusion.23, f32[752,896]{1,0:T(8,128)S(1)} %fusion.19, bf16[512,896]{1,0:T(8,128)(2,1)} %collective-permute-done.10, bf16[752,4096]{1,0:T(8,128)(2,1)S(1)} %bitcast.27), kind=kOutput, calls=%fused_computation.2 | convolution fusion | flops 691310592 | bytes 9773056 | tf_op jit(solution)/shard_map/dot_general | solution.py:83
  109.7 9.2 %collective-permute-done.11 = bf16[512,768]{1,0:T(8,128)(2,1)S(1)} collective-permute-done((bf16[512,768]{1,0:T(8,128)(2,1)}, bf16[512,768]{1,0:T(8,128)(2,1)S(1)}, u32[]{:S(2)}, u32[]{:S(2)}) %collective-permute-start.11) | collective-permute-done | bytes 786464 | tf_op jit(solution)/shard_map/ppermute | solution.py:69
  118.9 2.6 %collective-permute-start.13 = (bf16[256,768]{1,0:T(8,128)(2,1)S(1)}, bf16[256,768]{1,0:T(8,128)(2,1)S(1)}, u32[]{:S(2)}, u32[]{:S(2)}) collective-permute-start(bf16[256,768]{1,0:T(8,128)(2,1)S(1)} %slice.100), channel_id=1, source_target_pairs={{0,16},{16,32},{32,48},{48,64},{64,80},{80,96},{96,112},{112,0},{1... | collective-permute-start | bytes 1179656 | tf_op jit(solution)/shard_map/ppermute | solution.py:69
  123.7 14.9 %collective-permute-done.17 = bf16[512,896]{1,0:T(8,128)(2,1)S(1)} collective-permute-done((bf16[512,896]{1,0:T(8,128)(2,1)S(1)}, bf16[512,896]{1,0:T(8,128)(2,1)S(1)}, u32[]{:S(2)}, u32[]{:S(2)}) %collective-permute-start.17) | collective-permute-done | bytes 917536 | tf_op jit(solution)/shard_map/ppermute | solution.py:69
  138.5 2.5 %collective-permute-start.19 = (bf16[512,896]{1,0:T(8,128)(2,1)S(1)}, bf16[512,896]{1,0:T(8,128)(2,1)S(1)}, u32[]{:S(2)}, u32[]{:S(2)}) collective-permute-start(bf16[512,896]{1,0:T(8,128)(2,1)S(1)} %collective-permute-done.17), channel_id=1, source_target_pairs={{0,16},{16,32},{32,48},{48,64},{64,80},{80,96},{96,112},{112,0},{1... | collective-permute-start | bytes 2752520 | tf_op jit(solution)/shard_map/ppermute | solution.py:69
  143.6 3.3 %collective-permute-done.13 = bf16[256,768]{1,0:T(8,128)(2,1)S(1)} collective-permute-done((bf16[256,768]{1,0:T(8,128)(2,1)S(1)}, bf16[256,768]{1,0:T(8,128)(2,1)S(1)}, u32[]{:S(2)}, u32[]{:S(2)}) %collective-permute-start.13) | collective-permute-done | bytes 393248 | tf_op jit(solution)/shard_map/ppermute | solution.py:69
  147.4 18.6 %collective-permute-done.19 = bf16[512,896]{1,0:T(8,128)(2,1)S(1)} collective-permute-done((bf16[512,896]{1,0:T(8,128)(2,1)S(1)}, bf16[512,896]{1,0:T(8,128)(2,1)S(1)}, u32[]{:S(2)}, u32[]{:S(2)}) %collective-permute-start.19) | collective-permute-done | bytes 917536 | tf_op jit(solution)/shard_map/ppermute | solution.py:69
  171.9 8.3 %collective-permute-done.21 = bf16[256,896]{1,0:T(8,128)(2,1)S(1)} collective-permute-done((bf16[256,896]{1,0:T(8,128)(2,1)S(1)}, bf16[256,896]{1,0:T(8,128)(2,1)S(1)}, u32[]{:S(2)}, u32[]{:S(2)}) %collective-permute-start.21) | collective-permute-done | bytes 458784 | tf_op jit(solution)/shard_map/ppermute | solution.py:69
  186.5 2.4 %collective-permute-start.24 = (bf16[376,896]{1,0:T(8,128)(2,1)S(1)}, bf16[376,896]{1,0:T(8,128)(2,1)S(1)}, u32[]{:S(2)}, u32[]{:S(2)}) collective-permute-start(bf16[376,896]{1,0:T(8,128)(2,1)S(1)} %multiply_convert_fusion), channel_id=1, source_target_pairs={{0,0},{1,128},{128,129},{129,1},{2,2},{3,130},{130,131},{131,3},{4... | collective-permute-start | bytes 2021384 | tf_op jit(solution)/shard_map/ppermute | solution.py:105
  191.3 14.4 %collective-permute-done.16 = bf16[376,768]{1,0:T(8,128)(2,1)S(1)} collective-permute-done((bf16[376,768]{1,0:T(8,128)(2,1)S(1)}, bf16[376,768]{1,0:T(8,128)(2,1)S(1)}, u32[]{:S(2)}, u32[]{:S(2)}) %collective-permute-start.16) | collective-permute-done | bytes 577568 | tf_op jit(solution)/shard_map/ppermute | solution.py:105
  (75 shorter events, 42.6 us)
Async XLA Ops:
  6.5 80.1 %all-gather.3.cloned.1.call-start = ((), (), s32[]{:S(2)}) async-start(), calls=%async_computation | async-start | bytes 6545408 | tf_op jit(solution)/shard_map/all_gather | solution.py:114
  13.0 5.8 %collective-permute-start.1 = (bf16[256,768]{1,0:T(8,128)(2,1)S(1)}, bf16[256,768]{1,0:T(8,128)(2,1)S(1)}, u32[]{:S(2)}, u32[]{:S(2)}) collective-permute-start(bf16[256,768]{1,0:T(8,128)(2,1)S(1)} %get-tuple-element.81), channel_id=1, source_target_pairs={{0,1},{1,129},{128,0},{129,128},{2,3},{3,131},{130,2},{131,130},{4... | collective-permute-start | bytes 1179656 | tf_op jit(solution)/shard_map/ppermute | solution.py:92
  14.1 12.2 %collective-permute-start.2 = (bf16[256,768]{1,0:T(8,128)(2,1)S(1)}, bf16[256,768]{1,0:T(8,128)(2,1)S(1)}, u32[]{:S(2)}, u32[]{:S(2)}) collective-permute-start(bf16[256,768]{1,0:T(8,128)(2,1)S(1)} %get-tuple-element.82), channel_id=1, source_target_pairs={{0,0},{1,128},{128,1},{129,129},{2,2},{3,130},{130,3},{131,131},{4... | collective-permute-start | bytes 1179656 | tf_op jit(solution)/shard_map/ppermute | solution.py:91
  26.5 9.9 %collective-permute-start.7 = (bf16[256,896]{1,0:T(8,128)(2,1)S(1)}, bf16[256,896]{1,0:T(8,128)(2,1)S(1)}, u32[]{:S(2)}, u32[]{:S(2)}) collective-permute-start(bf16[256,896]{1,0:T(8,128)(2,1)S(1)} %get-tuple-element.77), channel_id=1, source_target_pairs={{0,1},{1,129},{128,0},{129,128},{2,3},{3,131},{130,2},{131,130},{4... | collective-permute-start | bytes 1376264 | tf_op jit(solution)/shard_map/ppermute | solution.py:92
  26.6 18.3 %collective-permute-start.8 = (bf16[256,896]{1,0:T(8,128)(2,1)S(1)}, bf16[256,896]{1,0:T(8,128)(2,1)S(1)}, u32[]{:S(2)}, u32[]{:S(2)}) collective-permute-start(bf16[256,896]{1,0:T(8,128)(2,1)S(1)} %get-tuple-element.78), channel_id=1, source_target_pairs={{0,0},{1,128},{128,1},{129,129},{2,2},{3,130},{130,3},{131,131},{4... | collective-permute-start | bytes 1376264 | tf_op jit(solution)/shard_map/ppermute | solution.py:91
  29.6 20.5 %collective-permute-start.3 = (bf16[512,768]{1,0:T(8,128)(2,1)S(1)}, bf16[512,768]{1,0:T(8,128)(2,1)}, u32[]{:S(2)}, u32[]{:S(2)}) collective-permute-start(bf16[512,768]{1,0:T(8,128)(2,1)S(1)} %pad_maximum_fusion.2), channel_id=1, source_target_pairs={{0,16},{16,32},{32,48},{48,64},{64,80},{80,96},{96,112},{112,0},{1... | collective-permute-start | bytes 2359304 | tf_op jit(solution)/shard_map/ppermute | solution.py:69
  31.0 21.5 %collective-permute-start.4 = (bf16[512,768]{1,0:T(8,128)(2,1)S(1)}, bf16[512,768]{1,0:T(8,128)(2,1)}, u32[]{:S(2)}, u32[]{:S(2)}) collective-permute-start(bf16[512,768]{1,0:T(8,128)(2,1)S(1)} %pad_maximum_fusion.2), channel_id=1, source_target_pairs={{0,112},{16,0},{32,16},{48,32},{64,48},{80,64},{96,80},{112,96},{1... | collective-permute-start | bytes 2359304 | tf_op jit(solution)/shard_map/ppermute | solution.py:69
  45.1 27.0 %collective-permute-start.10 = (bf16[512,896]{1,0:T(8,128)(2,1)S(1)}, bf16[512,896]{1,0:T(8,128)(2,1)}, u32[]{:S(2)}, u32[]{:S(2)}) collective-permute-start(bf16[512,896]{1,0:T(8,128)(2,1)S(1)} %pad_maximum_fusion.1), channel_id=1, source_target_pairs={{0,112},{16,0},{32,16},{48,32},{64,48},{80,64},{96,80},{112,96},{1... | collective-permute-start | bytes 2752520 | tf_op jit(solution)/shard_map/ppermute | solution.py:69
  50.1 23.7 %collective-permute-start.9 = (bf16[512,896]{1,0:T(8,128)(2,1)S(1)}, bf16[512,896]{1,0:T(8,128)(2,1)S(1)}, u32[]{:S(2)}, u32[]{:S(2)}) collective-permute-start(bf16[512,896]{1,0:T(8,128)(2,1)S(1)} %pad_maximum_fusion.1), channel_id=1, source_target_pairs={{0,16},{16,32},{32,48},{48,64},{64,80},{80,96},{96,112},{112,0},{1... | collective-permute-start | bytes 2752520 | tf_op jit(solution)/shard_map/ppermute | solution.py:69
  52.4 34.2 %collective-permute-start.5 = (bf16[512,768]{1,0:T(8,128)(2,1)}, bf16[512,768]{1,0:T(8,128)(2,1)}, u32[]{:S(2)}, u32[]{:S(2)}) collective-permute-start(bf16[512,768]{1,0:T(8,128)(2,1)} %collective-permute-done.3), channel_id=1, source_target_pairs={{0,16},{16,32},{32,48},{48,64},{64,80},{80,96},{96,112},{112,0},{1... | collective-permute-start | bytes 2359304 | tf_op jit(solution)/shard_map/ppermute | solution.py:69
  52.5 34.1 %collective-permute-start.6 = (bf16[512,768]{1,0:T(8,128)(2,1)}, bf16[512,768]{1,0:T(8,128)(2,1)}, u32[]{:S(2)}, u32[]{:S(2)}) collective-permute-start(bf16[512,768]{1,0:T(8,128)(2,1)} %collective-permute-done.4), channel_id=1, source_target_pairs={{0,112},{16,0},{32,16},{48,32},{64,48},{80,64},{96,80},{112,96},{1... | collective-permute-start | bytes 2359304 | tf_op jit(solution)/shard_map/ppermute | solution.py:69
  97.6 21.3 %collective-permute-start.11 = (bf16[512,768]{1,0:T(8,128)(2,1)}, bf16[512,768]{1,0:T(8,128)(2,1)S(1)}, u32[]{:S(2)}, u32[]{:S(2)}) collective-permute-start(bf16[512,768]{1,0:T(8,128)(2,1)} %collective-permute-done.5), channel_id=1, source_target_pairs={{0,16},{16,32},{32,48},{48,64},{64,80},{80,96},{96,112},{112,0},{1... | collective-permute-start | bytes 2359304 | tf_op jit(solution)/shard_map/ppermute | solution.py:69
  97.7 21.2 %collective-permute-start.12 = (bf16[512,768]{1,0:T(8,128)(2,1)}, bf16[512,768]{1,0:T(8,128)(2,1)S(1)}, u32[]{:S(2)}, u32[]{:S(2)}) collective-permute-start(bf16[512,768]{1,0:T(8,128)(2,1)} %collective-permute-done.6), channel_id=1, source_target_pairs={{0,112},{16,0},{32,16},{48,32},{64,48},{80,64},{96,80},{112,96},{1... | collective-permute-start | bytes 2359304 | tf_op jit(solution)/shard_map/ppermute | solution.py:69
  100.9 37.6 %collective-permute-start.17 = (bf16[512,896]{1,0:T(8,128)(2,1)S(1)}, bf16[512,896]{1,0:T(8,128)(2,1)S(1)}, u32[]{:S(2)}, u32[]{:S(2)}) collective-permute-start(bf16[512,896]{1,0:T(8,128)(2,1)S(1)} %collective-permute-done.9), channel_id=1, source_target_pairs={{0,16},{16,32},{32,48},{48,64},{64,80},{80,96},{96,112},{112,0},{1... | collective-permute-start | bytes 2752520 | tf_op jit(solution)/shard_map/ppermute | solution.py:69
  100.9 37.6 %collective-permute-start.18 = (bf16[512,896]{1,0:T(8,128)(2,1)}, bf16[512,896]{1,0:T(8,128)(2,1)S(1)}, u32[]{:S(2)}, u32[]{:S(2)}) collective-permute-start(bf16[512,896]{1,0:T(8,128)(2,1)} %collective-permute-done.10), channel_id=1, source_target_pairs={{0,112},{16,0},{32,16},{48,32},{64,48},{80,64},{96,80},{112,96},{1... | collective-permute-start | bytes 2752520 | tf_op jit(solution)/shard_map/ppermute | solution.py:69
  118.9 28.1 %collective-permute-start.13 = (bf16[256,768]{1,0:T(8,128)(2,1)S(1)}, bf16[256,768]{1,0:T(8,128)(2,1)S(1)}, u32[]{:S(2)}, u32[]{:S(2)}) collective-permute-start(bf16[256,768]{1,0:T(8,128)(2,1)S(1)} %slice.100), channel_id=1, source_target_pairs={{0,16},{16,32},{32,48},{48,64},{64,80},{80,96},{96,112},{112,0},{1... | collective-permute-start | bytes 1179656 | tf_op jit(solution)/shard_map/ppermute | solution.py:69
  121.5 25.5 %collective-permute-start.14 = (bf16[256,768]{1,0:T(8,128)(2,1)S(1)}, bf16[256,768]{1,0:T(8,128)(2,1)S(1)}, u32[]{:S(2)}, u32[]{:S(2)}) collective-permute-start(bf16[256,768]{1,0:T(8,128)(2,1)S(1)} %slice.101), channel_id=1, source_target_pairs={{0,112},{16,0},{32,16},{48,32},{64,48},{80,64},{96,80},{112,96},{1... | collective-permute-start | bytes 1179656 | tf_op jit(solution)/shard_map/ppermute | solution.py:69
  138.5 27.5 %collective-permute-start.19 = (bf16[512,896]{1,0:T(8,128)(2,1)S(1)}, bf16[512,896]{1,0:T(8,128)(2,1)S(1)}, u32[]{:S(2)}, u32[]{:S(2)}) collective-permute-start(bf16[512,896]{1,0:T(8,128)(2,1)S(1)} %collective-permute-done.17), channel_id=1, source_target_pairs={{0,16},{16,32},{32,48},{48,64},{64,80},{80,96},{96,112},{112,0},{1... | collective-permute-start | bytes 2752520 | tf_op jit(solution)/shard_map/ppermute | solution.py:69
  141.0 25.2 %collective-permute-start.20 = (bf16[512,896]{1,0:T(8,128)(2,1)S(1)}, bf16[512,896]{1,0:T(8,128)(2,1)S(1)}, u32[]{:S(2)}, u32[]{:S(2)}) collective-permute-start(bf16[512,896]{1,0:T(8,128)(2,1)S(1)} %collective-permute-done.18), channel_id=1, source_target_pairs={{0,112},{16,0},{32,16},{48,32},{64,48},{80,64},{96,80},{112,96},{1... | collective-permute-start | bytes 2752520 | tf_op jit(solution)/shard_map/ppermute | solution.py:69
  166.3 13.9 %collective-permute-start.21 = (bf16[256,896]{1,0:T(8,128)(2,1)S(1)}, bf16[256,896]{1,0:T(8,128)(2,1)S(1)}, u32[]{:S(2)}, u32[]{:S(2)}) collective-permute-start(bf16[256,896]{1,0:T(8,128)(2,1)S(1)} %slice.105), channel_id=1, source_target_pairs={{0,16},{16,32},{32,48},{48,64},{64,80},{80,96},{96,112},{112,0},{1... | collective-permute-start | bytes 1376264 | tf_op jit(solution)/shard_map/ppermute | solution.py:69
  167.8 12.8 %collective-permute-start.22 = (bf16[256,896]{1,0:T(8,128)(2,1)S(1)}, bf16[256,896]{1,0:T(8,128)(2,1)S(1)}, u32[]{:S(2)}, u32[]{:S(2)}) collective-permute-start(bf16[256,896]{1,0:T(8,128)(2,1)S(1)} %slice.106), channel_id=1, source_target_pairs={{0,112},{16,0},{32,16},{48,32},{64,48},{80,64},{96,80},{112,96},{1... | collective-permute-start | bytes 1376264 | tf_op jit(solution)/shard_map/ppermute | solution.py:69
  184.1 4.8 %collective-permute-start.15 = (f32[376,768]{1,0:T(8,128)S(1)}, f32[376,768]{1,0:T(8,128)S(1)}, u32[]{:S(2)}, u32[]{:S(2)}) collective-permute-start(f32[376,768]{1,0:T(8,128)S(1)} %slice_select_fusion.1), channel_id=1, source_target_pairs={{0,1},{1,0},{2,3},{3,2},{4,5},{5,4},{6,7},{7,6},{8,9},{9,8},{10,11... | collective-permute-start | bytes 3465224 | tf_op jit(solution)/shard_map/ppermute | solution.py:18
  186.5 19.2 %collective-permute-start.24 = (bf16[376,896]{1,0:T(8,128)(2,1)S(1)}, bf16[376,896]{1,0:T(8,128)(2,1)S(1)}, u32[]{:S(2)}, u32[]{:S(2)}) collective-permute-start(bf16[376,896]{1,0:T(8,128)(2,1)S(1)} %multiply_convert_fusion), channel_id=1, source_target_pairs={{0,0},{1,128},{128,129},{129,1},{2,2},{3,130},{130,131},{131,3},{4... | collective-permute-start | bytes 2021384 | tf_op jit(solution)/shard_map/ppermute | solution.py:105
  189.2 16.5 %collective-permute-start.16 = (bf16[376,768]{1,0:T(8,128)(2,1)S(1)}, bf16[376,768]{1,0:T(8,128)(2,1)S(1)}, u32[]{:S(2)}, u32[]{:S(2)}) collective-permute-start(bf16[376,768]{1,0:T(8,128)(2,1)S(1)} %multiply_convert_fusion.1), channel_id=1, source_target_pairs={{0,0},{1,128},{128,129},{129,1},{2,2},{3,130},{130,131},{131,3},{4... | collective-permute-start | bytes 1732616 | tf_op jit(solution)/shard_map/ppermute | solution.py:105
  (6 other events, 35.0 us)
Sparse Core Ops, SparseCore 0:
  13.0 72.2 all-gather.2

commit v4 on v3

--- a/solution.py
+++ b/solution.py
@@ -7,7 +7,7 @@
 
 AXES = ("xh", "z", "xl", "y", "core")
 SIZES = (2, 8, 2, 4, 2)
-WIDTHS = (768, 896)
+WIDTHS = (896, 768)
 
 TURN = [(h * 2 + c, c * 2 + h) for h in range(2) for c in range(2)]
 CROSS = [(h * 2 + c, c * 2 + 1 - h) for h in range(2) for c in range(2)]
@@ -110,33 +110,40 @@
     half = weight.shape[0] // 2
     parts = [weight[:, : WIDTHS[0]], weight[:, WIDTHS[0] :]]
     near = tokens_of_core(tokens)
-    near, parts[0] = together(near, parts[0])
-    plane = lax.all_gather(near[None], ("xh", "xl", "y"), axis=0, tiled=True)
+    plane = lax.all_to_all(
+        jnp.broadcast_to(near, (16, *near.shape)), ("xh", "xl", "y"), 0, 0, tiled=True
+    )
     mine = swapped(parts[0])
     mine, parts[1] = together(mine, parts[1])
     mine = [mine, swapped(parts[1])]
     front = [(value, value) for value in mine]
     blocks = [[(0, value)] for value in mine]
     totals = [0, 0]
-    gathered = None
+    outs = [None, None]
+
+    def fold(chunk, count):
+        totals[chunk] += product(gathered, blocks[chunk][:count], half)
+        del blocks[chunk][:count]
+
     for step in range(1, 5):
         for chunk in range(2):
-            if step == 2 and chunk:
-                gathered, *front[1] = together(order_tokens(plane, rows), *front[1])
-            if step > 2:
-                totals[chunk] += product(gathered, blocks[chunk][:-2], half)
-                blocks[chunk] = blocks[chunk][-2:]
-                *front[chunk], totals[chunk] = together(*front[chunk], totals[chunk])
-                blocks[chunk] = [(blocks[chunk][i][0], front[chunk][i]) for i in range(2)]
-            up, down = together(*step_along_z(step, *front[chunk]))
+            if step == 3 and not chunk:
+                gathered, *front[0] = together(order_tokens(plane, rows), *front[0])
+            if step == 4 and chunk:
+                fold(0, 9)
+                outs[0] = home(activate(totals[0]))
+            up, down = step_along_z(step, *front[chunk])
+            if step == 4 and chunk:
+                up, down, outs[0] = together(up, down, outs[0])
+            else:
+                up, down = together(up, down)
             front[chunk] = (up, down)
             if step == 4:
                 blocks[chunk] += [(8, up), (9, down)]
             else:
                 blocks[chunk] += [(2 * step, up), (2 * (8 - step), down)]
-    outs = [
-        home(activate(totals[chunk] + product(gathered, blocks[chunk], half))) for chunk in range(2)
-    ]
+    fold(1, 9)
+    outs[1] = home(activate(totals[1]))
     return jnp.concatenate(outs, axis=1)
 
 

time: 214 us -> 321 us (1.50)
  the two profiles are of different devices: /device:TPU:1 before, /device:TPU:3 now
where the time goes in v4:
time: 321 us
  waiting for transfers between devices  226 us (70%)
  starting transfers between devices  52.1 us (16%)
  matrix products  25 us (8%)
  other arithmetic  6.66 us (2%)
  local copies, waits for them, and re-layouts  6.23 us (2%)
  Pallas kernels  3.89 us (1%)
    ppermute x16, waiting for transfers between devices, along_z(): return lax.ppermute(value, 'z', [(i, (i + shift) % 8) for i in range(8)])  90.2 us
    ppermute x2, waiting for transfers between devices, swapped(): crossed = lax.ppermute(second, ('xh', 'core'), CROSS)  67.4 us
    ppermute x2, waiting for transfers between devices, swapped(): turned = lax.ppermute(first, ('xh', 'core'), TURN)  48.1 us
    ppermute x16, starting transfers between devices, along_z(): return lax.ppermute(value, 'z', [(i, (i + shift) % 8) for i in range(8)])  29 us
    dot_general x18, matrix products, product(): total += jnp.dot(features, piece, preferred_element_type=jnp.float32)  25 us
    ppermute x2, waiting for transfers between devices, home(): return lax.ppermute(out, ('xh', 'core'), HOME)  16.7 us
    all_to_all x1, starting transfers between devices, on_device(): lax.all_to_all(jnp.broadcast_to(near, (16, *near.shape)), ('xh', 'xl', 'y...  7.05 us
  transfers between devices with their start and end apart: 26, of which 14 were waited for; matrix products, arithmetic and copies ran while one was open for 9% of the time, Pallas kernels for 1%

profile of v4, /device:TPU:3, one launch (start us, length us, event | category | flops | bytes accessed | tf_op | source)
XLA Modules:
  0.0 320.6 jit_solution(7110289927277363438)
XLA Ops:
  4.0 3.0 broadcast_in_dim.3
  6.9 7.0 %all-to-all-start = ((bf16[16,376,512]{2,1,0:T(8,128)(2,1)}), bf16[16,376,512]{2,1,0:T(8,128)(2,1)}, u32[]{:S(2)}, u32[]{:S(2)}) async-start(bf16[16,376,512]{2,1,0:T(8,128)(2,1)} %broadcast_in_dim.3), calls=%async_computation | async-start | bytes 12320768 | tf_op jit(solution)/shard_map/all_to_all | solution.py:113
  16.7 4.3 %collective-permute-start.1 = (bf16[256,896]{1,0:T(8,128)(2,1)S(1)}, bf16[256,896]{1,0:T(8,128)(2,1)}, u32[]{:S(2)}, u32[]{:S(2)}) collective-permute-start(bf16[256,896]{1,0:T(8,128)(2,1)S(1)} %get-tuple-element.50), channel_id=1, source_target_pairs={{0,0},{1,128},{128,1},{129,129},{2,2},{3,130},{130,3},{131,131},{4... | collective-permute-start | bytes 1376264 | tf_op jit(solution)/shard_map/ppermute | solution.py:91
  21.0 67.4 %collective-permute-done = bf16[256,896]{1,0:T(8,128)(2,1)S(1)} collective-permute-done((bf16[256,896]{1,0:T(8,128)(2,1)}, bf16[256,896]{1,0:T(8,128)(2,1)S(1)}, u32[]{:S(2)}, u32[]{:S(2)}) %collective-permute-start) | collective-permute-done | bytes 458784 | tf_op jit(solution)/shard_map/ppermute | solution.py:92
  88.4 44.9 %collective-permute-done.1 = bf16[256,896]{1,0:T(8,128)(2,1)} collective-permute-done((bf16[256,896]{1,0:T(8,128)(2,1)S(1)}, bf16[256,896]{1,0:T(8,128)(2,1)}, u32[]{:S(2)}, u32[]{:S(2)}) %collective-permute-start.1) | collective-permute-done | bytes 458784 | tf_op jit(solution)/shard_map/ppermute | solution.py:91
  138.3 4.0 %collective-permute-start.14 = (bf16[512,896]{1,0:T(8,128)(2,1)S(1)}, bf16[512,896]{1,0:T(8,128)(2,1)S(1)}, u32[]{:S(2)}, u32[]{:S(2)}) collective-permute-start(bf16[512,896]{1,0:T(8,128)(2,1)S(1)} %pad_maximum_fusion.1), channel_id=1, source_target_pairs={{0,112},{16,0},{32,16},{48,32},{64,48},{80,64},{96,80},{112,96},{1... | collective-permute-start | bytes 2752520 | tf_op jit(solution)/shard_map/ppermute | solution.py:69
  142.3 3.2 %collective-permute-done.3 = bf16[256,768]{1,0:T(8,128)(2,1)S(1)} collective-permute-done((bf16[256,768]{1,0:T(8,128)(2,1)S(1)}, bf16[256,768]{1,0:T(8,128)(2,1)S(1)}, u32[]{:S(2)}, u32[]{:S(2)}) %collective-permute-start.3) | collective-permute-done | bytes 393248 | tf_op jit(solution)/shard_map/ppermute | solution.py:91
  147.1 4.3 %collective-permute-start.5 = (bf16[512,768]{1,0:T(8,128)(2,1)S(1)}, bf16[512,768]{1,0:T(8,128)(2,1)}, u32[]{:S(2)}, u32[]{:S(2)}) collective-permute-start(bf16[512,768]{1,0:T(8,128)(2,1)S(1)} %pad_maximum_fusion.2), channel_id=1, source_target_pairs={{0,112},{16,0},{32,16},{48,32},{64,48},{80,64},{96,80},{112,96},{1... | collective-permute-start | bytes 2359304 | tf_op jit(solution)/shard_map/ppermute | solution.py:69
  151.4 11.6 %collective-permute-done.13 = bf16[512,896]{1,0:T(8,128)(2,1)S(1)} collective-permute-done((bf16[512,896]{1,0:T(8,128)(2,1)S(1)}, bf16[512,896]{1,0:T(8,128)(2,1)S(1)}, u32[]{:S(2)}, u32[]{:S(2)}) %collective-permute-start.13) | collective-permute-done | bytes 917536 | tf_op jit(solution)/shard_map/ppermute | solution.py:69
  163.1 3.0 collective-permute-start.16
  166.1 13.9 %collective-permute-done.4 = bf16[512,768]{1,0:T(8,128)(2,1)S(1)} collective-permute-done((bf16[512,768]{1,0:T(8,128)(2,1)S(1)}, bf16[512,768]{1,0:T(8,128)(2,1)S(1)}, u32[]{:S(2)}, u32[]{:S(2)}) %collective-permute-start.4) | collective-permute-done | bytes 786464 | tf_op jit(solution)/shard_map/ppermute | solution.py:69
  180.1 2.8 collective-permute-start.7
  182.9 16.8 %collective-permute-done.15 = bf16[512,896]{1,0:T(8,128)(2,1)} collective-permute-done((bf16[512,896]{1,0:T(8,128)(2,1)S(1)}, bf16[512,896]{1,0:T(8,128)(2,1)}, u32[]{:S(2)}, u32[]{:S(2)}) %collective-permute-start.15) | collective-permute-done | bytes 917536 | tf_op jit(solution)/shard_map/ppermute | solution.py:69
  199.7 16.1 %collective-permute-done.6 = bf16[512,768]{1,0:T(8,128)(2,1)} collective-permute-done((bf16[512,768]{1,0:T(8,128)(2,1)S(1)}, bf16[512,768]{1,0:T(8,128)(2,1)}, u32[]{:S(2)}, u32[]{:S(2)}) %collective-permute-start.6) | collective-permute-done | bytes 786464 | tf_op jit(solution)/shard_map/ppermute | solution.py:69
  215.8 3.0 collective-permute-start.9
  218.8 3.9 %shard_map.28 = bf16[2,376,4096]{2,1,0:T(8,128)(2,1)S(1)} custom-call(s32[3]{0:T(128)S(1)} %pad_add_fusion.place, bf16[16,376,512]{2,1,0:T(8,128)(2,1)} %all-to-all-done.plane), custom_call_target="tpu_custom_call" | custom-call | bytes 12320768 | tf_op jit(solution)/shard_map/pallas_call | solution.py:51
  227.1 2.7 collective-permute-start.18
  232.7 23.6 %collective-permute-done.17 = bf16[512,896]{1,0:T(8,128)(2,1)S(1)} collective-permute-done((bf16[512,896]{1,0:T(8,128)(2,1)}, bf16[512,896]{1,0:T(8,128)(2,1)S(1)}, u32[]{:S(2)}, u32[]{:S(2)}) %collective-permute-start.17) | collective-permute-done | bytes 917536 | tf_op jit(solution)/shard_map/ppermute | solution.py:69
  261.1 7.6 %collective-permute-done.19 = bf16[256,896]{1,0:T(8,128)(2,1)S(1)} collective-permute-done((bf16[256,896]{1,0:T(8,128)(2,1)S(1)}, bf16[256,896]{1,0:T(8,128)(2,1)S(1)}, u32[]{:S(2)}, u32[]{:S(2)}) %collective-permute-start.19) | collective-permute-done | bytes 458784 | tf_op jit(solution)/shard_map/ppermute | solution.py:69
  270.7 2.7 add_add_fusion
  273.5 2.5 collective-permute-start.21
  295.1 7.3 %collective-permute-done.22 = bf16[376,896]{1,0:T(8,128)(2,1)S(1)} collective-permute-done((bf16[376,896]{1,0:T(8,128)(2,1)S(1)}, bf16[376,896]{1,0:T(8,128)(2,1)S(1)}, u32[]{:S(2)}, u32[]{:S(2)}) %collective-permute-start.22) | collective-permute-done | bytes 673824 | tf_op jit(solution)/shard_map/ppermute | solution.py:105
  304.3 2.8 collective-permute-done.23
  310.0 9.5 %collective-permute-done.24 = bf16[376,768]{1,0:T(8,128)(2,1)S(1)} collective-permute-done((bf16[376,768]{1,0:T(8,128)(2,1)S(1)}, bf16[376,768]{1,0:T(8,128)(2,1)S(1)}, u32[]{:S(2)}, u32[]{:S(2)}) %collective-permute-start.24) | collective-permute-done | bytes 577568 | tf_op jit(solution)/shard_map/ppermute | solution.py:105
  (85 shorter events, 52.3 us)
Async XLA Ops:
  6.9 211.9 %all-to-all-start = ((bf16[16,376,512]{2,1,0:T(8,128)(2,1)}), bf16[16,376,512]{2,1,0:T(8,128)(2,1)}, u32[]{:S(2)}, u32[]{:S(2)}) async-start(bf16[16,376,512]{2,1,0:T(8,128)(2,1)} %broadcast_in_dim.3), calls=%async_computation | async-start | bytes 12320768 | tf_op jit(solution)/shard_map/all_to_all | solution.py:113
  14.9 73.5 %collective-permute-start = (bf16[256,896]{1,0:T(8,128)(2,1)}, bf16[256,896]{1,0:T(8,128)(2,1)S(1)}, u32[]{:S(2)}, u32[]{:S(2)}) collective-permute-start(bf16[256,896]{1,0:T(8,128)(2,1)} %get-tuple-element.49), channel_id=1, source_target_pairs={{0,1},{1,129},{128,0},{129,128},{2,3},{3,131},{130,2},{131,130},{4... | collective-permute-start | bytes 1376264 | tf_op jit(solution)/shard_map/ppermute | solution.py:92
  16.7 116.6 %collective-permute-start.1 = (bf16[256,896]{1,0:T(8,128)(2,1)S(1)}, bf16[256,896]{1,0:T(8,128)(2,1)}, u32[]{:S(2)}, u32[]{:S(2)}) collective-permute-start(bf16[256,896]{1,0:T(8,128)(2,1)S(1)} %get-tuple-element.50), channel_id=1, source_target_pairs={{0,0},{1,128},{128,1},{129,129},{2,2},{3,130},{130,3},{131,131},{4... | collective-permute-start | bytes 1376264 | tf_op jit(solution)/shard_map/ppermute | solution.py:91
  134.6 7.8 %collective-permute-start.2 = (bf16[256,768]{1,0:T(8,128)(2,1)S(1)}, bf16[256,768]{1,0:T(8,128)(2,1)S(1)}, u32[]{:S(2)}, u32[]{:S(2)}) collective-permute-start(bf16[256,768]{1,0:T(8,128)(2,1)S(1)} %get-tuple-element.55), channel_id=1, source_target_pairs={{0,1},{1,129},{128,0},{129,128},{2,3},{3,131},{130,2},{131,130},{4... | collective-permute-start | bytes 1179656 | tf_op jit(solution)/shard_map/ppermute | solution.py:92
  134.7 10.9 %collective-permute-start.3 = (bf16[256,768]{1,0:T(8,128)(2,1)S(1)}, bf16[256,768]{1,0:T(8,128)(2,1)S(1)}, u32[]{:S(2)}, u32[]{:S(2)}) collective-permute-start(bf16[256,768]{1,0:T(8,128)(2,1)S(1)} %get-tuple-element.56), channel_id=1, source_target_pairs={{0,0},{1,128},{128,1},{129,129},{2,2},{3,130},{130,3},{131,131},{4... | collective-permute-start | bytes 1179656 | tf_op jit(solution)/shard_map/ppermute | solution.py:91
  136.6 26.5 %collective-permute-start.13 = (bf16[512,896]{1,0:T(8,128)(2,1)S(1)}, bf16[512,896]{1,0:T(8,128)(2,1)S(1)}, u32[]{:S(2)}, u32[]{:S(2)}) collective-permute-start(bf16[512,896]{1,0:T(8,128)(2,1)S(1)} %pad_maximum_fusion.1), channel_id=1, source_target_pairs={{0,16},{16,32},{32,48},{48,64},{64,80},{80,96},{96,112},{112,0},{1... | collective-permute-start | bytes 2752520 | tf_op jit(solution)/shard_map/ppermute | solution.py:69
  138.3 24.8 %collective-permute-start.14 = (bf16[512,896]{1,0:T(8,128)(2,1)S(1)}, bf16[512,896]{1,0:T(8,128)(2,1)S(1)}, u32[]{:S(2)}, u32[]{:S(2)}) collective-permute-start(bf16[512,896]{1,0:T(8,128)(2,1)S(1)} %pad_maximum_fusion.1), channel_id=1, source_target_pairs={{0,112},{16,0},{32,16},{48,32},{64,48},{80,64},{96,80},{112,96},{1... | collective-permute-start | bytes 2752520 | tf_op jit(solution)/shard_map/ppermute | solution.py:69
  145.7 34.3 %collective-permute-start.4 = (bf16[512,768]{1,0:T(8,128)(2,1)S(1)}, bf16[512,768]{1,0:T(8,128)(2,1)S(1)}, u32[]{:S(2)}, u32[]{:S(2)}) collective-permute-start(bf16[512,768]{1,0:T(8,128)(2,1)S(1)} %pad_maximum_fusion.2), channel_id=1, source_target_pairs={{0,16},{16,32},{32,48},{48,64},{64,80},{80,96},{96,112},{112,0},{1... | collective-permute-start | bytes 2359304 | tf_op jit(solution)/shard_map/ppermute | solution.py:69
  147.1 32.9 %collective-permute-start.5 = (bf16[512,768]{1,0:T(8,128)(2,1)S(1)}, bf16[512,768]{1,0:T(8,128)(2,1)}, u32[]{:S(2)}, u32[]{:S(2)}) collective-permute-start(bf16[512,768]{1,0:T(8,128)(2,1)S(1)} %pad_maximum_fusion.2), channel_id=1, source_target_pairs={{0,112},{16,0},{32,16},{48,32},{64,48},{80,64},{96,80},{112,96},{1... | collective-permute-start | bytes 2359304 | tf_op jit(solution)/shard_map/ppermute | solution.py:69
  163.1 36.6 %collective-permute-start.15 = (bf16[512,896]{1,0:T(8,128)(2,1)S(1)}, bf16[512,896]{1,0:T(8,128)(2,1)}, u32[]{:S(2)}, u32[]{:S(2)}) collective-permute-start(bf16[512,896]{1,0:T(8,128)(2,1)S(1)} %collective-permute-done.13), channel_id=1, source_target_pairs={{0,16},{16,32},{32,48},{48,64},{64,80},{80,96},{96,112},{112,0},{1... | collective-permute-start | bytes 2752520 | tf_op jit(solution)/shard_map/ppermute | solution.py:69
  163.1 36.6 %collective-permute-start.16 = (bf16[512,896]{1,0:T(8,128)(2,1)S(1)}, bf16[512,896]{1,0:T(8,128)(2,1)}, u32[]{:S(2)}, u32[]{:S(2)}) collective-permute-start(bf16[512,896]{1,0:T(8,128)(2,1)S(1)} %collective-permute-done.14), channel_id=1, source_target_pairs={{0,112},{16,0},{32,16},{48,32},{64,48},{80,64},{96,80},{112,96},{1... | collective-permute-start | bytes 2752520 | tf_op jit(solution)/shard_map/ppermute | solution.py:69
  180.1 35.7 %collective-permute-start.6 = (bf16[512,768]{1,0:T(8,128)(2,1)S(1)}, bf16[512,768]{1,0:T(8,128)(2,1)}, u32[]{:S(2)}, u32[]{:S(2)}) collective-permute-start(bf16[512,768]{1,0:T(8,128)(2,1)S(1)} %collective-permute-done.4), channel_id=1, source_target_pairs={{0,16},{16,32},{32,48},{48,64},{64,80},{80,96},{96,112},{112,0},{1... | collective-permute-start | bytes 2359304 | tf_op jit(solution)/shard_map/ppermute | solution.py:69
  180.1 35.7 %collective-permute-start.7 = (bf16[512,768]{1,0:T(8,128)(2,1)}, bf16[512,768]{1,0:T(8,128)(2,1)}, u32[]{:S(2)}, u32[]{:S(2)}) collective-permute-start(bf16[512,768]{1,0:T(8,128)(2,1)} %collective-permute-done.5), channel_id=1, source_target_pairs={{0,112},{16,0},{32,16},{48,32},{64,48},{80,64},{96,80},{112,96},{1... | collective-permute-start | bytes 2359304 | tf_op jit(solution)/shard_map/ppermute | solution.py:69
  215.8 60.2 %collective-permute-start.8 = (bf16[512,768]{1,0:T(8,128)(2,1)}, bf16[512,768]{1,0:T(8,128)(2,1)}, u32[]{:S(2)}, u32[]{:S(2)}) collective-permute-start(bf16[512,768]{1,0:T(8,128)(2,1)} %collective-permute-done.6), channel_id=1, source_target_pairs={{0,16},{16,32},{32,48},{48,64},{64,80},{80,96},{96,112},{112,0},{1... | collective-permute-start | bytes 2359304 | tf_op jit(solution)/shard_map/ppermute | solution.py:69
  215.8 60.2 %collective-permute-start.9 = (bf16[512,768]{1,0:T(8,128)(2,1)}, bf16[512,768]{1,0:T(8,128)(2,1)}, u32[]{:S(2)}, u32[]{:S(2)}) collective-permute-start(bf16[512,768]{1,0:T(8,128)(2,1)} %collective-permute-done.7), channel_id=1, source_target_pairs={{0,112},{16,0},{32,16},{48,32},{64,48},{80,64},{96,80},{112,96},{1... | collective-permute-start | bytes 2359304 | tf_op jit(solution)/shard_map/ppermute | solution.py:69
  227.0 29.2 %collective-permute-start.17 = (bf16[512,896]{1,0:T(8,128)(2,1)}, bf16[512,896]{1,0:T(8,128)(2,1)S(1)}, u32[]{:S(2)}, u32[]{:S(2)}) collective-permute-start(bf16[512,896]{1,0:T(8,128)(2,1)} %collective-permute-done.15), channel_id=1, source_target_pairs={{0,16},{16,32},{32,48},{48,64},{64,80},{80,96},{96,112},{112,0},{1... | collective-permute-start | bytes 2752520 | tf_op jit(solution)/shard_map/ppermute | solution.py:69
  227.1 29.1 %collective-permute-start.18 = (bf16[512,896]{1,0:T(8,128)(2,1)}, bf16[512,896]{1,0:T(8,128)(2,1)S(1)}, u32[]{:S(2)}, u32[]{:S(2)}) collective-permute-start(bf16[512,896]{1,0:T(8,128)(2,1)} %collective-permute-done.16), channel_id=1, source_target_pairs={{0,112},{16,0},{32,16},{48,32},{64,48},{80,64},{96,80},{112,96},{1... | collective-permute-start | bytes 2752520 | tf_op jit(solution)/shard_map/ppermute | solution.py:69
  256.3 12.4 %collective-permute-start.19 = (bf16[256,896]{1,0:T(8,128)(2,1)S(1)}, bf16[256,896]{1,0:T(8,128)(2,1)S(1)}, u32[]{:S(2)}, u32[]{:S(2)}) collective-permute-start(bf16[256,896]{1,0:T(8,128)(2,1)S(1)} %slice.101), channel_id=1, source_target_pairs={{0,16},{16,32},{32,48},{48,64},{64,80},{80,96},{96,112},{112,0},{1... | collective-permute-start | bytes 1376264 | tf_op jit(solution)/shard_map/ppermute | solution.py:69
  258.8 10.6 %collective-permute-start.20 = (bf16[256,896]{1,0:T(8,128)(2,1)S(1)}, bf16[256,896]{1,0:T(8,128)(2,1)S(1)}, u32[]{:S(2)}, u32[]{:S(2)}) collective-permute-start(bf16[256,896]{1,0:T(8,128)(2,1)S(1)} %slice.102), channel_id=1, source_target_pairs={{0,112},{16,0},{32,16},{48,32},{64,48},{80,64},{96,80},{112,96},{1... | collective-permute-start | bytes 1376264 | tf_op jit(solution)/shard_map/ppermute | solution.py:69
  273.5 15.2 %collective-permute-start.21 = (f32[376,896]{1,0:T(8,128)S(1)}, f32[376,896]{1,0:T(8,128)S(1)}, u32[]{:S(2)}, u32[]{:S(2)}) collective-permute-start(f32[376,896]{1,0:T(8,128)S(1)} %slice_select_fusion), channel_id=1, source_target_pairs={{0,1},{1,0},{2,3},{3,2},{4,5},{5,4},{6,7},{7,6},{8,9},{9,8},{10,11... | collective-permute-start | bytes 4042760 | tf_op jit(solution)/shard_map/ppermute | solution.py:18
  277.0 18.1 %collective-permute-start.10 = (bf16[256,768]{1,0:T(8,128)(2,1)S(1)}, bf16[256,768]{1,0:T(8,128)(2,1)S(1)}, u32[]{:S(2)}, u32[]{:S(2)}) collective-permute-start(bf16[256,768]{1,0:T(8,128)(2,1)S(1)} %slice.89), channel_id=1, source_target_pairs={{0,16},{16,32},{32,48},{48,64},{64,80},{80,96},{96,112},{112,0},{1... | collective-permute-start | bytes 1179656 | tf_op jit(solution)/shard_map/ppermute | solution.py:69
  279.4 15.8 %collective-permute-start.11 = (bf16[256,768]{1,0:T(8,128)(2,1)S(1)}, bf16[256,768]{1,0:T(8,128)(2,1)S(1)}, u32[]{:S(2)}, u32[]{:S(2)}) collective-permute-start(bf16[256,768]{1,0:T(8,128)(2,1)S(1)} %slice.90), channel_id=1, source_target_pairs={{0,112},{16,0},{32,16},{48,32},{64,48},{80,64},{96,80},{112,96},{1... | collective-permute-start | bytes 1179656 | tf_op jit(solution)/shard_map/ppermute | solution.py:69
  289.2 13.2 %collective-permute-start.22 = (bf16[376,896]{1,0:T(8,128)(2,1)S(1)}, bf16[376,896]{1,0:T(8,128)(2,1)S(1)}, u32[]{:S(2)}, u32[]{:S(2)}) collective-permute-start(bf16[376,896]{1,0:T(8,128)(2,1)S(1)} %multiply_convert_fusion), channel_id=1, source_target_pairs={{0,0},{1,128},{128,129},{129,1},{2,2},{3,130},{130,131},{131,3},{4... | collective-permute-start | bytes 2021384 | tf_op jit(solution)/shard_map/ppermute | solution.py:105
  307.5 12.0 %collective-permute-start.24 = (bf16[376,768]{1,0:T(8,128)(2,1)S(1)}, bf16[376,768]{1,0:T(8,128)(2,1)S(1)}, u32[]{:S(2)}, u32[]{:S(2)}) collective-permute-start(bf16[376,768]{1,0:T(8,128)(2,1)S(1)} %multiply_convert_fusion.1), channel_id=1, source_target_pairs={{0,0},{1,128},{128,129},{129,1},{2,2},{3,130},{130,131},{131,3},{4... | collective-permute-start | bytes 1732616 | tf_op jit(solution)/shard_map/ppermute | solution.py:105
  (11 other events, 217.1 us)

commit v5 on v2

v5 whole, which is shorter than its diff:
```python
import jax
import jax.numpy as jnp
from jax import lax
from jax.experimental import pallas as pl
from jax.experimental.pallas import tpu as pltpu
from jax.sharding import Mesh, PartitionSpec as P

AXES = ("xh", "z", "xl", "y", "core")
SIZES = (2, 8, 2, 4, 2)
WIDTHS = (896, 768)

TURN = [(h * 2 + c, c * 2 + h) for h in range(2) for c in range(2)]
CROSS = [(h * 2 + c, c * 2 + 1 - h) for h in range(2) for c in range(2)]
HOME = [(h * 2 + c, (h ^ c) * 2 + h) for h in range(2) for c in range(2)]


def exchange(value, axis, flip, size):
    return lax.ppermute(value, axis, [(i, i ^ flip) for i in range(size)])


def swap_if(flag, first, second):
    return jnp.where(flag, second, first), jnp.where(flag, first, second)


def together(*values):
    return lax.optimization_barrier(values)


def tokens_of_core(tokens):
    core = lax.axis_index("core")
    half = tokens.shape[1] // 2
    mine, other = swap_if(core == 1, tokens[:, :half], tokens[:, half:])
    received = exchange(other, "core", 1, 2)
    near = swap_if(core == 1, mine, received)
    far = exchange(jnp.concatenate(near, axis=1), "xl", 1, 2)
    return jnp.concatenate([near[0], far[:, :half], near[1], far[:, half:]], axis=1)


def along_y(value, shift):
    return lax.ppermute(value, "y", [(i, (i + shift) % 4) for i in range(4)])


def gather_along_y(both):
    up, down = along_y(both, 1), along_y(both, -1)
    return [both, up, down, along_y(up[0], 1), along_y(down[1], -1)]


def order_blocks(place, here, up, down, far_up, far_down, out):
    width = out.shape[2]
    at = lax.rem(place[0] + 8 - pl.program_id(0), 8)
    columns = pl.ds(pl.multiple_of(lax.rem(at, 2) * width, width), width)
    shift = lax.rem(lax.div(at, 2) + 4 - place[1], 4)
    for s, piece in ((0, here), (3, up), (1, down)):

        @pl.when(shift == s)
        def copy():
            for e in range(2):
                out[e] = piece[e, :, columns]

    @pl.when(shift == 2)
    def copy_far():
        out[0] = far_up[:, columns]
        out[1] = far_down[:, columns]


def order_tokens(pieces):
    two, rows, columns = pieces[0].shape
    place = jnp.stack([lax.axis_index("z"), lax.axis_index("y")])
    ordered = pl.pallas_call(
        order_blocks,
        grid=(8,),
        in_specs=[pl.BlockSpec(memory_space=pltpu.SMEM)]
        + [pl.BlockSpec(piece.shape, lambda r, n=piece.ndim: (0,) * n) for piece in pieces],
        out_specs=pl.BlockSpec((two, rows, columns // 2), lambda r: (0, 0, r)),
        out_shape=jax.ShapeDtypeStruct((two, rows, 4 * columns), pieces[0].dtype),
        compiler_params=pltpu.CompilerParams(vmem_limit_bytes=40 * 2**20),
        cost_estimate=pl.CostEstimate(
            flops=0, transcendentals=0, bytes_accessed=16 * two * rows * columns
        ),
    )(place, *pieces)
    return ordered.reshape(two * rows, 4 * columns)


def along_z(value, shift):
    return lax.ppermute(value, "z", [(i, (i + shift) % 8) for i in range(8)])


def step_along_z(step, up, down):
    if step == 4:
        half = up.shape[0] // 2
        up, down = up[:half], down[half:]
    return along_z(up, 1), along_z(down, -1)


def product(gathered, blocks, half):
    total = 0
    for block, piece in blocks:
        features = gathered[:, block * half : block * half + piece.shape[0]]
        total += jnp.dot(features, piece, preferred_element_type=jnp.float32)
    return total


def swapped(weight, also):
    xh, xl, core = (lax.axis_index(name) for name in ("xh", "xl", "core"))
    half = weight.shape[0] // 2
    first, second = swap_if(xh == 1, weight[:half], weight[half:])
    turned = lax.ppermute(first, ("xh", "core"), TURN)
    crossed = lax.ppermute(second, ("xh", "core"), CROSS)
    also, turned, crossed = together(also, turned, crossed)
    return jnp.concatenate(swap_if(xl != core, turned, crossed)), also


def activate(total):
    rows = total.shape[0] // 2
    core = lax.axis_index("core")
    kept, given = swap_if(core == 1, total[:rows], total[rows:])
    total = kept + exchange(given, "core", 1, 2)
    return jax.nn.silu(total).astype(jnp.bfloat16)


def home(out):
    return lax.ppermute(out, ("xh", "core"), HOME)


def on_device(tokens, weight):
    half = weight.shape[0] // 2
    piece = tokens_of_core(tokens)
    beside = exchange(piece, "xh", 1, 2)
    mine, piece = swapped(weight, piece)
    both = jnp.stack([piece, beside])
    pieces = gather_along_y(both)
    up = down = mine
    blocks = [(0, mine)]
    for step in range(1, 4):
        up, down = together(*step_along_z(step, up, down))
        blocks += [(2 * step, up), (2 * (8 - step), down)]
    gathered = order_tokens(pieces)
    early = product(gathered, blocks[:5], half)
    early, up, down = together(early, up, down)
    early += product(gathered, [(6, up), (10, down)], half)
    up, down, early = together(*step_along_z(4, up, down), early)
    cut = WIDTHS[0]
    outs = []
    for columns in (slice(0, cut), slice(cut, None)):
        last = product(gathered, ((8, up[:, columns]), (9, down[:, columns])), half)
        outs.append(home(activate(early[:, columns] + last)))
    return jnp.concatenate(outs, axis=1)


def solution(mesh):
    fine = Mesh(mesh.devices.reshape(SIZES), AXES)
    placed = P(("xh", "z"), ("xl", "y", "core"))
    return jax.shard_map(
        on_device, mesh=fine, in_specs=(placed, placed), out_specs=placed, check_vma=False
    )
```

time: 220 us -> 218 us (level)
  starting transfers between devices: 47.1 us -> 37.4 us
  waiting for transfers between devices: 129 us -> 136 us
  Pallas kernels: 0 us -> 2.63 us
  local copies, waits for them, and re-layouts: 8.11 us -> 5.66 us
    ppermute x2 -> x6, waiting for transfers between devices: 14.9 us -> 40.6 us  [the longest x4 25.6 us: along_y(): return lax.ppermute(value, 'y', [(i, (i + shift) % 4) for i in range(4)])]
    ppermute x2 -> x1, waiting for transfers between devices: 18.2 us -> 0.01 us  [swapped(): turned = lax.ppermute(first, ('xh', 'core'), TURN)]
    ppermute x16 -> x8, waiting for transfers between devices: 41.3 us -> 52.9 us  [along_z(): return lax.ppermute(value, 'z', [(i, (i + shift) % 8) for i in range(8)])]
    ppermute x8 -> x5, waiting for transfers between devices: 49.6 us -> 42.1 us  [exchange(): return lax.ppermute(value, axis, [(i, i ^ flip) for i in range(size)])]
    ppermute x2 -> x1, starting transfers between devices: 9.07 us -> 2.82 us  [swapped(): turned = lax.ppermute(first, ('xh', 'core'), TURN)]
    ppermute x2 -> x6, starting transfers between devices: 3.84 us -> 9.42 us  [the longest x4 5.58 us: along_y(): return lax.ppermute(value, 'y', [(i, (i + shift) % 4) for i in range(4)])]
    ppermute x2 -> x1, waiting for transfers between devices: 5.28 us -> 0.01 us  [swapped(): crossed = lax.ppermute(second, ('xh', 'core'), CROSS)]
    dynamic_update_slice x8 -> x0, local copies, waits for them, and re-layouts: 5.24 us -> none  [gather_tokens(): lax.dynamic_update_slice(out, arrived[:, c * features:(c + 1) * features]...]
  transfers between devices with their start and end apart: 30 -> 21, of which waited for: 15 -> 11; matrix products, arithmetic and copies ran while one was open for 16% -> 14% of each run, Pallas kernels for 0% -> 1%
where the time goes in v5:
time: 218 us; the launch traced here: 214 us
  waiting for transfers between devices  136 us (62%)
  starting transfers between devices  37.4 us (17%)
  matrix products  25.6 us (12%)
  other arithmetic  7.16 us (3%)
  local copies, waits for them, and re-layouts  5.66 us (3%)
  Pallas kernels  2.63 us (1%)
    ppermute x8, waiting for transfers between devices, along_z(): return lax.ppermute(value, 'z', [(i, (i + shift) % 8) for i in range(8)])  52.9 us
    ppermute x5, waiting for transfers between devices, exchange(): return lax.ppermute(value, axis, [(i, i ^ flip) for i in range(size)])  42.1 us
    ppermute x4, waiting for transfers between devices, along_y(): return lax.ppermute(value, 'y', [(i, (i + shift) % 4) for i in range(4)])  25.6 us
    dot_general x11, matrix products, product(): total += jnp.dot(features, piece, preferred_element_type=jnp.float32)  25.6 us
    ppermute x8, starting transfers between devices, along_z(): return lax.ppermute(value, 'z', [(i, (i + shift) % 8) for i in range(8)])  17 us
    ppermute x2, waiting for transfers between devices, home(): return lax.ppermute(out, ('xh', 'core'), HOME)  15 us
    ppermute x5, starting transfers between devices, exchange(): return lax.ppermute(value, axis, [(i, i ^ flip) for i in range(size)])  8.09 us
    ppermute x4, starting transfers between devices, along_y(): return lax.ppermute(value, 'y', [(i, (i + shift) % 4) for i in range(4)])  5.58 us
  transfers between devices with their start and end apart: 21, of which 11 were waited for; matrix products, arithmetic and copies ran while one was open for 14% of the time, Pallas kernels for 1%

profile of v5, /device:TPU:1, one launch (start us, length us, event | category | flops | bytes accessed | tf_op | source)
XLA Modules:
  0.0 214.5 jit_solution(16132832134446478717)
XLA Ops:
  1.0 3.3 %collective-permute-start = (bf16[376,256]{1,0:T(8,128)(2,1)S(1)}, bf16[376,256]{1,0:T(8,128)(2,1)S(1)}, u32[]{:S(2)}, u32[]{:S(2)}) collective-permute-start(bf16[376,256]{1,0:T(8,128)(2,1)S(1)} %broadcast_select_fusion.7), channel_id=1, source_target_pairs={{0,1},{1,0},{2,3},{3,2},{4,5},{5,4},{6,7},{7,6},{8,9},{9,8},{10,11... | collective-permute-start | bytes 577544 | tf_op jit(solution)/shard_map/ppermute | solution.py:18
  4.4 2.5 %broadcast_select_fusion.2 = (bf16[256,1664]{1,0:T(8,128)(2,1)S(1)}, bf16[256,1664]{1,0:T(8,128)(2,1)}) fusion(pred[]{:T(512)S(6)} %eq.10, bf16[512,1664]{1,0:T(8,128)(2,1)} %param.3), kind=kLoop, calls=%fused_computation.13 | loop fusion | flops 851968 | bytes 3407873 | tf_op jit(solution)/shard_map/jit(_where)/select_n | solution.py:22
  6.9 2.8 %collective-permute-start.2 = (bf16[256,1664]{1,0:T(8,128)(2,1)}, bf16[256,1664]{1,0:T(8,128)(2,1)S(1)}, u32[]{:S(2)}, u32[]{:S(2)}) collective-permute-start(bf16[256,1664]{1,0:T(8,128)(2,1)} %get-tuple-element.38), channel_id=1, source_target_pairs={{0,0},{1,128},{128,1},{129,129},{2,2},{3,130},{130,3},{131,131},{4... | collective-permute-start | bytes 2555912 | tf_op jit(solution)/shard_map/ppermute | solution.py:107
  11.0 26.7 %collective-permute-done.1 = bf16[376,512]{1,0:T(8,128)(2,1)S(1)} collective-permute-done((bf16[376,512]{1,0:T(8,128)(2,1)}, bf16[376,512]{1,0:T(8,128)(2,1)S(1)}, u32[]{:S(2)}, u32[]{:S(2)}) %collective-permute-start.1) | collective-permute-done | bytes 385056 | tf_op jit(solution)/shard_map/ppermute | solution.py:18
  39.3 5.6 %collective-permute-start.10 = (bf16[512,1664]{1,0:T(8,128)(2,1)S(1)}, bf16[512,1664]{1,0:T(8,128)(2,1)}, u32[]{:S(2)}, u32[]{:S(2)}) collective-permute-start(bf16[512,1664]{1,0:T(8,128)(2,1)S(1)} %pad_maximum_fusion), channel_id=1, source_target_pairs={{0,112},{16,0},{32,16},{48,32},{64,48},{80,64},{96,80},{112,96},{1... | collective-permute-start | bytes 5111816 | tf_op jit(solution)/shard_map/ppermute | solution.py:85
  44.9 13.4 %collective-permute-done.4 = bf16[376,1024]{1,0:T(8,128)(2,1)S(1)} collective-permute-done((bf16[376,1024]{1,0:T(8,128)(2,1)S(1)}, bf16[376,1024]{1,0:T(8,128)(2,1)S(1)}, u32[]{:S(2)}, u32[]{:S(2)}) %collective-permute-start.4) | collective-permute-done | bytes 770080 | tf_op jit(solution)/shard_map/ppermute | solution.py:18
  61.4 16.7 %collective-permute-done.10 = bf16[512,1664]{1,0:T(8,128)(2,1)} collective-permute-done((bf16[512,1664]{1,0:T(8,128)(2,1)S(1)}, bf16[512,1664]{1,0:T(8,128)(2,1)}, u32[]{:S(2)}, u32[]{:S(2)}) %collective-permute-start.10) | collective-permute-done | bytes 1703968 | tf_op jit(solution)/shard_map/ppermute | solution.py:85
  78.0 3.2 %collective-permute-done.9 = bf16[512,1664]{1,0:T(8,128)(2,1)} collective-permute-done((bf16[512,1664]{1,0:T(8,128)(2,1)S(1)}, bf16[512,1664]{1,0:T(8,128)(2,1)}, u32[]{:S(2)}, u32[]{:S(2)}) %collective-permute-start.9) | collective-permute-done | bytes 1703968 | tf_op jit(solution)/shard_map/ppermute | solution.py:85
  81.3 2.7 %collective-permute-start.12 = (bf16[512,1664]{1,0:T(8,128)(2,1)}, bf16[512,1664]{1,0:T(8,128)(2,1)}, u32[]{:S(2)}, u32[]{:S(2)}) collective-permute-start(bf16[512,1664]{1,0:T(8,128)(2,1)} %collective-permute-done.10), channel_id=1, source_target_pairs={{0,112},{16,0},{32,16},{48,32},{64,48},{80,64},{96,80},{112,96},{1... | collective-permute-start | bytes 5111816 | tf_op jit(solution)/shard_map/ppermute | solution.py:85
  83.9 10.6 %collective-permute-done.5.up = bf16[2,376,1024]{2,1,0:T(8,128)(2,1)S(1)} collective-permute-done((bf16[2,376,1024]{2,1,0:T(8,128)(2,1)S(1)}, bf16[2,376,1024]{2,1,0:T(8,128)(2,1)S(1)}, u32[]{:S(2)}, u32[]{:S(2)}) %collective-permute-start.5) | collective-permute-done | bytes 1540128 | tf_op jit(solution)/shard_map/ppermute | solution.py:40
  97.6 2.7 %collective-permute-start.8 = (bf16[376,1024]{1,0:T(8,128)(2,1)}, bf16[376,1024]{1,0:T(8,128)(2,1)}, u32[]{:S(2)}, u32[]{:S(2)}) collective-permute-start(bf16[376,1024]{1,0:T(8,128)(2,1)} %slice_bitcast_fusion), channel_id=1, source_target_pairs={{0,6},{2,0},{4,2},{6,4},{1,7},{3,1},{5,3},{7,5},{8,14},{10,8},{12,... | collective-permute-start | bytes 2310152 | tf_op jit(solution)/shard_map/ppermute | solution.py:40
  100.3 14.0 %collective-permute-done.7.far_up = bf16[376,1024]{1,0:T(8,128)(2,1)} collective-permute-done((bf16[376,1024]{1,0:T(8,128)(2,1)}, bf16[376,1024]{1,0:T(8,128)(2,1)}, u32[]{:S(2)}, u32[]{:S(2)}) %collective-permute-start.7) | collective-permute-done | bytes 770080 | tf_op jit(solution)/shard_map/ppermute | solution.py:40
  116.8 2.6 %shard_map.28 = bf16[2,376,4096]{2,1,0:T(8,128)(2,1)S(1)} custom-call(s32[2]{0:T(128)S(1)} %pad_add_fusion.place, bf16[2,376,1024]{2,1,0:T(8,128)(2,1)S(1)} %pad_maximum_fusion.1.here, bf16[2,376,1024]{2,1,0:T(8,128)(2,1)S(1)} %collective-permute-done.5.up, bf16[2,376,1024]{2,1,0:T(8,128)(2,1)S(1)} %copy-done.1, ...), custom_call_target="tpu_custom_call" | custom-call | bytes 12320768 | tf_op jit(solution)/shard_map/pallas_call | solution.py:69
  119.4 3.0 %fusion.11 = f32[752,1664]{1,0:T(8,128)S(1)} fusion(bf16[512,1664]{1,0:T(8,128)(2,1)} %collective-permute-done.9, bf16[752,4096]{1,0:T(8,128)(2,1)S(1)} %bitcast.15), kind=kOutput, calls=%fused_computation.24 | convolution fusion | flops 1281359872 | bytes 7479296 | tf_op jit(solution)/shard_map/dot_general | solution.py:99
  122.4 3.1 %fusion.9 = f32[752,1664]{1,0:T(8,128)S(1)} fusion(bf16[512,1664]{1,0:T(8,128)(2,1)} %collective-permute-done.10, bf16[752,4096]{1,0:T(8,128)(2,1)S(1)} %bitcast.16), kind=kOutput, calls=%fused_computation.22 | convolution fusion | flops 1281359872 | bytes 7479296 | tf_op jit(solution)/shard_map/dot_general | solution.py:99
  127.1 4.2 %collective-permute-start.14 = (bf16[512,1664]{1,0:T(8,128)(2,1)}, bf16[512,1664]{1,0:T(8,128)(2,1)S(1)}, u32[]{:S(2)}, u32[]{:S(2)}) collective-permute-start(bf16[512,1664]{1,0:T(8,128)(2,1)} %collective-permute-done.12), channel_id=1, source_target_pairs={{0,112},{16,0},{32,16},{48,32},{64,48},{80,64},{96,80},{112,96},{1... | collective-permute-start | bytes 5111816 | tf_op jit(solution)/shard_map/ppermute | solution.py:85
  132.9 5.3 %fusion.7 = f32[752,1664]{1,0:T(8,128)} fusion(bf16[512,1664]{1,0:T(8,128)(2,1)} %collective-permute-done.11, bf16[752,4096]{1,0:T(8,128)(2,1)S(1)} %bitcast.18), kind=kOutput, calls=%fused_computation.20 | convolution fusion | flops 1281359872 | bytes 7479296 | tf_op jit(solution)/shard_map/dot_general | solution.py:99
  138.2 7.2 %add_add_fusion.1 = f32[752,1664]{1,0:T(8,128)} fusion(f32[752,1664]{1,0:T(8,128)} %fusion.7, f32[752,1664]{1,0:T(8,128)S(1)} %fusion.9, f32[752,1664]{1,0:T(8,128)S(1)} %fusion.13, f32[752,1664]{1,0:T(8,128)S(1)} %fusion.11, bf16[512,1664]{1,0:T(8,128)(2,1)} %collective-permute-done.12, bf16[752,4096]{1,0:T(8,128)(2,1)S(1)} %bitcast.19), kind=kOutput, calls=%fused_computation.1 | convolution fusion | flops 1286365184 | bytes 27500544 | tf_op jit(solution)/shard_map/dot_general | solution.py:99
  145.4 21.0 %collective-permute-done.13 = bf16[512,1664]{1,0:T(8,128)(2,1)S(1)} collective-permute-done((bf16[512,1664]{1,0:T(8,128)(2,1)}, bf16[512,1664]{1,0:T(8,128)(2,1)S(1)}, u32[]{:S(2)}, u32[]{:S(2)}) %collective-permute-start.13) | collective-permute-done | bytes 1703968 | tf_op jit(solution)/shard_map/ppermute | solution.py:85
  166.6 2.9 %collective-permute-start.16 = (bf16[256,1664]{1,0:T(8,128)(2,1)S(1)}, bf16[256,1664]{1,0:T(8,128)(2,1)S(1)}, u32[]{:S(2)}, u32[]{:S(2)}) collective-permute-start(bf16[256,1664]{1,0:T(8,128)(2,1)S(1)} %slice.103), channel_id=1, source_target_pairs={{0,112},{16,0},{32,16},{48,32},{64,48},{80,64},{96,80},{112,96},{1... | collective-permute-start | bytes 2555912 | tf_op jit(solution)/shard_map/ppermute | solution.py:85
  172.9 12.0 %collective-permute-done.15 = bf16[256,1664]{1,0:T(8,128)(2,1)S(1)} collective-permute-done((bf16[256,1664]{1,0:T(8,128)(2,1)S(1)}, bf16[256,1664]{1,0:T(8,128)(2,1)S(1)}, u32[]{:S(2)}, u32[]{:S(2)}) %collective-permute-start.15) | collective-permute-done | bytes 852000 | tf_op jit(solution)/shard_map/ppermute | solution.py:85
  186.7 4.3 %collective-permute-start.17 = (f32[376,896]{1,0:T(8,128)S(1)}, f32[376,896]{1,0:T(8,128)S(1)}, u32[]{:S(2)}, u32[]{:S(2)}) collective-permute-start(f32[376,896]{1,0:T(8,128)S(1)} %slice_select_fusion), channel_id=1, source_target_pairs={{0,1},{1,0},{2,3},{3,2},{4,5},{5,4},{6,7},{7,6},{8,9},{9,8},{10,11... | collective-permute-start | bytes 4042760 | tf_op jit(solution)/shard_map/ppermute | solution.py:18
  191.7 2.0 collective-permute-done.17
  198.3 15.0 %collective-permute-done.20 = bf16[376,768]{1,0:T(8,128)(2,1)S(1)} collective-permute-done((bf16[376,768]{1,0:T(8,128)(2,1)S(1)}, bf16[376,768]{1,0:T(8,128)(2,1)S(1)}, u32[]{:S(2)}, u32[]{:S(2)}) %collective-permute-start.20) | collective-permute-done | bytes 577568 | tf_op jit(solution)/shard_map/ppermute | solution.py:122
  (68 shorter events, 27.3 us)
Async XLA Ops:
  1.0 8.8 %collective-permute-start = (bf16[376,256]{1,0:T(8,128)(2,1)S(1)}, bf16[376,256]{1,0:T(8,128)(2,1)S(1)}, u32[]{:S(2)}, u32[]{:S(2)}) collective-permute-start(bf16[376,256]{1,0:T(8,128)(2,1)S(1)} %broadcast_select_fusion.7), channel_id=1, source_target_pairs={{0,1},{1,0},{2,3},{3,2},{4,5},{5,4},{6,7},{7,6},{8,9},{9,8},{10,11... | collective-permute-start | bytes 577544 | tf_op jit(solution)/shard_map/ppermute | solution.py:18
  4.4 5.5 %copy-start.6 = (bf16[376,512]{1,0:T(8,128)(2,1)S(1)}, bf16[376,512]{1,0:T(8,128)(2,1)}, u32[]{:S(2)}) copy-start(bf16[376,512]{1,0:T(8,128)(2,1)} %param.2) | copy-start | bytes 1155076
  6.9 31.0 %collective-permute-start.2 = (bf16[256,1664]{1,0:T(8,128)(2,1)}, bf16[256,1664]{1,0:T(8,128)(2,1)S(1)}, u32[]{:S(2)}, u32[]{:S(2)}) collective-permute-start(bf16[256,1664]{1,0:T(8,128)(2,1)} %get-tuple-element.38), channel_id=1, source_target_pairs={{0,0},{1,128},{128,1},{129,129},{2,2},{3,130},{130,3},{131,131},{4... | collective-permute-start | bytes 2555912 | tf_op jit(solution)/shard_map/ppermute | solution.py:107
  9.7 28.2 %collective-permute-start.3 = (bf16[256,1664]{1,0:T(8,128)(2,1)S(1)}, bf16[256,1664]{1,0:T(8,128)(2,1)S(1)}, u32[]{:S(2)}, u32[]{:S(2)}) collective-permute-start(bf16[256,1664]{1,0:T(8,128)(2,1)S(1)} %get-tuple-element.37), channel_id=1, source_target_pairs={{0,1},{1,129},{128,0},{129,128},{2,3},{3,131},{130,2},{131,130},{4... | collective-permute-start | bytes 2555912 | tf_op jit(solution)/shard_map/ppermute | solution.py:108
  10.7 27.0 %collective-permute-start.1 = (bf16[376,512]{1,0:T(8,128)(2,1)}, bf16[376,512]{1,0:T(8,128)(2,1)S(1)}, u32[]{:S(2)}, u32[]{:S(2)}) collective-permute-start(bf16[376,512]{1,0:T(8,128)(2,1)} %pad_maximum_fusion.4), channel_id=1, source_target_pairs={{0,8},{8,0},{1,9},{9,1},{2,10},{10,2},{3,11},{11,3},{4,12},{12,4},... | collective-permute-start | bytes 1155080 | tf_op jit(solution)/shard_map/ppermute | solution.py:18
  37.8 20.5 %collective-permute-start.4 = (bf16[376,1024]{1,0:T(8,128)(2,1)S(1)}, bf16[376,1024]{1,0:T(8,128)(2,1)S(1)}, u32[]{:S(2)}, u32[]{:S(2)}) collective-permute-start(bf16[376,1024]{1,0:T(8,128)(2,1)S(1)} %pad_maximum_fusion.3), channel_id=1, source_target_pairs={{0,128},{128,0},{1,129},{129,1},{2,130},{130,2},{3,131},{131,3},{4... | collective-permute-start | bytes 2310152 | tf_op jit(solution)/shard_map/ppermute | solution.py:18
  39.3 38.7 %collective-permute-start.10 = (bf16[512,1664]{1,0:T(8,128)(2,1)S(1)}, bf16[512,1664]{1,0:T(8,128)(2,1)}, u32[]{:S(2)}, u32[]{:S(2)}) collective-permute-start(bf16[512,1664]{1,0:T(8,128)(2,1)S(1)} %pad_maximum_fusion), channel_id=1, source_target_pairs={{0,112},{16,0},{32,16},{48,32},{64,48},{80,64},{96,80},{112,96},{1... | collective-permute-start | bytes 5111816 | tf_op jit(solution)/shard_map/ppermute | solution.py:85
  44.8 36.4 %collective-permute-start.9 = (bf16[512,1664]{1,0:T(8,128)(2,1)S(1)}, bf16[512,1664]{1,0:T(8,128)(2,1)}, u32[]{:S(2)}, u32[]{:S(2)}) collective-permute-start(bf16[512,1664]{1,0:T(8,128)(2,1)S(1)} %pad_maximum_fusion), channel_id=1, source_target_pairs={{0,16},{16,32},{32,48},{48,64},{64,80},{80,96},{96,112},{112,0},{1... | collective-permute-start | bytes 5111816 | tf_op jit(solution)/shard_map/ppermute | solution.py:85
  58.4 36.1 %collective-permute-start.5 = (bf16[2,376,1024]{2,1,0:T(8,128)(2,1)S(1)}, bf16[2,376,1024]{2,1,0:T(8,128)(2,1)S(1)}, u32[]{:S(2)}, u32[]{:S(2)}) collective-permute-start(bf16[2,376,1024]{2,1,0:T(8,128)(2,1)S(1)} %pad_maximum_fusion.1.here), channel_id=1, source_target_pairs={{0,2},{2,4},{4,6},{6,0},{1,3},{3,5},{5,7},{7,1},{8,10},{10,12},{12... | collective-permute-start | bytes 4620296 | tf_op jit(solution)/shard_map/ppermute | solution.py:40
  59.8 35.7 %collective-permute-start.6 = (bf16[2,376,1024]{2,1,0:T(8,128)(2,1)S(1)}, bf16[2,376,1024]{2,1,0:T(8,128)(2,1)S(1)}, u32[]{:S(2)}, u32[]{:S(2)}) collective-permute-start(bf16[2,376,1024]{2,1,0:T(8,128)(2,1)S(1)} %pad_maximum_fusion.1.here), channel_id=1, source_target_pairs={{0,6},{2,0},{4,2},{6,4},{1,7},{3,1},{5,3},{7,5},{8,14},{10,8},{12,... | collective-permute-start | bytes 4620296 | tf_op jit(solution)/shard_map/ppermute | solution.py:40
  81.3 44.3 %collective-permute-start.11 = (bf16[512,1664]{1,0:T(8,128)(2,1)}, bf16[512,1664]{1,0:T(8,128)(2,1)}, u32[]{:S(2)}, u32[]{:S(2)}) collective-permute-start(bf16[512,1664]{1,0:T(8,128)(2,1)} %collective-permute-done.9), channel_id=1, source_target_pairs={{0,16},{16,32},{32,48},{48,64},{64,80},{80,96},{96,112},{112,0},{1... | collective-permute-start | bytes 5111816 | tf_op jit(solution)/shard_map/ppermute | solution.py:85
  81.3 44.3 %collective-permute-start.12 = (bf16[512,1664]{1,0:T(8,128)(2,1)}, bf16[512,1664]{1,0:T(8,128)(2,1)}, u32[]{:S(2)}, u32[]{:S(2)}) collective-permute-start(bf16[512,1664]{1,0:T(8,128)(2,1)} %collective-permute-done.10), channel_id=1, source_target_pairs={{0,112},{16,0},{32,16},{48,32},{64,48},{80,64},{96,80},{112,96},{1... | collective-permute-start | bytes 5111816 | tf_op jit(solution)/shard_map/ppermute | solution.py:85
  95.5 18.8 %collective-permute-start.7 = (bf16[376,1024]{1,0:T(8,128)(2,1)}, bf16[376,1024]{1,0:T(8,128)(2,1)}, u32[]{:S(2)}, u32[]{:S(2)}) collective-permute-start(bf16[376,1024]{1,0:T(8,128)(2,1)} %slice_bitcast_fusion.1), channel_id=1, source_target_pairs={{0,2},{2,4},{4,6},{6,0},{1,3},{3,5},{5,7},{7,1},{8,10},{10,12},{12... | collective-permute-start | bytes 2310152 | tf_op jit(solution)/shard_map/ppermute | solution.py:40
  97.6 17.8 %collective-permute-start.8 = (bf16[376,1024]{1,0:T(8,128)(2,1)}, bf16[376,1024]{1,0:T(8,128)(2,1)}, u32[]{:S(2)}, u32[]{:S(2)}) collective-permute-start(bf16[376,1024]{1,0:T(8,128)(2,1)} %slice_bitcast_fusion), channel_id=1, source_target_pairs={{0,6},{2,0},{4,2},{6,4},{1,7},{3,1},{5,3},{7,5},{8,14},{10,8},{12,... | collective-permute-start | bytes 2310152 | tf_op jit(solution)/shard_map/ppermute | solution.py:40
  122.4 8.9 %copy-start.3 = (bf16[256,1664]{1,0:T(8,128)(2,1)S(1)}, bf16[256,1664]{1,0:T(8,128)(2,1)}, u32[]{:S(2)}) copy-start(bf16[256,1664]{1,0:T(8,128)(2,1)} %copy-done.2) | copy-start | bytes 2555908
  122.4 8.9 %copy-start.5 = (bf16[256,1664]{1,0:T(8,128)(2,1)S(1)}, bf16[256,1664]{1,0:T(8,128)(2,1)}, u32[]{:S(2)}) copy-start(bf16[256,1664]{1,0:T(8,128)(2,1)} %copy-done.4) | copy-start | bytes 2555908
  125.6 40.8 %collective-permute-start.13 = (bf16[512,1664]{1,0:T(8,128)(2,1)}, bf16[512,1664]{1,0:T(8,128)(2,1)S(1)}, u32[]{:S(2)}, u32[]{:S(2)}) collective-permute-start(bf16[512,1664]{1,0:T(8,128)(2,1)} %collective-permute-done.11), channel_id=1, source_target_pairs={{0,16},{16,32},{32,48},{48,64},{64,80},{80,96},{96,112},{112,0},{1... | collective-permute-start | bytes 5111816 | tf_op jit(solution)/shard_map/ppermute | solution.py:85
  127.1 39.3 %collective-permute-start.14 = (bf16[512,1664]{1,0:T(8,128)(2,1)}, bf16[512,1664]{1,0:T(8,128)(2,1)S(1)}, u32[]{:S(2)}, u32[]{:S(2)}) collective-permute-start(bf16[512,1664]{1,0:T(8,128)(2,1)} %collective-permute-done.12), channel_id=1, source_target_pairs={{0,112},{16,0},{32,16},{48,32},{64,48},{80,64},{96,80},{112,96},{1... | collective-permute-start | bytes 5111816 | tf_op jit(solution)/shard_map/ppermute | solution.py:85
  166.4 18.5 %collective-permute-start.15 = (bf16[256,1664]{1,0:T(8,128)(2,1)S(1)}, bf16[256,1664]{1,0:T(8,128)(2,1)S(1)}, u32[]{:S(2)}, u32[]{:S(2)}) collective-permute-start(bf16[256,1664]{1,0:T(8,128)(2,1)S(1)} %slice.102), channel_id=1, source_target_pairs={{0,16},{16,32},{32,48},{48,64},{64,80},{80,96},{96,112},{112,0},{1... | collective-permute-start | bytes 2555912 | tf_op jit(solution)/shard_map/ppermute | solution.py:85
  166.6 18.3 %collective-permute-start.16 = (bf16[256,1664]{1,0:T(8,128)(2,1)S(1)}, bf16[256,1664]{1,0:T(8,128)(2,1)S(1)}, u32[]{:S(2)}, u32[]{:S(2)}) collective-permute-start(bf16[256,1664]{1,0:T(8,128)(2,1)S(1)} %slice.103), channel_id=1, source_target_pairs={{0,112},{16,0},{32,16},{48,32},{64,48},{80,64},{96,80},{112,96},{1... | collective-permute-start | bytes 2555912 | tf_op jit(solution)/shard_map/ppermute | solution.py:85
  186.7 7.0 %collective-permute-start.17 = (f32[376,896]{1,0:T(8,128)S(1)}, f32[376,896]{1,0:T(8,128)S(1)}, u32[]{:S(2)}, u32[]{:S(2)}) collective-permute-start(f32[376,896]{1,0:T(8,128)S(1)} %slice_select_fusion), channel_id=1, source_target_pairs={{0,1},{1,0},{2,3},{3,2},{4,5},{5,4},{6,7},{7,6},{8,9},{9,8},{10,11... | collective-permute-start | bytes 4042760 | tf_op jit(solution)/shard_map/ppermute | solution.py:18
  191.6 4.4 %collective-permute-start.19 = (f32[376,768]{1,0:T(8,128)S(1)}, f32[376,768]{1,0:T(8,128)S(1)}, u32[]{:S(2)}, u32[]{:S(2)}) collective-permute-start(f32[376,768]{1,0:T(8,128)S(1)} %slice_select_fusion.1), channel_id=1, source_target_pairs={{0,1},{1,0},{2,3},{3,2},{4,5},{5,4},{6,7},{7,6},{8,9},{9,8},{10,11... | collective-permute-start | bytes 3465224 | tf_op jit(solution)/shard_map/ppermute | solution.py:18
  194.1 19.2 %collective-permute-start.18 = (bf16[376,896]{1,0:T(8,128)(2,1)S(1)}, bf16[376,896]{1,0:T(8,128)(2,1)S(1)}, u32[]{:S(2)}, u32[]{:S(2)}) collective-permute-start(bf16[376,896]{1,0:T(8,128)(2,1)S(1)} %multiply_convert_fusion), channel_id=1, source_target_pairs={{0,0},{1,128},{128,129},{129,1},{2,2},{3,130},{130,131},{131,3},{4... | collective-permute-start | bytes 2021384 | tf_op jit(solution)/shard_map/ppermute | solution.py:122
  196.4 16.9 %collective-permute-start.20 = (bf16[376,768]{1,0:T(8,128)(2,1)S(1)}, bf16[376,768]{1,0:T(8,128)(2,1)S(1)}, u32[]{:S(2)}, u32[]{:S(2)}) collective-permute-start(bf16[376,768]{1,0:T(8,128)(2,1)S(1)} %multiply_convert_fusion.1), channel_id=1, source_target_pairs={{0,0},{1,128},{128,129},{129,1},{2,2},{3,130},{130,131},{131,3},{4... | collective-permute-start | bytes 1732616 | tf_op jit(solution)/shard_map/ppermute | solution.py:122
  (6 other events, 13.8 us)

commit v6 on v5

--- a/solution.py
+++ b/solution.py
@@ -100,14 +100,14 @@
     return total
 
 
-def swapped(weight, also):
+def swapped(weight, *also):
     xh, xl, core = (lax.axis_index(name) for name in ("xh", "xl", "core"))
     half = weight.shape[0] // 2
     first, second = swap_if(xh == 1, weight[:half], weight[half:])
     turned = lax.ppermute(first, ("xh", "core"), TURN)
     crossed = lax.ppermute(second, ("xh", "core"), CROSS)
-    also, turned, crossed = together(also, turned, crossed)
-    return jnp.concatenate(swap_if(xl != core, turned, crossed)), also
+    *also, turned, crossed = together(*also, turned, crossed)
+    return jnp.concatenate(swap_if(xl != core, turned, crossed)), *also
 
 
 def activate(total):
@@ -124,22 +124,30 @@
 
 def on_device(tokens, weight):
     half = weight.shape[0] // 2
+    cut = WIDTHS[0]
     piece = tokens_of_core(tokens)
     beside = exchange(piece, "xh", 1, 2)
-    mine, piece = swapped(weight, piece)
+    mine, piece = swapped(weight[:, :cut], piece)
+    rest, mine = together(weight[:, cut:], mine)
+    up, down = together(*step_along_z(1, mine, mine))
+    (rest,) = swapped(rest)
+    rest_up, rest_down = together(*step_along_z(1, rest, rest))
     both = jnp.stack([piece, beside])
     pieces = gather_along_y(both)
-    up = down = mine
-    blocks = [(0, mine)]
-    for step in range(1, 4):
+    mine = jnp.concatenate([mine, rest], axis=1)
+    up = jnp.concatenate([up, rest_up], axis=1)
+    down = jnp.concatenate([down, rest_down], axis=1)
+    blocks = [(0, mine), (2, up), (14, down)]
+    for step in range(2, 4):
         up, down = together(*step_along_z(step, up, down))
-        blocks += [(2 * step, up), (2 * (8 - step), down)]
+        if step == 2:
+            tied_up, tied_down, *pieces = together(up, down, *pieces)
+            blocks += [(2 * step, tied_up), (2 * (8 - step), tied_down)]
     gathered = order_tokens(pieces)
     early = product(gathered, blocks[:5], half)
     early, up, down = together(early, up, down)
     early += product(gathered, [(6, up), (10, down)], half)
     up, down, early = together(*step_along_z(4, up, down), early)
-    cut = WIDTHS[0]
     outs = []
     for columns in (slice(0, cut), slice(cut, None)):
         last = product(gathered, ((8, up[:, columns]), (9, down[:, columns])), half)

time: 218 us -> 214 us (0.982); the launches traced: 214 us -> 213 us
  waiting for transfers between devices: 136 us -> 109 us
  starting transfers between devices: 37.4 us -> 53.1 us
  local copies, waits for them, and re-layouts: 5.66 us -> 12.1 us
  matrix products: 25.6 us -> 28.5 us
    ppermute x5, waiting for transfers between devices: 42.1 us -> 8.2 us  [exchange(): return lax.ppermute(value, axis, [(i, i ^ flip) for i in range(size)])]
    ppermute x4, waiting for transfers between devices: 25.6 us -> 10.7 us  [along_y(): return lax.ppermute(value, 'y', [(i, (i + shift) % 4) for i in range(4)])]
    ppermute x1 -> x2, waiting for transfers between devices: 0.01 us -> 8.71 us  [swapped(): turned = lax.ppermute(first, ('xh', 'core'), TURN)]
    ppermute x1 -> x2, waiting for transfers between devices: 0.01 us -> 7.7 us  [swapped(): crossed = lax.ppermute(second, ('xh', 'core'), CROSS)]
    ppermute x1 -> x2, starting transfers between devices: 2.82 us -> 10.1 us  [swapped(): turned = lax.ppermute(first, ('xh', 'core'), TURN)]
    ppermute x8 -> x10, waiting for transfers between devices: 52.9 us -> 58.5 us  [along_z(): return lax.ppermute(value, 'z', [(i, (i + shift) % 8) for i in range(8)])]
    ppermute x8 -> x10, starting transfers between devices: 17 us -> 21.5 us  [along_z(): return lax.ppermute(value, 'z', [(i, (i + shift) % 8) for i in range(8)])]
    dot_general x11, matrix products: 25.6 us -> 28.5 us  [product(): total += jnp.dot(features, piece, preferred_element_type=jnp.float32)]
  transfers between devices with their start and end apart: 21 -> 25, of which waited for: 11 -> 16; matrix products, arithmetic and copies ran while one was open for 14% -> 18% of each run, Pallas kernels for 1% -> 1%
where the time goes in v6:
time: 214 us; the launch traced here: 213 us
  waiting for transfers between devices  109 us (51%)
  starting transfers between devices  53.1 us (25%)
  matrix products  28.5 us (13%)
  local copies, waits for them, and re-layouts  12.1 us (6%)
  other arithmetic  7.71 us (4%)
  Pallas kernels  2.63 us (1%)
    ppermute x10, waiting for transfers between devices, along_z(): return lax.ppermute(value, 'z', [(i, (i + shift) % 8) for i in range(8)])  58.5 us
    dot_general x11, matrix products, product(): total += jnp.dot(features, piece, preferred_element_type=jnp.float32)  28.5 us
    ppermute x10, starting transfers between devices, along_z(): return lax.ppermute(value, 'z', [(i, (i + shift) % 8) for i in range(8)])  21.5 us
    ppermute x2, waiting for transfers between devices, home(): return lax.ppermute(out, ('xh', 'core'), HOME)  15 us
    ppermute x4, waiting for transfers between devices, along_y(): return lax.ppermute(value, 'y', [(i, (i + shift) % 4) for i in range(4)])  10.7 us
    ppermute x2, starting transfers between devices, swapped(): turned = lax.ppermute(first, ('xh', 'core'), TURN)  10.1 us
    ppermute x5, starting transfers between devices, exchange(): return lax.ppermute(value, axis, [(i, i ^ flip) for i in range(size)])  9.09 us
    ppermute x2, waiting for transfers between devices, swapped(): turned = lax.ppermute(first, ('xh', 'core'), TURN)  8.71 us
  transfers between devices with their start and end apart: 25, of which 16 were waited for; matrix products, arithmetic and copies ran while one was open for 18% of the time, Pallas kernels for 1%

profile of v6, /device:TPU:1, one launch (start us, length us, event | category | flops | bytes accessed | tf_op | source)
XLA Modules:
  0.0 213.1 jit_solution(12081031110624932546)
XLA Ops:
  1.2 3.3 %collective-permute-start = (bf16[376,256]{1,0:T(8,128)(2,1)S(1)}, bf16[376,256]{1,0:T(8,128)(2,1)S(1)}, u32[]{:S(2)}, u32[]{:S(2)}) collective-permute-start(bf16[376,256]{1,0:T(8,128)(2,1)S(1)} %broadcast_select_fusion.11), channel_id=1, source_target_pairs={{0,1},{1,0},{2,3},{3,2},{4,5},{5,4},{6,7},{7,6},{8,9},{9,8},{10,11... | collective-permute-start | bytes 577544 | tf_op jit(solution)/shard_map/ppermute | solution.py:18
  8.3 4.4 %collective-permute-start.2 = (bf16[256,896]{1,0:T(8,128)(2,1)}, bf16[256,896]{1,0:T(8,128)(2,1)S(1)}, u32[]{:S(2)}, u32[]{:S(2)}) collective-permute-start(bf16[256,896]{1,0:T(8,128)(2,1)} %get-tuple-element.62), channel_id=1, source_target_pairs={{0,0},{1,128},{128,1},{129,129},{2,2},{3,130},{130,3},{131,131},{4... | collective-permute-start | bytes 1376264 | tf_op jit(solution)/shard_map/ppermute | solution.py:107
  12.7 5.1 %collective-permute-done.1 = bf16[376,512]{1,0:T(8,128)(2,1)} collective-permute-done((bf16[376,512]{1,0:T(8,128)(2,1)}, bf16[376,512]{1,0:T(8,128)(2,1)}, u32[]{:S(2)}, u32[]{:S(2)}) %collective-permute-start.1) | collective-permute-done | bytes 385056 | tf_op jit(solution)/shard_map/ppermute | solution.py:18
  20.1 4.1 %collective-permute-done.2 = bf16[256,896]{1,0:T(8,128)(2,1)S(1)} collective-permute-done((bf16[256,896]{1,0:T(8,128)(2,1)}, bf16[256,896]{1,0:T(8,128)(2,1)S(1)}, u32[]{:S(2)}, u32[]{:S(2)}) %collective-permute-start.2) | collective-permute-done | bytes 458784 | tf_op jit(solution)/shard_map/ppermute | solution.py:107
  24.2 5.8 %collective-permute-done.3 = bf16[256,896]{1,0:T(8,128)(2,1)} collective-permute-done((bf16[256,896]{1,0:T(8,128)(2,1)S(1)}, bf16[256,896]{1,0:T(8,128)(2,1)}, u32[]{:S(2)}, u32[]{:S(2)}) %collective-permute-start.3) | collective-permute-done | bytes 458784 | tf_op jit(solution)/shard_map/ppermute | solution.py:108
  31.3 5.7 %collective-permute-start.6 = (bf16[256,768]{1,0:T(8,128)(2,1)S(1)}, bf16[256,768]{1,0:T(8,128)(2,1)S(1)}, u32[]{:S(2)}, u32[]{:S(2)}) collective-permute-start(bf16[256,768]{1,0:T(8,128)(2,1)S(1)} %get-tuple-element.68), channel_id=1, source_target_pairs={{0,0},{1,128},{128,1},{129,129},{2,2},{3,130},{130,3},{131,131},{4... | collective-permute-start | bytes 1179656 | tf_op jit(solution)/shard_map/ppermute | solution.py:107
  37.2 3.5 %collective-permute-start.4 = (bf16[512,896]{1,0:T(8,128)(2,1)S(1)}, bf16[512,896]{1,0:T(8,128)(2,1)S(1)}, u32[]{:S(2)}, u32[]{:S(2)}) collective-permute-start(bf16[512,896]{1,0:T(8,128)(2,1)S(1)} %pad_maximum_fusion.2), channel_id=1, source_target_pairs={{0,16},{16,32},{32,48},{48,64},{64,80},{80,96},{96,112},{112,0},{1... | collective-permute-start | bytes 2752520 | tf_op jit(solution)/shard_map/ppermute | solution.py:85
  40.6 4.0 %collective-permute-start.5 = (bf16[512,896]{1,0:T(8,128)(2,1)S(1)}, bf16[512,896]{1,0:T(8,128)(2,1)S(1)}, u32[]{:S(2)}, u32[]{:S(2)}) collective-permute-start(bf16[512,896]{1,0:T(8,128)(2,1)S(1)} %pad_maximum_fusion.2), channel_id=1, source_target_pairs={{0,112},{16,0},{32,16},{48,32},{64,48},{80,64},{96,80},{112,96},{1... | collective-permute-start | bytes 2752520 | tf_op jit(solution)/shard_map/ppermute | solution.py:85
  44.7 4.6 %collective-permute-done.6 = bf16[256,768]{1,0:T(8,128)(2,1)S(1)} collective-permute-done((bf16[256,768]{1,0:T(8,128)(2,1)S(1)}, bf16[256,768]{1,0:T(8,128)(2,1)S(1)}, u32[]{:S(2)}, u32[]{:S(2)}) %collective-permute-start.6) | collective-permute-done | bytes 393248 | tf_op jit(solution)/shard_map/ppermute | solution.py:107
  54.0 4.0 %collective-permute-start.9 = (bf16[512,768]{1,0:T(8,128)(2,1)S(1)}, bf16[512,768]{1,0:T(8,128)(2,1)S(1)}, u32[]{:S(2)}, u32[]{:S(2)}) collective-permute-start(bf16[512,768]{1,0:T(8,128)(2,1)S(1)} %pad_maximum_fusion.3), channel_id=1, source_target_pairs={{0,112},{16,0},{32,16},{48,32},{64,48},{80,64},{96,80},{112,96},{1... | collective-permute-start | bytes 2359304 | tf_op jit(solution)/shard_map/ppermute | solution.py:85
  58.0 6.9 %collective-permute-done.4 = bf16[512,896]{1,0:T(8,128)(2,1)S(1)} collective-permute-done((bf16[512,896]{1,0:T(8,128)(2,1)S(1)}, bf16[512,896]{1,0:T(8,128)(2,1)S(1)}, u32[]{:S(2)}, u32[]{:S(2)}) %collective-permute-start.4) | collective-permute-done | bytes 917536 | tf_op jit(solution)/shard_map/ppermute | solution.py:85
  69.8 12.0 %collective-permute-done.8 = bf16[512,768]{1,0:T(8,128)(2,1)S(1)} collective-permute-done((bf16[512,768]{1,0:T(8,128)(2,1)S(1)}, bf16[512,768]{1,0:T(8,128)(2,1)S(1)}, u32[]{:S(2)}, u32[]{:S(2)}) %collective-permute-start.8) | collective-permute-done | bytes 786464 | tf_op jit(solution)/shard_map/ppermute | solution.py:85
  88.5 10.7 %collective-permute-done.14.down = bf16[2,376,1024]{2,1,0:T(8,128)(2,1)S(1)} collective-permute-done((bf16[2,376,1024]{2,1,0:T(8,128)(2,1)S(1)}, bf16[2,376,1024]{2,1,0:T(8,128)(2,1)S(1)}, u32[]{:S(2)}, u32[]{:S(2)}) %collective-permute-start.14) | collective-permute-done | bytes 1540128 | tf_op jit(solution)/shard_map/ppermute | solution.py:40
  101.3 3.5 %collective-permute-start.16 = (bf16[376,1024]{1,0:T(8,128)(2,1)}, bf16[376,1024]{1,0:T(8,128)(2,1)}, u32[]{:S(2)}, u32[]{:S(2)}) collective-permute-start(bf16[376,1024]{1,0:T(8,128)(2,1)} %slice_bitcast_fusion), channel_id=1, source_target_pairs={{0,6},{2,0},{4,2},{6,4},{1,7},{3,1},{5,3},{7,5},{8,14},{10,8},{12,... | collective-permute-start | bytes 2310152 | tf_op jit(solution)/shard_map/ppermute | solution.py:40
  104.9 16.1 %collective-permute-done.11 = bf16[512,1664]{1,0:T(8,128)(2,1)} collective-permute-done((bf16[512,1664]{1,0:T(8,128)(2,1)}, bf16[512,1664]{1,0:T(8,128)(2,1)}, u32[]{:S(2)}, u32[]{:S(2)}) %collective-permute-start.11) | collective-permute-done | bytes 1703968 | tf_op jit(solution)/shard_map/ppermute | solution.py:85
  121.0 4.1 %collective-permute-done.10 = bf16[512,1664]{1,0:T(8,128)(2,1)} collective-permute-done((bf16[512,1664]{1,0:T(8,128)(2,1)}, bf16[512,1664]{1,0:T(8,128)(2,1)}, u32[]{:S(2)}, u32[]{:S(2)}) %collective-permute-start.10) | collective-permute-done | bytes 1703968 | tf_op jit(solution)/shard_map/ppermute | solution.py:85
  134.8 3.1 %fusion.15 = f32[752,1664]{1,0:T(8,128)S(1)} fusion(bf16[512,1664]{1,0:T(8,128)(2,1)} %constant_dynamic-update-slice_fusion.2, bf16[752,4096]{1,0:T(8,128)(2,1)S(1)} %bitcast.16), kind=kOutput, calls=%fused_computation.25 | convolution fusion | flops 1281359872 | bytes 7479296 | tf_op jit(solution)/shard_map/dot_general | solution.py:99
  137.9 3.8 %fusion = f32[752,1664]{1,0:T(8,128)} fusion(bf16[256,768]{1,0:T(8,128)(2,1)S(1)} %copy-done.4, bf16[256,768]{1,0:T(8,128)(2,1)S(1)} %get-tuple-element.65, bf16[512,896]{1,0:T(8,128)(2,1)S(1)} %copy-done.6, bf16[752,4096]{1,0:T(8,128)(2,1)S(1)} %bitcast.17), kind=kOutput, calls=%fused_computation.4 | convolution fusion | flops 1286471680 | bytes 7479296 | tf_op jit(solution)/shard_map/dot_general | solution.py:99
  144.8 7.2 %add_add_fusion.1 = f32[752,1664]{1,0:T(8,128)} fusion(f32[752,1664]{1,0:T(8,128)S(1)} %fusion.13, f32[752,1664]{1,0:T(8,128)S(1)} %fusion.15, f32[752,1664]{1,0:T(8,128)} %fusion, f32[752,1664]{1,0:T(8,128)S(1)} %fusion.17, bf16[512,1664]{1,0:T(8,128)(2,1)} %collective-permute-done.11, bf16[752,4096]{1,0:T(8,128)(2,1)S(1)} %bitcast.19), kind=kOutput, calls=%fused_computation.1 | convolution fusion | flops 1286365184 | bytes 27500544 | tf_op jit(solution)/shard_map/dot_general | solution.py:99
  152.0 10.9 %collective-permute-done.17 = bf16[512,1664]{1,0:T(8,128)(2,1)} collective-permute-done((bf16[512,1664]{1,0:T(8,128)(2,1)}, bf16[512,1664]{1,0:T(8,128)(2,1)}, u32[]{:S(2)}, u32[]{:S(2)}) %collective-permute-start.17) | collective-permute-done | bytes 1703968 | tf_op jit(solution)/shard_map/ppermute | solution.py:85
  171.6 3.2 %add_add_fusion = f32[752,1664]{1,0:T(8,128)S(1)} fusion(f32[752,1664]{1,0:T(8,128)S(1)} %bitcast.27, f32[752,1664]{1,0:T(8,128)S(1)} %fusion.7, bf16[512,1664]{1,0:T(8,128)(2,1)} %collective-permute-done.18, bf16[752,4096]{1,0:T(8,128)(2,1)S(1)} %bitcast.21), kind=kOutput, calls=%fused_computation | convolution fusion | flops 1283862528 | bytes 17489920 | tf_op jit(solution)/shard_map/dot_general | solution.py:99
  174.8 7.8 %collective-permute-done.19 = bf16[256,1664]{1,0:T(8,128)(2,1)S(1)} collective-permute-done((bf16[256,1664]{1,0:T(8,128)(2,1)S(1)}, bf16[256,1664]{1,0:T(8,128)(2,1)S(1)}, u32[]{:S(2)}, u32[]{:S(2)}) %collective-permute-start.19) | collective-permute-done | bytes 852000 | tf_op jit(solution)/shard_map/ppermute | solution.py:85
  185.0 4.6 %collective-permute-start.21 = (f32[376,896]{1,0:T(8,128)S(1)}, f32[376,896]{1,0:T(8,128)S(1)}, u32[]{:S(2)}, u32[]{:S(2)}) collective-permute-start(f32[376,896]{1,0:T(8,128)S(1)} %slice_select_fusion), channel_id=1, source_target_pairs={{0,1},{1,0},{2,3},{3,2},{4,5},{5,4},{6,7},{7,6},{8,9},{9,8},{10,11... | collective-permute-start | bytes 4042760 | tf_op jit(solution)/shard_map/ppermute | solution.py:18
  197.0 15.0 %collective-permute-done.24 = bf16[376,768]{1,0:T(8,128)(2,1)S(1)} collective-permute-done((bf16[376,768]{1,0:T(8,128)(2,1)S(1)}, bf16[376,768]{1,0:T(8,128)(2,1)S(1)}, u32[]{:S(2)}, u32[]{:S(2)}) %collective-permute-start.24) | collective-permute-done | bytes 577568 | tf_op jit(solution)/shard_map/ppermute | solution.py:122
  (85 shorter events, 59.2 us)
Async XLA Ops:
  7.4 10.5 %collective-permute-start.1 = (bf16[376,512]{1,0:T(8,128)(2,1)}, bf16[376,512]{1,0:T(8,128)(2,1)}, u32[]{:S(2)}, u32[]{:S(2)}) collective-permute-start(bf16[376,512]{1,0:T(8,128)(2,1)} %pad_maximum_fusion.5), channel_id=1, source_target_pairs={{0,8},{8,0},{1,9},{9,1},{2,10},{10,2},{3,11},{11,3},{4,12},{12,4},... | collective-permute-start | bytes 1155080 | tf_op jit(solution)/shard_map/ppermute | solution.py:18
  8.3 15.9 %collective-permute-start.2 = (bf16[256,896]{1,0:T(8,128)(2,1)}, bf16[256,896]{1,0:T(8,128)(2,1)S(1)}, u32[]{:S(2)}, u32[]{:S(2)}) collective-permute-start(bf16[256,896]{1,0:T(8,128)(2,1)} %get-tuple-element.62), channel_id=1, source_target_pairs={{0,0},{1,128},{128,1},{129,129},{2,2},{3,130},{130,3},{131,131},{4... | collective-permute-start | bytes 1376264 | tf_op jit(solution)/shard_map/ppermute | solution.py:107
  12.6 17.4 %collective-permute-start.3 = (bf16[256,896]{1,0:T(8,128)(2,1)S(1)}, bf16[256,896]{1,0:T(8,128)(2,1)}, u32[]{:S(2)}, u32[]{:S(2)}) collective-permute-start(bf16[256,896]{1,0:T(8,128)(2,1)S(1)} %get-tuple-element.61), channel_id=1, source_target_pairs={{0,1},{1,129},{128,0},{129,128},{2,3},{3,131},{130,2},{131,130},{4... | collective-permute-start | bytes 1376264 | tf_op jit(solution)/shard_map/ppermute | solution.py:108
  19.0 32.2 %collective-permute-start.12 = (bf16[376,1024]{1,0:T(8,128)(2,1)S(1)}, bf16[376,1024]{1,0:T(8,128)(2,1)S(1)}, u32[]{:S(2)}, u32[]{:S(2)}) collective-permute-start(bf16[376,1024]{1,0:T(8,128)(2,1)S(1)} %pad_maximum_fusion.4), channel_id=1, source_target_pairs={{0,128},{128,0},{1,129},{129,1},{2,130},{130,2},{3,131},{131,3},{4... | collective-permute-start | bytes 2310152 | tf_op jit(solution)/shard_map/ppermute | solution.py:18
  31.3 17.9 %collective-permute-start.6 = (bf16[256,768]{1,0:T(8,128)(2,1)S(1)}, bf16[256,768]{1,0:T(8,128)(2,1)S(1)}, u32[]{:S(2)}, u32[]{:S(2)}) collective-permute-start(bf16[256,768]{1,0:T(8,128)(2,1)S(1)} %get-tuple-element.68), channel_id=1, source_target_pairs={{0,0},{1,128},{128,1},{129,129},{2,2},{3,130},{130,3},{131,131},{4... | collective-permute-start | bytes 1179656 | tf_op jit(solution)/shard_map/ppermute | solution.py:107
  37.1 14.1 %collective-permute-start.7 = (bf16[256,768]{1,0:T(8,128)(2,1)S(1)}, bf16[256,768]{1,0:T(8,128)(2,1)S(1)}, u32[]{:S(2)}, u32[]{:S(2)}) collective-permute-start(bf16[256,768]{1,0:T(8,128)(2,1)S(1)} %get-tuple-element.67), channel_id=1, source_target_pairs={{0,1},{1,129},{128,0},{129,128},{2,3},{3,131},{130,2},{131,130},{4... | collective-permute-start | bytes 1179656 | tf_op jit(solution)/shard_map/ppermute | solution.py:108
  37.2 27.8 %collective-permute-start.4 = (bf16[512,896]{1,0:T(8,128)(2,1)S(1)}, bf16[512,896]{1,0:T(8,128)(2,1)S(1)}, u32[]{:S(2)}, u32[]{:S(2)}) collective-permute-start(bf16[512,896]{1,0:T(8,128)(2,1)S(1)} %pad_maximum_fusion.2), channel_id=1, source_target_pairs={{0,16},{16,32},{32,48},{48,64},{64,80},{80,96},{96,112},{112,0},{1... | collective-permute-start | bytes 2752520 | tf_op jit(solution)/shard_map/ppermute | solution.py:85
  40.6 27.0 %collective-permute-start.5 = (bf16[512,896]{1,0:T(8,128)(2,1)S(1)}, bf16[512,896]{1,0:T(8,128)(2,1)S(1)}, u32[]{:S(2)}, u32[]{:S(2)}) collective-permute-start(bf16[512,896]{1,0:T(8,128)(2,1)S(1)} %pad_maximum_fusion.2), channel_id=1, source_target_pairs={{0,112},{16,0},{32,16},{48,32},{64,48},{80,64},{96,80},{112,96},{1... | collective-permute-start | bytes 2752520 | tf_op jit(solution)/shard_map/ppermute | solution.py:85
  51.4 34.9 %collective-permute-start.13 = (bf16[2,376,1024]{2,1,0:T(8,128)(2,1)S(1)}, bf16[2,376,1024]{2,1,0:T(8,128)(2,1)S(1)}, u32[]{:S(2)}, u32[]{:S(2)}) collective-permute-start(bf16[2,376,1024]{2,1,0:T(8,128)(2,1)S(1)} %pad_maximum_fusion.here), channel_id=1, source_target_pairs={{0,2},{2,4},{4,6},{6,0},{1,3},{3,5},{5,7},{7,1},{8,10},{10,12},{12... | collective-permute-start | bytes 4620296 | tf_op jit(solution)/shard_map/ppermute | solution.py:40
  52.3 29.5 %collective-permute-start.8 = (bf16[512,768]{1,0:T(8,128)(2,1)S(1)}, bf16[512,768]{1,0:T(8,128)(2,1)S(1)}, u32[]{:S(2)}, u32[]{:S(2)}) collective-permute-start(bf16[512,768]{1,0:T(8,128)(2,1)S(1)} %pad_maximum_fusion.3), channel_id=1, source_target_pairs={{0,16},{16,32},{32,48},{48,64},{64,80},{80,96},{96,112},{112,0},{1... | collective-permute-start | bytes 2359304 | tf_op jit(solution)/shard_map/ppermute | solution.py:85
  54.0 27.8 %collective-permute-start.9 = (bf16[512,768]{1,0:T(8,128)(2,1)S(1)}, bf16[512,768]{1,0:T(8,128)(2,1)S(1)}, u32[]{:S(2)}, u32[]{:S(2)}) collective-permute-start(bf16[512,768]{1,0:T(8,128)(2,1)S(1)} %pad_maximum_fusion.3), channel_id=1, source_target_pairs={{0,112},{16,0},{32,16},{48,32},{64,48},{80,64},{96,80},{112,96},{1... | collective-permute-start | bytes 2359304 | tf_op jit(solution)/shard_map/ppermute | solution.py:85
  64.9 34.3 %collective-permute-start.14 = (bf16[2,376,1024]{2,1,0:T(8,128)(2,1)S(1)}, bf16[2,376,1024]{2,1,0:T(8,128)(2,1)S(1)}, u32[]{:S(2)}, u32[]{:S(2)}) collective-permute-start(bf16[2,376,1024]{2,1,0:T(8,128)(2,1)S(1)} %pad_maximum_fusion.here), channel_id=1, source_target_pairs={{0,6},{2,0},{4,2},{6,4},{1,7},{3,1},{5,3},{7,5},{8,14},{10,8},{12,... | collective-permute-start | bytes 4620296 | tf_op jit(solution)/shard_map/ppermute | solution.py:40
  82.8 38.2 %collective-permute-start.11 = (bf16[512,1664]{1,0:T(8,128)(2,1)}, bf16[512,1664]{1,0:T(8,128)(2,1)}, u32[]{:S(2)}, u32[]{:S(2)}) collective-permute-start(bf16[512,1664]{1,0:T(8,128)(2,1)} %constant_dynamic-update-slice_fusion.2), channel_id=1, source_target_pairs={{0,112},{16,0},{32,16},{48,32},{64,48},{80,64},{96,80},{112,96},{1... | collective-permute-start | bytes 5111816 | tf_op jit(solution)/shard_map/ppermute | solution.py:85
  86.2 38.8 %collective-permute-start.10 = (bf16[512,1664]{1,0:T(8,128)(2,1)}, bf16[512,1664]{1,0:T(8,128)(2,1)}, u32[]{:S(2)}, u32[]{:S(2)}) collective-permute-start(bf16[512,1664]{1,0:T(8,128)(2,1)} %constant_dynamic-update-slice_fusion), channel_id=1, source_target_pairs={{0,16},{16,32},{32,48},{48,64},{64,80},{80,96},{96,112},{112,0},{1... | collective-permute-start | bytes 5111816 | tf_op jit(solution)/shard_map/ppermute | solution.py:85
  87.2 40.5 %collective-permute-start.15 = (bf16[376,1024]{1,0:T(8,128)(2,1)}, bf16[376,1024]{1,0:T(8,128)(2,1)}, u32[]{:S(2)}, u32[]{:S(2)}) collective-permute-start(bf16[376,1024]{1,0:T(8,128)(2,1)} %slice_bitcast_fusion.1), channel_id=1, source_target_pairs={{0,2},{2,4},{4,6},{6,0},{1,3},{3,5},{5,7},{7,1},{8,10},{10,12},{12... | collective-permute-start | bytes 2310152 | tf_op jit(solution)/shard_map/ppermute | solution.py:40
  101.3 26.4 %collective-permute-start.16 = (bf16[376,1024]{1,0:T(8,128)(2,1)}, bf16[376,1024]{1,0:T(8,128)(2,1)}, u32[]{:S(2)}, u32[]{:S(2)}) collective-permute-start(bf16[376,1024]{1,0:T(8,128)(2,1)} %slice_bitcast_fusion), channel_id=1, source_target_pairs={{0,6},{2,0},{4,2},{6,4},{1,7},{3,1},{5,3},{7,5},{8,14},{10,8},{12,... | collective-permute-start | bytes 2310152 | tf_op jit(solution)/shard_map/ppermute | solution.py:40
  125.0 37.9 %collective-permute-start.17 = (bf16[512,1664]{1,0:T(8,128)(2,1)}, bf16[512,1664]{1,0:T(8,128)(2,1)}, u32[]{:S(2)}, u32[]{:S(2)}) collective-permute-start(bf16[512,1664]{1,0:T(8,128)(2,1)} %collective-permute-done.10), channel_id=1, source_target_pairs={{0,16},{16,32},{32,48},{48,64},{64,80},{80,96},{96,112},{112,0},{1... | collective-permute-start | bytes 5111816 | tf_op jit(solution)/shard_map/ppermute | solution.py:85
  125.0 37.9 %collective-permute-start.18 = (bf16[512,1664]{1,0:T(8,128)(2,1)}, bf16[512,1664]{1,0:T(8,128)(2,1)}, u32[]{:S(2)}, u32[]{:S(2)}) collective-permute-start(bf16[512,1664]{1,0:T(8,128)(2,1)} %collective-permute-done.11), channel_id=1, source_target_pairs={{0,112},{16,0},{32,16},{48,32},{64,48},{80,64},{96,80},{112,96},{1... | collective-permute-start | bytes 5111816 | tf_op jit(solution)/shard_map/ppermute | solution.py:85
  164.1 18.4 %collective-permute-start.19 = (bf16[256,1664]{1,0:T(8,128)(2,1)S(1)}, bf16[256,1664]{1,0:T(8,128)(2,1)S(1)}, u32[]{:S(2)}, u32[]{:S(2)}) collective-permute-start(bf16[256,1664]{1,0:T(8,128)(2,1)S(1)} %slice.117), channel_id=1, source_target_pairs={{0,16},{16,32},{32,48},{48,64},{64,80},{80,96},{96,112},{112,0},{1... | collective-permute-start | bytes 2555912 | tf_op jit(solution)/shard_map/ppermute | solution.py:85
  165.6 17.6 %collective-permute-start.20 = (bf16[256,1664]{1,0:T(8,128)(2,1)S(1)}, bf16[256,1664]{1,0:T(8,128)(2,1)S(1)}, u32[]{:S(2)}, u32[]{:S(2)}) collective-permute-start(bf16[256,1664]{1,0:T(8,128)(2,1)S(1)} %slice.118), channel_id=1, source_target_pairs={{0,112},{16,0},{32,16},{48,32},{64,48},{80,64},{96,80},{112,96},{1... | collective-permute-start | bytes 2555912 | tf_op jit(solution)/shard_map/ppermute | solution.py:85
  185.0 7.3 %collective-permute-start.21 = (f32[376,896]{1,0:T(8,128)S(1)}, f32[376,896]{1,0:T(8,128)S(1)}, u32[]{:S(2)}, u32[]{:S(2)}) collective-permute-start(f32[376,896]{1,0:T(8,128)S(1)} %slice_select_fusion), channel_id=1, source_target_pairs={{0,1},{1,0},{2,3},{3,2},{4,5},{5,4},{6,7},{7,6},{8,9},{9,8},{10,11... | collective-permute-start | bytes 4042760 | tf_op jit(solution)/shard_map/ppermute | solution.py:18
  190.2 4.5 %collective-permute-start.23 = (f32[376,768]{1,0:T(8,128)S(1)}, f32[376,768]{1,0:T(8,128)S(1)}, u32[]{:S(2)}, u32[]{:S(2)}) collective-permute-start(f32[376,768]{1,0:T(8,128)S(1)} %slice_select_fusion.1), channel_id=1, source_target_pairs={{0,1},{1,0},{2,3},{3,2},{4,5},{5,4},{6,7},{7,6},{8,9},{9,8},{10,11... | collective-permute-start | bytes 3465224 | tf_op jit(solution)/shard_map/ppermute | solution.py:18
  192.7 19.2 %collective-permute-start.22 = (bf16[376,896]{1,0:T(8,128)(2,1)S(1)}, bf16[376,896]{1,0:T(8,128)(2,1)S(1)}, u32[]{:S(2)}, u32[]{:S(2)}) collective-permute-start(bf16[376,896]{1,0:T(8,128)(2,1)S(1)} %multiply_convert_fusion), channel_id=1, source_target_pairs={{0,0},{1,128},{128,129},{129,1},{2,2},{3,130},{130,131},{131,3},{4... | collective-permute-start | bytes 2021384 | tf_op jit(solution)/shard_map/ppermute | solution.py:122
  195.0 16.9 %collective-permute-start.24 = (bf16[376,768]{1,0:T(8,128)(2,1)S(1)}, bf16[376,768]{1,0:T(8,128)(2,1)S(1)}, u32[]{:S(2)}, u32[]{:S(2)}) collective-permute-start(bf16[376,768]{1,0:T(8,128)(2,1)S(1)} %multiply_convert_fusion.1), channel_id=1, source_target_pairs={{0,0},{1,128},{128,129},{129,1},{2,2},{3,130},{130,131},{131,3},{4... | collective-permute-start | bytes 1732616 | tf_op jit(solution)/shard_map/ppermute | solution.py:122
  (11 other events, 67.4 us)

commit v7 on v6

--- a/solution.py
+++ b/solution.py
@@ -7,7 +7,8 @@
 
 AXES = ("xh", "z", "xl", "y", "core")
 SIZES = (2, 8, 2, 4, 2)
-WIDTHS = (896, 768)
+FIRST = 768
+LAST = 1024
 
 TURN = [(h * 2 + c, c * 2 + h) for h in range(2) for c in range(2)]
 CROSS = [(h * 2 + c, c * 2 + 1 - h) for h in range(2) for c in range(2)]
@@ -30,10 +31,13 @@
     core = lax.axis_index("core")
     half = tokens.shape[1] // 2
     mine, other = swap_if(core == 1, tokens[:, :half], tokens[:, half:])
-    received = exchange(other, "core", 1, 2)
-    near = swap_if(core == 1, mine, received)
-    far = exchange(jnp.concatenate(near, axis=1), "xl", 1, 2)
-    return jnp.concatenate([near[0], far[:, :half], near[1], far[:, half:]], axis=1)
+    return jnp.concatenate(swap_if(core == 1, mine, exchange(other, "core", 1, 2)), axis=1)
+
+
+def tokens_of_pair(near):
+    half = near.shape[1] // 2
+    far = exchange(near, "xl", 1, 2)
+    return jnp.concatenate([near[:, :half], far[:, :half], near[:, half:], far[:, half:]], axis=1)
 
 
 def along_y(value, shift):
@@ -100,14 +104,13 @@
     return total
 
 
-def swapped(weight, *also):
+def swapped(weight):
     xh, xl, core = (lax.axis_index(name) for name in ("xh", "xl", "core"))
     half = weight.shape[0] // 2
     first, second = swap_if(xh == 1, weight[:half], weight[half:])
     turned = lax.ppermute(first, ("xh", "core"), TURN)
     crossed = lax.ppermute(second, ("xh", "core"), CROSS)
-    *also, turned, crossed = together(*also, turned, crossed)
-    return jnp.concatenate(swap_if(xl != core, turned, crossed)), *also
+    return jnp.concatenate(swap_if(xl != core, turned, crossed))
 
 
 def activate(total):
@@ -124,14 +127,13 @@
 
 def on_device(tokens, weight):
     half = weight.shape[0] // 2
-    cut = WIDTHS[0]
-    piece = tokens_of_core(tokens)
+    mine, tokens = together(swapped(weight[:, :FIRST]), tokens)
+    up, down = together(*step_along_z(1, mine, mine))
+    near, rest = together(tokens_of_core(tokens), weight[:, FIRST:])
+    rest = swapped(rest)
+    rest_up, rest_down = together(*step_along_z(1, rest, rest))
+    piece, up, down = together(tokens_of_pair(near), up, down)
     beside = exchange(piece, "xh", 1, 2)
-    mine, piece = swapped(weight[:, :cut], piece)
-    rest, mine = together(weight[:, cut:], mine)
-    up, down = together(*step_along_z(1, mine, mine))
-    (rest,) = swapped(rest)
-    rest_up, rest_down = together(*step_along_z(1, rest, rest))
     both = jnp.stack([piece, beside])
     pieces = gather_along_y(both)
     mine = jnp.concatenate([mine, rest], axis=1)
@@ -147,12 +149,15 @@
     early = product(gathered, blocks[:5], half)
     early, up, down = together(early, up, down)
     early += product(gathered, [(6, up), (10, down)], half)
-    up, down, early = together(*step_along_z(4, up, down), early)
-    outs = []
-    for columns in (slice(0, cut), slice(cut, None)):
-        last = product(gathered, ((8, up[:, columns]), (9, down[:, columns])), half)
-        outs.append(home(activate(early[:, columns] + last)))
-    return jnp.concatenate(outs, axis=1)
+    ends = [
+        step_along_z(4, up[:, columns], down[:, columns])
+        for columns in (slice(0, LAST), slice(LAST, None))
+    ]
+    up, down, early = together(*ends[0], early)
+    first = activate(early[:, :LAST] + product(gathered, ((8, up), (9, down)), half))
+    up, down, first = together(*ends[1], first)
+    second = activate(early[:, LAST:] + product(gathered, ((8, up), (9, down)), half))
+    return jnp.concatenate([home(first), home(second)], axis=1)
 
 
 def solution(mesh):

time: 214 us -> 212 us (level)
  waiting for transfers between devices: 109 us -> 113 us
  starting transfers between devices: 53.1 us -> 49.3 us
  other arithmetic: 7.71 us -> 4.56 us
    ppermute x4, waiting for transfers between devices: 10.7 us -> 24.6 us  [along_y(): return lax.ppermute(value, 'y', [(i, (i + shift) % 4) for i in range(4)])]
    ppermute x10 -> x12, waiting for transfers between devices: 58.5 us -> 47.6 us  [along_z(): return lax.ppermute(value, 'z', [(i, (i + shift) % 8) for i in range(8)])]
    ppermute x2, waiting for transfers between devices: 7.7 us -> 0.01 us  [swapped(): crossed = lax.ppermute(second, ('xh', 'core'), CROSS)]
    ppermute x5, waiting for transfers between devices: 8.2 us -> 15 us  [exchange(): return lax.ppermute(value, axis, [(i, i ^ flip) for i in range(size)])]
    ppermute x2, starting transfers between devices: 0.19 us -> 5.57 us  [swapped(): crossed = lax.ppermute(second, ('xh', 'core'), CROSS)]
    ppermute x4, starting transfers between devices: 8.39 us -> 5.58 us  [along_y(): return lax.ppermute(value, 'y', [(i, (i + shift) % 4) for i in range(4)])]
    select_n x8, other arithmetic: 4.57 us -> 1.91 us  [swap_if(): return (jnp.where(flag, second, first), jnp.where(flag, first, second))]
    ppermute x10 -> x12, starting transfers between devices: 21.5 us -> 18.9 us  [along_z(): return lax.ppermute(value, 'z', [(i, (i + shift) % 8) for i in range(8)])]
  transfers between devices with their start and end apart: 25 -> 27, of which waited for: 16 -> 18; matrix products, arithmetic and copies ran while one was open for 18% -> 16% of each run, Pallas kernels for 1% -> 1%
where the time goes in v7:
time: 212 us; the launch traced here: 211 us
  waiting for transfers between devices  113 us (53%)
  starting transfers between devices  49.3 us (23%)
  matrix products  28.7 us (14%)
  local copies, waits for them, and re-layouts  12.7 us (6%)
  other arithmetic  4.56 us (2%)
  Pallas kernels  2.63 us (1%)
    ppermute x12, waiting for transfers between devices, along_z(): return lax.ppermute(value, 'z', [(i, (i + shift) % 8) for i in range(8)])  47.6 us
    dot_general x11, matrix products, product(): total += jnp.dot(features, piece, preferred_element_type=jnp.float32)  28.7 us
    ppermute x4, waiting for transfers between devices, along_y(): return lax.ppermute(value, 'y', [(i, (i + shift) % 4) for i in range(4)])  24.6 us
    ppermute x12, starting transfers between devices, along_z(): return lax.ppermute(value, 'z', [(i, (i + shift) % 8) for i in range(8)])  18.9 us
    ppermute x5, waiting for transfers between devices, exchange(): return lax.ppermute(value, axis, [(i, i ^ flip) for i in range(size)])  15 us
    ppermute x2, waiting for transfers between devices, home(): return lax.ppermute(out, ('xh', 'core'), HOME)  14.8 us
    ppermute x2, waiting for transfers between devices, swapped(): turned = lax.ppermute(first, ('xh', 'core'), TURN)  10.8 us
    ppermute x2, starting transfers between devices, swapped(): turned = lax.ppermute(first, ('xh', 'core'), TURN)  8.8 us
  transfers between devices with their start and end apart: 27, of which 18 were waited for; matrix products, arithmetic and copies ran while one was open for 16% of the time, Pallas kernels for 1%

profile of v7, /device:TPU:1, one launch (start us, length us, event | category | flops | bytes accessed | tf_op | source)
XLA Modules:
  0.0 211.1 jit_solution(7641587536589134176)
XLA Ops:
  1.2 3.7 %collective-permute-start = (bf16[256,768]{1,0:T(8,128)(2,1)S(1)}, bf16[256,768]{1,0:T(8,128)(2,1)S(1)}, u32[]{:S(2)}, u32[]{:S(2)}) collective-permute-start(bf16[256,768]{1,0:T(8,128)(2,1)S(1)} %get-tuple-element.67), channel_id=1, source_target_pairs={{0,1},{1,129},{128,0},{129,128},{2,3},{3,131},{130,2},{131,130},{4... | collective-permute-start | bytes 1179656 | tf_op jit(solution)/shard_map/ppermute | solution.py:112
  4.8 4.7 %collective-permute-start.1 = (bf16[256,768]{1,0:T(8,128)(2,1)S(1)}, bf16[256,768]{1,0:T(8,128)(2,1)S(1)}, u32[]{:S(2)}, u32[]{:S(2)}) collective-permute-start(bf16[256,768]{1,0:T(8,128)(2,1)S(1)} %get-tuple-element.68), channel_id=1, source_target_pairs={{0,0},{1,128},{128,1},{129,129},{2,2},{3,130},{130,3},{131,131},{4... | collective-permute-start | bytes 1179656 | tf_op jit(solution)/shard_map/ppermute | solution.py:111
  9.6 7.7 %collective-permute-done.1 = bf16[256,768]{1,0:T(8,128)(2,1)S(1)} collective-permute-done((bf16[256,768]{1,0:T(8,128)(2,1)S(1)}, bf16[256,768]{1,0:T(8,128)(2,1)S(1)}, u32[]{:S(2)}, u32[]{:S(2)}) %collective-permute-start.1) | collective-permute-done | bytes 393248 | tf_op jit(solution)/shard_map/ppermute | solution.py:111
  17.7 3.9 %collective-permute-start.5 = (bf16[512,768]{1,0:T(8,128)(2,1)S(1)}, bf16[512,768]{1,0:T(8,128)(2,1)S(1)}, u32[]{:S(2)}, u32[]{:S(2)}) collective-permute-start(bf16[512,768]{1,0:T(8,128)(2,1)S(1)} %pad_maximum_fusion.3), channel_id=1, source_target_pairs={{0,112},{16,0},{32,16},{48,32},{64,48},{80,64},{96,80},{112,96},{1... | collective-permute-start | bytes 2359304 | tf_op jit(solution)/shard_map/ppermute | solution.py:89
  25.0 4.1 %collective-permute-start.7 = (bf16[256,896]{1,0:T(8,128)(2,1)S(1)}, bf16[256,896]{1,0:T(8,128)(2,1)S(1)}, u32[]{:S(2)}, u32[]{:S(2)}) collective-permute-start(bf16[256,896]{1,0:T(8,128)(2,1)S(1)} %get-tuple-element.72), channel_id=1, source_target_pairs={{0,0},{1,128},{128,1},{129,129},{2,2},{3,130},{130,3},{131,131},{4... | collective-permute-start | bytes 1376264 | tf_op jit(solution)/shard_map/ppermute | solution.py:111
  31.8 7.3 %collective-permute-done.4 = bf16[512,768]{1,0:T(8,128)(2,1)S(1)} collective-permute-done((bf16[512,768]{1,0:T(8,128)(2,1)S(1)}, bf16[512,768]{1,0:T(8,128)(2,1)S(1)}, u32[]{:S(2)}, u32[]{:S(2)}) %collective-permute-start.4) | collective-permute-done | bytes 786464 | tf_op jit(solution)/shard_map/ppermute | solution.py:89
  41.6 3.1 %collective-permute-done.7 = bf16[256,896]{1,0:T(8,128)(2,1)S(1)} collective-permute-done((bf16[256,896]{1,0:T(8,128)(2,1)S(1)}, bf16[256,896]{1,0:T(8,128)(2,1)S(1)}, u32[]{:S(2)}, u32[]{:S(2)}) %collective-permute-start.7) | collective-permute-done | bytes 458784 | tf_op jit(solution)/shard_map/ppermute | solution.py:111
  47.6 12.3 %collective-permute-done.12 = bf16[376,1024]{1,0:T(8,128)(2,1)S(1)} collective-permute-done((bf16[376,1024]{1,0:T(8,128)(2,1)S(1)}, bf16[376,1024]{1,0:T(8,128)(2,1)S(1)}, u32[]{:S(2)}, u32[]{:S(2)}) %collective-permute-start.12) | collective-permute-done | bytes 770080 | tf_op jit(solution)/shard_map/ppermute | solution.py:19
  71.8 23.7 %collective-permute-done.13.up = bf16[2,376,1024]{2,1,0:T(8,128)(2,1)S(1)} collective-permute-done((bf16[2,376,1024]{2,1,0:T(8,128)(2,1)S(1)}, bf16[2,376,1024]{2,1,0:T(8,128)(2,1)S(1)}, u32[]{:S(2)}, u32[]{:S(2)}) %collective-permute-start.13) | collective-permute-done | bytes 1540128 | tf_op jit(solution)/shard_map/ppermute | solution.py:44
  101.3 6.2 %collective-permute-done.11 = bf16[512,1664]{1,0:T(8,128)(2,1)} collective-permute-done((bf16[512,1664]{1,0:T(8,128)(2,1)}, bf16[512,1664]{1,0:T(8,128)(2,1)}, u32[]{:S(2)}, u32[]{:S(2)}) %collective-permute-start.11) | collective-permute-done | bytes 1703968 | tf_op jit(solution)/shard_map/ppermute | solution.py:89
  107.6 4.7 %collective-permute-done.10 = bf16[512,1664]{1,0:T(8,128)(2,1)} collective-permute-done((bf16[512,1664]{1,0:T(8,128)(2,1)}, bf16[512,1664]{1,0:T(8,128)(2,1)}, u32[]{:S(2)}, u32[]{:S(2)}) %collective-permute-start.10) | collective-permute-done | bytes 1703968 | tf_op jit(solution)/shard_map/ppermute | solution.py:89
  119.9 3.0 %fusion.17 = f32[752,1664]{1,0:T(8,128)S(1)} fusion(bf16[512,1664]{1,0:T(8,128)(2,1)} %constant_dynamic-update-slice_fusion, bf16[752,4096]{1,0:T(8,128)(2,1)S(1)} %bitcast.19), kind=kOutput, calls=%fused_computation.27 | convolution fusion | flops 1281359872 | bytes 7479296 | tf_op jit(solution)/shard_map/dot_general | solution.py:103
  122.9 3.1 %fusion.15 = f32[752,1664]{1,0:T(8,128)S(1)} fusion(bf16[512,1664]{1,0:T(8,128)(2,1)} %constant_dynamic-update-slice_fusion.2, bf16[752,4096]{1,0:T(8,128)(2,1)S(1)} %bitcast.20), kind=kOutput, calls=%fused_computation.25 | convolution fusion | flops 1281359872 | bytes 7479296 | tf_op jit(solution)/shard_map/dot_general | solution.py:103
  126.0 3.8 %fusion = f32[752,1664]{1,0:T(8,128)} fusion(bf16[256,896]{1,0:T(8,128)(2,1)S(1)} %copy-done.4, bf16[256,896]{1,0:T(8,128)(2,1)S(1)} %get-tuple-element.69, bf16[512,768]{1,0:T(8,128)(2,1)S(1)} %copy-done.7, bf16[752,4096]{1,0:T(8,128)(2,1)S(1)} %bitcast.21), kind=kOutput, calls=%fused_computation.4 | convolution fusion | flops 1286471680 | bytes 7479296 | tf_op jit(solution)/shard_map/dot_general | solution.py:103
  129.9 3.0 %fusion.13 = f32[752,1664]{1,0:T(8,128)S(1)} fusion(bf16[512,1664]{1,0:T(8,128)(2,1)} %collective-permute-done.10, bf16[752,4096]{1,0:T(8,128)(2,1)S(1)} %bitcast.22), kind=kOutput, calls=%fused_computation.23 | convolution fusion | flops 1281359872 | bytes 7479296 | tf_op jit(solution)/shard_map/dot_general | solution.py:103
  132.9 7.2 %add_add_fusion.1 = f32[752,1664]{1,0:T(8,128)} fusion(f32[752,1664]{1,0:T(8,128)S(1)} %fusion.13, f32[752,1664]{1,0:T(8,128)S(1)} %fusion.15, f32[752,1664]{1,0:T(8,128)} %fusion, f32[752,1664]{1,0:T(8,128)S(1)} %fusion.17, bf16[512,1664]{1,0:T(8,128)(2,1)} %collective-permute-done.11, bf16[752,4096]{1,0:T(8,128)(2,1)S(1)} %bitcast.23), kind=kOutput, calls=%fused_computation.1 | convolution fusion | flops 1286365184 | bytes 27500544 | tf_op jit(solution)/shard_map/dot_general | solution.py:103
  140.1 12.5 %collective-permute-done.17 = bf16[512,1664]{1,0:T(8,128)(2,1)} collective-permute-done((bf16[512,1664]{1,0:T(8,128)(2,1)}, bf16[512,1664]{1,0:T(8,128)(2,1)}, u32[]{:S(2)}, u32[]{:S(2)}) %collective-permute-start.17) | collective-permute-done | bytes 1703968 | tf_op jit(solution)/shard_map/ppermute | solution.py:89
  152.6 3.2 %fusion.7 = f32[752,1664]{1,0:T(8,128)S(1)} fusion(bf16[512,1664]{1,0:T(8,128)(2,1)} %collective-permute-done.17, bf16[752,4096]{1,0:T(8,128)(2,1)S(1)} %bitcast.24), kind=kOutput, calls=%fused_computation.19 | convolution fusion | flops 1281359872 | bytes 7479296 | tf_op jit(solution)/shard_map/dot_general | solution.py:103
  158.0 3.0 %collective-permute-start.22 = (bf16[256,1024]{1,0:T(8,128)(2,1)S(1)}, bf16[256,1024]{1,0:T(8,128)(2,1)S(1)}, u32[]{:S(2)}, u32[]{:S(2)}) collective-permute-start(bf16[256,1024]{1,0:T(8,128)(2,1)S(1)} %slice.130), channel_id=1, source_target_pairs={{0,112},{16,0},{32,16},{48,32},{64,48},{80,64},{96,80},{112,96},{1... | collective-permute-start | bytes 1572872 | tf_op jit(solution)/shard_map/ppermute | solution.py:89
  160.9 3.2 %add_add_fusion = f32[752,1664]{1,0:T(8,128)S(1)} fusion(f32[752,1664]{1,0:T(8,128)S(1)} %copy-done.2, f32[752,1664]{1,0:T(8,128)S(1)} %fusion.7, bf16[512,1664]{1,0:T(8,128)(2,1)} %collective-permute-done.18, bf16[752,4096]{1,0:T(8,128)(2,1)S(1)} %bitcast.25), kind=kOutput, calls=%fused_computation | convolution fusion | flops 1283862528 | bytes 17489920 | tf_op jit(solution)/shard_map/dot_general | solution.py:103
  164.1 6.6 %collective-permute-done.21 = bf16[256,1024]{1,0:T(8,128)(2,1)S(1)} collective-permute-done((bf16[256,1024]{1,0:T(8,128)(2,1)S(1)}, bf16[256,1024]{1,0:T(8,128)(2,1)S(1)}, u32[]{:S(2)}, u32[]{:S(2)}) %collective-permute-start.21) | collective-permute-done | bytes 524320 | tf_op jit(solution)/shard_map/ppermute | solution.py:89
  181.1 7.3 %collective-permute-done.19 = bf16[256,640]{1,0:T(8,128)(2,1)S(1)} collective-permute-done((bf16[256,640]{1,0:T(8,128)(2,1)S(1)}, bf16[256,640]{1,0:T(8,128)(2,1)S(1)}, u32[]{:S(2)}, u32[]{:S(2)}) %collective-permute-start.19) | collective-permute-done | bytes 327712 | tf_op jit(solution)/shard_map/ppermute | solution.py:89
  195.1 9.6 %collective-permute-done.24 = bf16[376,1024]{1,0:T(8,128)(2,1)S(1)} collective-permute-done((bf16[376,1024]{1,0:T(8,128)(2,1)S(1)}, bf16[376,1024]{1,0:T(8,128)(2,1)S(1)}, u32[]{:S(2)}, u32[]{:S(2)}) %collective-permute-start.24) | collective-permute-done | bytes 770080 | tf_op jit(solution)/shard_map/ppermute | solution.py:125
  204.8 5.2 %collective-permute-done.26 = bf16[376,640]{1,0:T(8,128)(2,1)S(1)} collective-permute-done((bf16[376,640]{1,0:T(8,128)(2,1)S(1)}, bf16[376,640]{1,0:T(8,128)(2,1)S(1)}, u32[]{:S(2)}, u32[]{:S(2)}) %collective-permute-start.26) | collective-permute-done | bytes 481312 | tf_op jit(solution)/shard_map/ppermute | solution.py:125
  (89 shorter events, 58.8 us)
Async XLA Ops:
  1.2 8.4 %collective-permute-start = (bf16[256,768]{1,0:T(8,128)(2,1)S(1)}, bf16[256,768]{1,0:T(8,128)(2,1)S(1)}, u32[]{:S(2)}, u32[]{:S(2)}) collective-permute-start(bf16[256,768]{1,0:T(8,128)(2,1)S(1)} %get-tuple-element.67), channel_id=1, source_target_pairs={{0,1},{1,129},{128,0},{129,128},{2,3},{3,131},{130,2},{131,130},{4... | collective-permute-start | bytes 1179656 | tf_op jit(solution)/shard_map/ppermute | solution.py:112
  4.8 12.5 %collective-permute-start.1 = (bf16[256,768]{1,0:T(8,128)(2,1)S(1)}, bf16[256,768]{1,0:T(8,128)(2,1)S(1)}, u32[]{:S(2)}, u32[]{:S(2)}) collective-permute-start(bf16[256,768]{1,0:T(8,128)(2,1)S(1)} %get-tuple-element.68), channel_id=1, source_target_pairs={{0,0},{1,128},{128,1},{129,129},{2,2},{3,130},{130,3},{131,131},{4... | collective-permute-start | bytes 1179656 | tf_op jit(solution)/shard_map/ppermute | solution.py:111
  17.6 21.5 %collective-permute-start.4 = (bf16[512,768]{1,0:T(8,128)(2,1)S(1)}, bf16[512,768]{1,0:T(8,128)(2,1)S(1)}, u32[]{:S(2)}, u32[]{:S(2)}) collective-permute-start(bf16[512,768]{1,0:T(8,128)(2,1)S(1)} %pad_maximum_fusion.3), channel_id=1, source_target_pairs={{0,16},{16,32},{32,48},{48,64},{64,80},{80,96},{96,112},{112,0},{1... | collective-permute-start | bytes 2359304 | tf_op jit(solution)/shard_map/ppermute | solution.py:89
  17.7 21.4 %collective-permute-start.5 = (bf16[512,768]{1,0:T(8,128)(2,1)S(1)}, bf16[512,768]{1,0:T(8,128)(2,1)S(1)}, u32[]{:S(2)}, u32[]{:S(2)}) collective-permute-start(bf16[512,768]{1,0:T(8,128)(2,1)S(1)} %pad_maximum_fusion.3), channel_id=1, source_target_pairs={{0,112},{16,0},{32,16},{48,32},{64,48},{80,64},{96,80},{112,96},{1... | collective-permute-start | bytes 2359304 | tf_op jit(solution)/shard_map/ppermute | solution.py:89
  21.7 10.0 %collective-permute-start.3 = (bf16[376,512]{1,0:T(8,128)(2,1)S(1)}, bf16[376,512]{1,0:T(8,128)(2,1)S(1)}, u32[]{:S(2)}, u32[]{:S(2)}) collective-permute-start(bf16[376,512]{1,0:T(8,128)(2,1)S(1)} %pad_maximum_fusion.5), channel_id=1, source_target_pairs={{0,8},{8,0},{1,9},{9,1},{2,10},{10,2},{3,11},{11,3},{4,12},{12,4},... | collective-permute-start | bytes 1155080 | tf_op jit(solution)/shard_map/ppermute | solution.py:19
  23.1 18.5 %collective-permute-start.6 = (bf16[256,896]{1,0:T(8,128)(2,1)S(1)}, bf16[256,896]{1,0:T(8,128)(2,1)S(1)}, u32[]{:S(2)}, u32[]{:S(2)}) collective-permute-start(bf16[256,896]{1,0:T(8,128)(2,1)S(1)} %get-tuple-element.71), channel_id=1, source_target_pairs={{0,1},{1,129},{128,0},{129,128},{2,3},{3,131},{130,2},{131,130},{4... | collective-permute-start | bytes 1376264 | tf_op jit(solution)/shard_map/ppermute | solution.py:112
  25.0 19.6 %collective-permute-start.7 = (bf16[256,896]{1,0:T(8,128)(2,1)S(1)}, bf16[256,896]{1,0:T(8,128)(2,1)S(1)}, u32[]{:S(2)}, u32[]{:S(2)}) collective-permute-start(bf16[256,896]{1,0:T(8,128)(2,1)S(1)} %get-tuple-element.72), channel_id=1, source_target_pairs={{0,0},{1,128},{128,1},{129,129},{2,2},{3,130},{130,3},{131,131},{4... | collective-permute-start | bytes 1376264 | tf_op jit(solution)/shard_map/ppermute | solution.py:111
  39.1 20.8 %collective-permute-start.12 = (bf16[376,1024]{1,0:T(8,128)(2,1)S(1)}, bf16[376,1024]{1,0:T(8,128)(2,1)S(1)}, u32[]{:S(2)}, u32[]{:S(2)}) collective-permute-start(bf16[376,1024]{1,0:T(8,128)(2,1)S(1)} %pad_maximum_fusion.4), channel_id=1, source_target_pairs={{0,128},{128,0},{1,129},{129,1},{2,130},{130,2},{3,131},{131,3},{4... | collective-permute-start | bytes 2310152 | tf_op jit(solution)/shard_map/ppermute | solution.py:19
  44.8 22.0 %collective-permute-start.8 = (bf16[512,896]{1,0:T(8,128)(2,1)S(1)}, bf16[512,896]{1,0:T(8,128)(2,1)S(1)}, u32[]{:S(2)}, u32[]{:S(2)}) collective-permute-start(bf16[512,896]{1,0:T(8,128)(2,1)S(1)} %pad_maximum_fusion.2), channel_id=1, source_target_pairs={{0,16},{16,32},{32,48},{48,64},{64,80},{80,96},{96,112},{112,0},{1... | collective-permute-start | bytes 2752520 | tf_op jit(solution)/shard_map/ppermute | solution.py:89
  44.9 21.9 %collective-permute-start.9 = (bf16[512,896]{1,0:T(8,128)(2,1)S(1)}, bf16[512,896]{1,0:T(8,128)(2,1)S(1)}, u32[]{:S(2)}, u32[]{:S(2)}) collective-permute-start(bf16[512,896]{1,0:T(8,128)(2,1)S(1)} %pad_maximum_fusion.2), channel_id=1, source_target_pairs={{0,112},{16,0},{32,16},{48,32},{64,48},{80,64},{96,80},{112,96},{1... | collective-permute-start | bytes 2752520 | tf_op jit(solution)/shard_map/ppermute | solution.py:89
  60.0 35.5 %collective-permute-start.13 = (bf16[2,376,1024]{2,1,0:T(8,128)(2,1)S(1)}, bf16[2,376,1024]{2,1,0:T(8,128)(2,1)S(1)}, u32[]{:S(2)}, u32[]{:S(2)}) collective-permute-start(bf16[2,376,1024]{2,1,0:T(8,128)(2,1)S(1)} %pad_maximum_fusion.here), channel_id=1, source_target_pairs={{0,2},{2,4},{4,6},{6,0},{1,3},{3,5},{5,7},{7,1},{8,10},{10,12},{12... | collective-permute-start | bytes 4620296 | tf_op jit(solution)/shard_map/ppermute | solution.py:44
  61.4 35.1 %collective-permute-start.14 = (bf16[2,376,1024]{2,1,0:T(8,128)(2,1)S(1)}, bf16[2,376,1024]{2,1,0:T(8,128)(2,1)S(1)}, u32[]{:S(2)}, u32[]{:S(2)}) collective-permute-start(bf16[2,376,1024]{2,1,0:T(8,128)(2,1)S(1)} %pad_maximum_fusion.here), channel_id=1, source_target_pairs={{0,6},{2,0},{4,2},{6,4},{1,7},{3,1},{5,3},{7,5},{8,14},{10,8},{12,... | collective-permute-start | bytes 4620296 | tf_op jit(solution)/shard_map/ppermute | solution.py:44
  67.8 39.7 %collective-permute-start.11 = (bf16[512,1664]{1,0:T(8,128)(2,1)}, bf16[512,1664]{1,0:T(8,128)(2,1)}, u32[]{:S(2)}, u32[]{:S(2)}) collective-permute-start(bf16[512,1664]{1,0:T(8,128)(2,1)} %constant_dynamic-update-slice_fusion.2), channel_id=1, source_target_pairs={{0,112},{16,0},{32,16},{48,32},{64,48},{80,64},{96,80},{112,96},{1... | collective-permute-start | bytes 5111816 | tf_op jit(solution)/shard_map/ppermute | solution.py:89
  71.8 40.4 %collective-permute-start.10 = (bf16[512,1664]{1,0:T(8,128)(2,1)}, bf16[512,1664]{1,0:T(8,128)(2,1)}, u32[]{:S(2)}, u32[]{:S(2)}) collective-permute-start(bf16[512,1664]{1,0:T(8,128)(2,1)} %constant_dynamic-update-slice_fusion), channel_id=1, source_target_pairs={{0,16},{16,32},{32,48},{48,64},{64,80},{80,96},{96,112},{112,0},{1... | collective-permute-start | bytes 5111816 | tf_op jit(solution)/shard_map/ppermute | solution.py:89
  96.5 18.5 %collective-permute-start.15 = (bf16[376,1024]{1,0:T(8,128)(2,1)}, bf16[376,1024]{1,0:T(8,128)(2,1)}, u32[]{:S(2)}, u32[]{:S(2)}) collective-permute-start(bf16[376,1024]{1,0:T(8,128)(2,1)} %slice_bitcast_fusion.1), channel_id=1, source_target_pairs={{0,2},{2,4},{4,6},{6,0},{1,3},{3,5},{5,7},{7,1},{8,10},{10,12},{12... | collective-permute-start | bytes 2310152 | tf_op jit(solution)/shard_map/ppermute | solution.py:44
  98.6 17.3 %collective-permute-start.16 = (bf16[376,1024]{1,0:T(8,128)(2,1)}, bf16[376,1024]{1,0:T(8,128)(2,1)}, u32[]{:S(2)}, u32[]{:S(2)}) collective-permute-start(bf16[376,1024]{1,0:T(8,128)(2,1)} %slice_bitcast_fusion), channel_id=1, source_target_pairs={{0,6},{2,0},{4,2},{6,4},{1,7},{3,1},{5,3},{7,5},{8,14},{10,8},{12,... | collective-permute-start | bytes 2310152 | tf_op jit(solution)/shard_map/ppermute | solution.py:44
  112.3 40.3 %collective-permute-start.17 = (bf16[512,1664]{1,0:T(8,128)(2,1)}, bf16[512,1664]{1,0:T(8,128)(2,1)}, u32[]{:S(2)}, u32[]{:S(2)}) collective-permute-start(bf16[512,1664]{1,0:T(8,128)(2,1)} %collective-permute-done.10), channel_id=1, source_target_pairs={{0,16},{16,32},{32,48},{48,64},{64,80},{80,96},{96,112},{112,0},{1... | collective-permute-start | bytes 5111816 | tf_op jit(solution)/shard_map/ppermute | solution.py:89
  112.3 40.3 %collective-permute-start.18 = (bf16[512,1664]{1,0:T(8,128)(2,1)}, bf16[512,1664]{1,0:T(8,128)(2,1)}, u32[]{:S(2)}, u32[]{:S(2)}) collective-permute-start(bf16[512,1664]{1,0:T(8,128)(2,1)} %collective-permute-done.11), channel_id=1, source_target_pairs={{0,112},{16,0},{32,16},{48,32},{64,48},{80,64},{96,80},{112,96},{1... | collective-permute-start | bytes 5111816 | tf_op jit(solution)/shard_map/ppermute | solution.py:89
  156.8 13.9 %collective-permute-start.21 = (bf16[256,1024]{1,0:T(8,128)(2,1)S(1)}, bf16[256,1024]{1,0:T(8,128)(2,1)S(1)}, u32[]{:S(2)}, u32[]{:S(2)}) collective-permute-start(bf16[256,1024]{1,0:T(8,128)(2,1)S(1)} %slice.129), channel_id=1, source_target_pairs={{0,16},{16,32},{32,48},{48,64},{64,80},{80,96},{96,112},{112,0},{1... | collective-permute-start | bytes 1572872 | tf_op jit(solution)/shard_map/ppermute | solution.py:89
  158.0 13.7 %collective-permute-start.22 = (bf16[256,1024]{1,0:T(8,128)(2,1)S(1)}, bf16[256,1024]{1,0:T(8,128)(2,1)S(1)}, u32[]{:S(2)}, u32[]{:S(2)}) collective-permute-start(bf16[256,1024]{1,0:T(8,128)(2,1)S(1)} %slice.130), channel_id=1, source_target_pairs={{0,112},{16,0},{32,16},{48,32},{64,48},{80,64},{96,80},{112,96},{1... | collective-permute-start | bytes 1572872 | tf_op jit(solution)/shard_map/ppermute | solution.py:89
  176.9 11.4 %collective-permute-start.19 = (bf16[256,640]{1,0:T(8,128)(2,1)S(1)}, bf16[256,640]{1,0:T(8,128)(2,1)S(1)}, u32[]{:S(2)}, u32[]{:S(2)}) collective-permute-start(bf16[256,640]{1,0:T(8,128)(2,1)S(1)} %slice.127), channel_id=1, source_target_pairs={{0,16},{16,32},{32,48},{48,64},{64,80},{80,96},{96,112},{112,0},{1... | collective-permute-start | bytes 983048 | tf_op jit(solution)/shard_map/ppermute | solution.py:89
  179.4 9.0 %collective-permute-start.20 = (bf16[256,640]{1,0:T(8,128)(2,1)S(1)}, bf16[256,640]{1,0:T(8,128)(2,1)S(1)}, u32[]{:S(2)}, u32[]{:S(2)}) collective-permute-start(bf16[256,640]{1,0:T(8,128)(2,1)S(1)} %slice.128), channel_id=1, source_target_pairs={{0,112},{16,0},{32,16},{48,32},{64,48},{80,64},{96,80},{112,96},{1... | collective-permute-start | bytes 983048 | tf_op jit(solution)/shard_map/ppermute | solution.py:89
  190.7 14.1 %collective-permute-start.24 = (bf16[376,1024]{1,0:T(8,128)(2,1)S(1)}, bf16[376,1024]{1,0:T(8,128)(2,1)S(1)}, u32[]{:S(2)}, u32[]{:S(2)}) collective-permute-start(bf16[376,1024]{1,0:T(8,128)(2,1)S(1)} %multiply_convert_fusion), channel_id=1, source_target_pairs={{0,0},{1,128},{128,129},{129,1},{2,2},{3,130},{130,131},{131,3},{4... | collective-permute-start | bytes 2310152 | tf_op jit(solution)/shard_map/ppermute | solution.py:125
  193.2 16.7 %collective-permute-start.26 = (bf16[376,640]{1,0:T(8,128)(2,1)S(1)}, bf16[376,640]{1,0:T(8,128)(2,1)S(1)}, u32[]{:S(2)}, u32[]{:S(2)}) collective-permute-start(bf16[376,640]{1,0:T(8,128)(2,1)S(1)} %multiply_convert_fusion.1), channel_id=1, source_target_pairs={{0,0},{1,128},{128,129},{129,1},{2,2},{3,130},{130,131},{131,3},{4... | collective-permute-start | bytes 1443848 | tf_op jit(solution)/shard_map/ppermute | solution.py:125
  (12 other events, 72.9 us)

commit v8 on v7

--- a/solution.py
+++ b/solution.py
@@ -89,10 +89,7 @@
     return lax.ppermute(value, "z", [(i, (i + shift) % 8) for i in range(8)])
 
 
-def step_along_z(step, up, down):
-    if step == 4:
-        half = up.shape[0] // 2
-        up, down = up[:half], down[half:]
+def step_along_z(up, down):
     return along_z(up, 1), along_z(down, -1)
 
 
@@ -128,10 +125,10 @@
 def on_device(tokens, weight):
     half = weight.shape[0] // 2
     mine, tokens = together(swapped(weight[:, :FIRST]), tokens)
-    up, down = together(*step_along_z(1, mine, mine))
+    up, down = together(*step_along_z(mine, mine))
     near, rest = together(tokens_of_core(tokens), weight[:, FIRST:])
     rest = swapped(rest)
-    rest_up, rest_down = together(*step_along_z(1, rest, rest))
+    rest_up, rest_down = together(*step_along_z(rest, rest))
     piece, up, down = together(tokens_of_pair(near), up, down)
     beside = exchange(piece, "xh", 1, 2)
     both = jnp.stack([piece, beside])
@@ -141,23 +138,27 @@
     down = jnp.concatenate([down, rest_down], axis=1)
     blocks = [(0, mine), (2, up), (14, down)]
     for step in range(2, 4):
-        up, down = together(*step_along_z(step, up, down))
+        up, down = together(*step_along_z(up, down))
         if step == 2:
             tied_up, tied_down, *pieces = together(up, down, *pieces)
             blocks += [(2 * step, tied_up), (2 * (8 - step), tied_down)]
     gathered = order_tokens(pieces)
     early = product(gathered, blocks[:5], half)
     early, up, down = together(early, up, down)
-    early += product(gathered, [(6, up), (10, down)], half)
-    ends = [
-        step_along_z(4, up[:, columns], down[:, columns])
+    quarter = slice(0, half), slice(half, None)
+    sent = [
+        (up[quarter[0], columns], down[quarter[1], columns])
         for columns in (slice(0, LAST), slice(LAST, None))
     ]
+    (*sent[0], up, down) = together(*sent[0], up, down)
+    early += product(gathered, [(6, up), (10, down)], half)
+    ends = [step_along_z(*pair) for pair in sent]
     up, down, early = together(*ends[0], early)
-    first = activate(early[:, :LAST] + product(gathered, ((8, up), (9, down)), half))
-    up, down, first = together(*ends[1], first)
+    total = early[:, :LAST] + product(gathered, ((8, up), (9, down)), half)
+    total, up, down = together(total, *ends[1])
+    first = home(activate(total))
     second = activate(early[:, LAST:] + product(gathered, ((8, up), (9, down)), half))
-    return jnp.concatenate([home(first), home(second)], axis=1)
+    return jnp.concatenate([first, home(second)], axis=1)
 
 
 def solution(mesh):

time: 212 us -> 208 us (0.981)
    ppermute x12, waiting for transfers between devices: 47.6 us -> 43.7 us  [along_z(): return lax.ppermute(value, 'z', [(i, (i + shift) % 8) for i in range(8)])]
    unnamed x18 -> x20, local copies, waits for them, and re-layouts: 4.55 us -> 4.57 us
  transfers between devices with their start and end apart: 27 -> 27, of which waited for: 18 -> 15; matrix products, arithmetic and copies ran while one was open for 16% -> 16% of each run, Pallas kernels for 1% -> 1%
where the time goes in v8:
time: 208 us; the launch traced here: 207 us
  waiting for transfers between devices  111 us (53%)
  starting transfers between devices  47.4 us (23%)
  matrix products  28.7 us (14%)
  local copies, waits for them, and re-layouts  13.1 us (6%)
  other arithmetic  4.45 us (2%)
  Pallas kernels  2.63 us (1%)
    ppermute x12, waiting for transfers between devices, along_z(): return lax.ppermute(value, 'z', [(i, (i + shift) % 8) for i in range(8)])  43.7 us
    dot_general x11, matrix products, product(): total += jnp.dot(features, piece, preferred_element_type=jnp.float32)  28.7 us
    ppermute x4, waiting for transfers between devices, along_y(): return lax.ppermute(value, 'y', [(i, (i + shift) % 4) for i in range(4)])  24.5 us
    ppermute x12, starting transfers between devices, along_z(): return lax.ppermute(value, 'z', [(i, (i + shift) % 8) for i in range(8)])  17.8 us
    ppermute x5, waiting for transfers between devices, exchange(): return lax.ppermute(value, axis, [(i, i ^ flip) for i in range(size)])  16.5 us
    ppermute x2, waiting for transfers between devices, home(): return lax.ppermute(out, ('xh', 'core'), HOME)  15 us
    ppermute x2, waiting for transfers between devices, swapped(): turned = lax.ppermute(first, ('xh', 'core'), TURN)  10.8 us
    ppermute x2, starting transfers between devices, swapped(): turned = lax.ppermute(first, ('xh', 'core'), TURN)  8.8 us
  transfers between devices with their start and end apart: 27, of which 15 were waited for; matrix products, arithmetic and copies ran while one was open for 16% of the time, Pallas kernels for 1%

profile of v8, /device:TPU:1, one launch (start us, length us, event | category | flops | bytes accessed | tf_op | source)
XLA Modules:
  0.0 207.3 jit_solution(12647579768998244260)
XLA Ops:
  1.2 3.7 %collective-permute-start = (bf16[256,768]{1,0:T(8,128)(2,1)S(1)}, bf16[256,768]{1,0:T(8,128)(2,1)S(1)}, u32[]{:S(2)}, u32[]{:S(2)}) collective-permute-start(bf16[256,768]{1,0:T(8,128)(2,1)S(1)} %get-tuple-element.75), channel_id=1, source_target_pairs={{0,1},{1,129},{128,0},{129,128},{2,3},{3,131},{130,2},{131,130},{4... | collective-permute-start | bytes 1179656 | tf_op jit(solution)/shard_map/ppermute | solution.py:109
  4.8 4.7 %collective-permute-start.1 = (bf16[256,768]{1,0:T(8,128)(2,1)S(1)}, bf16[256,768]{1,0:T(8,128)(2,1)S(1)}, u32[]{:S(2)}, u32[]{:S(2)}) collective-permute-start(bf16[256,768]{1,0:T(8,128)(2,1)S(1)} %get-tuple-element.76), channel_id=1, source_target_pairs={{0,0},{1,128},{128,1},{129,129},{2,2},{3,130},{130,3},{131,131},{4... | collective-permute-start | bytes 1179656 | tf_op jit(solution)/shard_map/ppermute | solution.py:108
  9.6 7.7 %collective-permute-done.1 = bf16[256,768]{1,0:T(8,128)(2,1)S(1)} collective-permute-done((bf16[256,768]{1,0:T(8,128)(2,1)S(1)}, bf16[256,768]{1,0:T(8,128)(2,1)S(1)}, u32[]{:S(2)}, u32[]{:S(2)}) %collective-permute-start.1) | collective-permute-done | bytes 393248 | tf_op jit(solution)/shard_map/ppermute | solution.py:108
  17.7 3.9 %collective-permute-start.5 = (bf16[512,768]{1,0:T(8,128)(2,1)S(1)}, bf16[512,768]{1,0:T(8,128)(2,1)S(1)}, u32[]{:S(2)}, u32[]{:S(2)}) collective-permute-start(bf16[512,768]{1,0:T(8,128)(2,1)S(1)} %pad_maximum_fusion.3), channel_id=1, source_target_pairs={{0,112},{16,0},{32,16},{48,32},{64,48},{80,64},{96,80},{112,96},{1... | collective-permute-start | bytes 2359304 | tf_op jit(solution)/shard_map/ppermute | solution.py:89
  25.0 4.1 %collective-permute-start.7 = (bf16[256,896]{1,0:T(8,128)(2,1)S(1)}, bf16[256,896]{1,0:T(8,128)(2,1)S(1)}, u32[]{:S(2)}, u32[]{:S(2)}) collective-permute-start(bf16[256,896]{1,0:T(8,128)(2,1)S(1)} %get-tuple-element.80), channel_id=1, source_target_pairs={{0,0},{1,128},{128,1},{129,129},{2,2},{3,130},{130,3},{131,131},{4... | collective-permute-start | bytes 1376264 | tf_op jit(solution)/shard_map/ppermute | solution.py:108
  31.8 7.3 %collective-permute-done.4 = bf16[512,768]{1,0:T(8,128)(2,1)S(1)} collective-permute-done((bf16[512,768]{1,0:T(8,128)(2,1)S(1)}, bf16[512,768]{1,0:T(8,128)(2,1)S(1)}, u32[]{:S(2)}, u32[]{:S(2)}) %collective-permute-start.4) | collective-permute-done | bytes 786464 | tf_op jit(solution)/shard_map/ppermute | solution.py:89
  41.6 3.1 %collective-permute-done.7 = bf16[256,896]{1,0:T(8,128)(2,1)S(1)} collective-permute-done((bf16[256,896]{1,0:T(8,128)(2,1)S(1)}, bf16[256,896]{1,0:T(8,128)(2,1)S(1)}, u32[]{:S(2)}, u32[]{:S(2)}) %collective-permute-start.7) | collective-permute-done | bytes 458784 | tf_op jit(solution)/shard_map/ppermute | solution.py:108
  47.6 12.3 %collective-permute-done.12 = bf16[376,1024]{1,0:T(8,128)(2,1)S(1)} collective-permute-done((bf16[376,1024]{1,0:T(8,128)(2,1)S(1)}, bf16[376,1024]{1,0:T(8,128)(2,1)S(1)}, u32[]{:S(2)}, u32[]{:S(2)}) %collective-permute-start.12) | collective-permute-done | bytes 770080 | tf_op jit(solution)/shard_map/ppermute | solution.py:19
  67.9 3.0 %collective-permute-start.11 = (bf16[512,1664]{1,0:T(8,128)(2,1)}, bf16[512,1664]{1,0:T(8,128)(2,1)}, u32[]{:S(2)}, u32[]{:S(2)}) collective-permute-start(bf16[512,1664]{1,0:T(8,128)(2,1)} %constant_dynamic-update-slice_fusion.2), channel_id=1, source_target_pairs={{0,112},{16,0},{32,16},{48,32},{64,48},{80,64},{96,80},{112,96},{1... | collective-permute-start | bytes 5111816 | tf_op jit(solution)/shard_map/ppermute | solution.py:89
  71.9 23.7 %collective-permute-done.13.up = bf16[2,376,1024]{2,1,0:T(8,128)(2,1)S(1)} collective-permute-done((bf16[2,376,1024]{2,1,0:T(8,128)(2,1)S(1)}, bf16[2,376,1024]{2,1,0:T(8,128)(2,1)S(1)}, u32[]{:S(2)}, u32[]{:S(2)}) %collective-permute-start.13) | collective-permute-done | bytes 1540128 | tf_op jit(solution)/shard_map/ppermute | solution.py:44
  101.3 6.3 %collective-permute-done.11 = bf16[512,1664]{1,0:T(8,128)(2,1)} collective-permute-done((bf16[512,1664]{1,0:T(8,128)(2,1)}, bf16[512,1664]{1,0:T(8,128)(2,1)}, u32[]{:S(2)}, u32[]{:S(2)}) %collective-permute-start.11) | collective-permute-done | bytes 1703968 | tf_op jit(solution)/shard_map/ppermute | solution.py:89
  107.6 4.7 %collective-permute-done.10 = bf16[512,1664]{1,0:T(8,128)(2,1)} collective-permute-done((bf16[512,1664]{1,0:T(8,128)(2,1)}, bf16[512,1664]{1,0:T(8,128)(2,1)}, u32[]{:S(2)}, u32[]{:S(2)}) %collective-permute-start.10) | collective-permute-done | bytes 1703968 | tf_op jit(solution)/shard_map/ppermute | solution.py:89
  112.3 2.7 %collective-permute-start.18 = (bf16[512,1664]{1,0:T(8,128)(2,1)}, bf16[512,1664]{1,0:T(8,128)(2,1)}, u32[]{:S(2)}, u32[]{:S(2)}) collective-permute-start(bf16[512,1664]{1,0:T(8,128)(2,1)} %collective-permute-done.11), channel_id=1, source_target_pairs={{0,112},{16,0},{32,16},{48,32},{64,48},{80,64},{96,80},{112,96},{1... | collective-permute-start | bytes 5111816 | tf_op jit(solution)/shard_map/ppermute | solution.py:89
  119.9 3.0 %fusion.17 = f32[752,1664]{1,0:T(8,128)S(1)} fusion(bf16[512,1664]{1,0:T(8,128)(2,1)} %constant_dynamic-update-slice_fusion, bf16[752,4096]{1,0:T(8,128)(2,1)S(1)} %bitcast.19), kind=kOutput, calls=%fused_computation.27 | convolution fusion | flops 1281359872 | bytes 7479296 | tf_op jit(solution)/shard_map/dot_general | solution.py:100
  122.9 3.1 %fusion.15 = f32[752,1664]{1,0:T(8,128)S(1)} fusion(bf16[512,1664]{1,0:T(8,128)(2,1)} %constant_dynamic-update-slice_fusion.2, bf16[752,4096]{1,0:T(8,128)(2,1)S(1)} %bitcast.20), kind=kOutput, calls=%fused_computation.25 | convolution fusion | flops 1281359872 | bytes 7479296 | tf_op jit(solution)/shard_map/dot_general | solution.py:100
  126.0 3.8 %fusion = f32[752,1664]{1,0:T(8,128)} fusion(bf16[256,896]{1,0:T(8,128)(2,1)S(1)} %copy-done.3, bf16[256,896]{1,0:T(8,128)(2,1)S(1)} %get-tuple-element.77, bf16[512,768]{1,0:T(8,128)(2,1)S(1)} %copy-done.6, bf16[752,4096]{1,0:T(8,128)(2,1)S(1)} %bitcast.21), kind=kOutput, calls=%fused_computation.4 | convolution fusion | flops 1286471680 | bytes 7479296 | tf_op jit(solution)/shard_map/dot_general | solution.py:100
  129.9 3.0 %fusion.13 = f32[752,1664]{1,0:T(8,128)S(1)} fusion(bf16[512,1664]{1,0:T(8,128)(2,1)} %collective-permute-done.10, bf16[752,4096]{1,0:T(8,128)(2,1)S(1)} %bitcast.22), kind=kOutput, calls=%fused_computation.23 | convolution fusion | flops 1281359872 | bytes 7479296 | tf_op jit(solution)/shard_map/dot_general | solution.py:100
  132.9 7.2 %add_add_fusion.1 = f32[752,1664]{1,0:T(8,128)} fusion(f32[752,1664]{1,0:T(8,128)S(1)} %fusion.13, f32[752,1664]{1,0:T(8,128)S(1)} %fusion.15, f32[752,1664]{1,0:T(8,128)} %fusion, f32[752,1664]{1,0:T(8,128)S(1)} %fusion.17, bf16[512,1664]{1,0:T(8,128)(2,1)} %collective-permute-done.11, bf16[752,4096]{1,0:T(8,128)(2,1)S(1)} %bitcast.23), kind=kOutput, calls=%fused_computation.1 | convolution fusion | flops 1286365184 | bytes 27500544 | tf_op jit(solution)/shard_map/dot_general | solution.py:100
  140.1 12.5 %collective-permute-done.17 = bf16[512,1664]{1,0:T(8,128)(2,1)} collective-permute-done((bf16[512,1664]{1,0:T(8,128)(2,1)}, bf16[512,1664]{1,0:T(8,128)(2,1)}, u32[]{:S(2)}, u32[]{:S(2)}) %collective-permute-start.17) | collective-permute-done | bytes 1703968 | tf_op jit(solution)/shard_map/ppermute | solution.py:89
  157.1 3.1 %fusion.7 = f32[752,1664]{1,0:T(8,128)S(1)} fusion(bf16[512,1664]{1,0:T(8,128)(2,1)} %collective-permute-done.17, bf16[752,4096]{1,0:T(8,128)(2,1)S(1)} %bitcast.24), kind=kOutput, calls=%fused_computation.19 | convolution fusion | flops 1281359872 | bytes 7479296 | tf_op jit(solution)/shard_map/dot_general | solution.py:100
  165.7 3.2 %add_add_fusion = f32[752,1664]{1,0:T(8,128)S(1)} fusion(f32[752,1664]{1,0:T(8,128)S(1)} %bitcast.31, f32[752,1664]{1,0:T(8,128)S(1)} %fusion.7, bf16[512,1664]{1,0:T(8,128)(2,1)} %collective-permute-done.18, bf16[752,4096]{1,0:T(8,128)(2,1)S(1)} %bitcast.25), kind=kOutput, calls=%fused_computation | convolution fusion | flops 1283862528 | bytes 17489920 | tf_op jit(solution)/shard_map/dot_general | solution.py:100
  168.8 5.3 %collective-permute-done.19 = bf16[256,1024]{1,0:T(8,128)(2,1)S(1)} collective-permute-done((bf16[256,1024]{1,0:T(8,128)(2,1)S(1)}, bf16[256,1024]{1,0:T(8,128)(2,1)S(1)}, u32[]{:S(2)}, u32[]{:S(2)}) %collective-permute-start.19) | collective-permute-done | bytes 524320 | tf_op jit(solution)/shard_map/ppermute | solution.py:89
  175.3 5.8 %collective-permute-done.21 = bf16[256,640]{1,0:T(8,128)(2,1)S(1)} collective-permute-done((bf16[256,640]{1,0:T(8,128)(2,1)S(1)}, bf16[256,640]{1,0:T(8,128)(2,1)S(1)}, u32[]{:S(2)}, u32[]{:S(2)}) %collective-permute-start.21) | collective-permute-done | bytes 327712 | tf_op jit(solution)/shard_map/ppermute | solution.py:89
  191.1 15.0 %collective-permute-done.26 = bf16[376,640]{1,0:T(8,128)(2,1)S(1)} collective-permute-done((bf16[376,640]{1,0:T(8,128)(2,1)S(1)}, bf16[376,640]{1,0:T(8,128)(2,1)S(1)}, u32[]{:S(2)}, u32[]{:S(2)}) %collective-permute-start.26) | collective-permute-done | bytes 481312 | tf_op jit(solution)/shard_map/ppermute | solution.py:122
  (92 shorter events, 54.9 us)
Async XLA Ops:
  1.2 8.4 %collective-permute-start = (bf16[256,768]{1,0:T(8,128)(2,1)S(1)}, bf16[256,768]{1,0:T(8,128)(2,1)S(1)}, u32[]{:S(2)}, u32[]{:S(2)}) collective-permute-start(bf16[256,768]{1,0:T(8,128)(2,1)S(1)} %get-tuple-element.75), channel_id=1, source_target_pairs={{0,1},{1,129},{128,0},{129,128},{2,3},{3,131},{130,2},{131,130},{4... | collective-permute-start | bytes 1179656 | tf_op jit(solution)/shard_map/ppermute | solution.py:109
  4.8 12.5 %collective-permute-start.1 = (bf16[256,768]{1,0:T(8,128)(2,1)S(1)}, bf16[256,768]{1,0:T(8,128)(2,1)S(1)}, u32[]{:S(2)}, u32[]{:S(2)}) collective-permute-start(bf16[256,768]{1,0:T(8,128)(2,1)S(1)} %get-tuple-element.76), channel_id=1, source_target_pairs={{0,0},{1,128},{128,1},{129,129},{2,2},{3,130},{130,3},{131,131},{4... | collective-permute-start | bytes 1179656 | tf_op jit(solution)/shard_map/ppermute | solution.py:108
  17.6 21.5 %collective-permute-start.4 = (bf16[512,768]{1,0:T(8,128)(2,1)S(1)}, bf16[512,768]{1,0:T(8,128)(2,1)S(1)}, u32[]{:S(2)}, u32[]{:S(2)}) collective-permute-start(bf16[512,768]{1,0:T(8,128)(2,1)S(1)} %pad_maximum_fusion.3), channel_id=1, source_target_pairs={{0,16},{16,32},{32,48},{48,64},{64,80},{80,96},{96,112},{112,0},{1... | collective-permute-start | bytes 2359304 | tf_op jit(solution)/shard_map/ppermute | solution.py:89
  17.7 21.4 %collective-permute-start.5 = (bf16[512,768]{1,0:T(8,128)(2,1)S(1)}, bf16[512,768]{1,0:T(8,128)(2,1)S(1)}, u32[]{:S(2)}, u32[]{:S(2)}) collective-permute-start(bf16[512,768]{1,0:T(8,128)(2,1)S(1)} %pad_maximum_fusion.3), channel_id=1, source_target_pairs={{0,112},{16,0},{32,16},{48,32},{64,48},{80,64},{96,80},{112,96},{1... | collective-permute-start | bytes 2359304 | tf_op jit(solution)/shard_map/ppermute | solution.py:89
  21.7 10.0 %collective-permute-start.3 = (bf16[376,512]{1,0:T(8,128)(2,1)S(1)}, bf16[376,512]{1,0:T(8,128)(2,1)S(1)}, u32[]{:S(2)}, u32[]{:S(2)}) collective-permute-start(bf16[376,512]{1,0:T(8,128)(2,1)S(1)} %pad_maximum_fusion.5), channel_id=1, source_target_pairs={{0,8},{8,0},{1,9},{9,1},{2,10},{10,2},{3,11},{11,3},{4,12},{12,4},... | collective-permute-start | bytes 1155080 | tf_op jit(solution)/shard_map/ppermute | solution.py:19
  23.1 18.5 %collective-permute-start.6 = (bf16[256,896]{1,0:T(8,128)(2,1)S(1)}, bf16[256,896]{1,0:T(8,128)(2,1)S(1)}, u32[]{:S(2)}, u32[]{:S(2)}) collective-permute-start(bf16[256,896]{1,0:T(8,128)(2,1)S(1)} %get-tuple-element.79), channel_id=1, source_target_pairs={{0,1},{1,129},{128,0},{129,128},{2,3},{3,131},{130,2},{131,130},{4... | collective-permute-start | bytes 1376264 | tf_op jit(solution)/shard_map/ppermute | solution.py:109
  25.0 19.6 %collective-permute-start.7 = (bf16[256,896]{1,0:T(8,128)(2,1)S(1)}, bf16[256,896]{1,0:T(8,128)(2,1)S(1)}, u32[]{:S(2)}, u32[]{:S(2)}) collective-permute-start(bf16[256,896]{1,0:T(8,128)(2,1)S(1)} %get-tuple-element.80), channel_id=1, source_target_pairs={{0,0},{1,128},{128,1},{129,129},{2,2},{3,130},{130,3},{131,131},{4... | collective-permute-start | bytes 1376264 | tf_op jit(solution)/shard_map/ppermute | solution.py:108
  39.1 20.8 %collective-permute-start.12 = (bf16[376,1024]{1,0:T(8,128)(2,1)S(1)}, bf16[376,1024]{1,0:T(8,128)(2,1)S(1)}, u32[]{:S(2)}, u32[]{:S(2)}) collective-permute-start(bf16[376,1024]{1,0:T(8,128)(2,1)S(1)} %pad_maximum_fusion.4), channel_id=1, source_target_pairs={{0,128},{128,0},{1,129},{129,1},{2,130},{130,2},{3,131},{131,3},{4... | collective-permute-start | bytes 2310152 | tf_op jit(solution)/shard_map/ppermute | solution.py:19
  44.8 22.0 %collective-permute-start.8 = (bf16[512,896]{1,0:T(8,128)(2,1)S(1)}, bf16[512,896]{1,0:T(8,128)(2,1)S(1)}, u32[]{:S(2)}, u32[]{:S(2)}) collective-permute-start(bf16[512,896]{1,0:T(8,128)(2,1)S(1)} %pad_maximum_fusion.2), channel_id=1, source_target_pairs={{0,16},{16,32},{32,48},{48,64},{64,80},{80,96},{96,112},{112,0},{1... | collective-permute-start | bytes 2752520 | tf_op jit(solution)/shard_map/ppermute | solution.py:89
  44.9 21.9 %collective-permute-start.9 = (bf16[512,896]{1,0:T(8,128)(2,1)S(1)}, bf16[512,896]{1,0:T(8,128)(2,1)S(1)}, u32[]{:S(2)}, u32[]{:S(2)}) collective-permute-start(bf16[512,896]{1,0:T(8,128)(2,1)S(1)} %pad_maximum_fusion.2), channel_id=1, source_target_pairs={{0,112},{16,0},{32,16},{48,32},{64,48},{80,64},{96,80},{112,96},{1... | collective-permute-start | bytes 2752520 | tf_op jit(solution)/shard_map/ppermute | solution.py:89
  60.0 35.5 %collective-permute-start.13 = (bf16[2,376,1024]{2,1,0:T(8,128)(2,1)S(1)}, bf16[2,376,1024]{2,1,0:T(8,128)(2,1)S(1)}, u32[]{:S(2)}, u32[]{:S(2)}) collective-permute-start(bf16[2,376,1024]{2,1,0:T(8,128)(2,1)S(1)} %pad_maximum_fusion.here), channel_id=1, source_target_pairs={{0,2},{2,4},{4,6},{6,0},{1,3},{3,5},{5,7},{7,1},{8,10},{10,12},{12... | collective-permute-start | bytes 4620296 | tf_op jit(solution)/shard_map/ppermute | solution.py:44
  61.4 35.1 %collective-permute-start.14 = (bf16[2,376,1024]{2,1,0:T(8,128)(2,1)S(1)}, bf16[2,376,1024]{2,1,0:T(8,128)(2,1)S(1)}, u32[]{:S(2)}, u32[]{:S(2)}) collective-permute-start(bf16[2,376,1024]{2,1,0:T(8,128)(2,1)S(1)} %pad_maximum_fusion.here), channel_id=1, source_target_pairs={{0,6},{2,0},{4,2},{6,4},{1,7},{3,1},{5,3},{7,5},{8,14},{10,8},{12,... | collective-permute-start | bytes 4620296 | tf_op jit(solution)/shard_map/ppermute | solution.py:44
  67.9 39.7 %collective-permute-start.11 = (bf16[512,1664]{1,0:T(8,128)(2,1)}, bf16[512,1664]{1,0:T(8,128)(2,1)}, u32[]{:S(2)}, u32[]{:S(2)}) collective-permute-start(bf16[512,1664]{1,0:T(8,128)(2,1)} %constant_dynamic-update-slice_fusion.2), channel_id=1, source_target_pairs={{0,112},{16,0},{32,16},{48,32},{64,48},{80,64},{96,80},{112,96},{1... | collective-permute-start | bytes 5111816 | tf_op jit(solution)/shard_map/ppermute | solution.py:89
  71.9 40.4 %collective-permute-start.10 = (bf16[512,1664]{1,0:T(8,128)(2,1)}, bf16[512,1664]{1,0:T(8,128)(2,1)}, u32[]{:S(2)}, u32[]{:S(2)}) collective-permute-start(bf16[512,1664]{1,0:T(8,128)(2,1)} %constant_dynamic-update-slice_fusion), channel_id=1, source_target_pairs={{0,16},{16,32},{32,48},{48,64},{64,80},{80,96},{96,112},{112,0},{1... | collective-permute-start | bytes 5111816 | tf_op jit(solution)/shard_map/ppermute | solution.py:89
  96.5 18.5 %collective-permute-start.15 = (bf16[376,1024]{1,0:T(8,128)(2,1)}, bf16[376,1024]{1,0:T(8,128)(2,1)}, u32[]{:S(2)}, u32[]{:S(2)}) collective-permute-start(bf16[376,1024]{1,0:T(8,128)(2,1)} %slice_bitcast_fusion.1), channel_id=1, source_target_pairs={{0,2},{2,4},{4,6},{6,0},{1,3},{3,5},{5,7},{7,1},{8,10},{10,12},{12... | collective-permute-start | bytes 2310152 | tf_op jit(solution)/shard_map/ppermute | solution.py:44
  98.6 17.3 %collective-permute-start.16 = (bf16[376,1024]{1,0:T(8,128)(2,1)}, bf16[376,1024]{1,0:T(8,128)(2,1)}, u32[]{:S(2)}, u32[]{:S(2)}) collective-permute-start(bf16[376,1024]{1,0:T(8,128)(2,1)} %slice_bitcast_fusion), channel_id=1, source_target_pairs={{0,6},{2,0},{4,2},{6,4},{1,7},{3,1},{5,3},{7,5},{8,14},{10,8},{12,... | collective-permute-start | bytes 2310152 | tf_op jit(solution)/shard_map/ppermute | solution.py:44
  112.3 40.3 %collective-permute-start.17 = (bf16[512,1664]{1,0:T(8,128)(2,1)}, bf16[512,1664]{1,0:T(8,128)(2,1)}, u32[]{:S(2)}, u32[]{:S(2)}) collective-permute-start(bf16[512,1664]{1,0:T(8,128)(2,1)} %collective-permute-done.10), channel_id=1, source_target_pairs={{0,16},{16,32},{32,48},{48,64},{64,80},{80,96},{96,112},{112,0},{1... | collective-permute-start | bytes 5111816 | tf_op jit(solution)/shard_map/ppermute | solution.py:89
  112.3 40.3 %collective-permute-start.18 = (bf16[512,1664]{1,0:T(8,128)(2,1)}, bf16[512,1664]{1,0:T(8,128)(2,1)}, u32[]{:S(2)}, u32[]{:S(2)}) collective-permute-start(bf16[512,1664]{1,0:T(8,128)(2,1)} %collective-permute-done.11), channel_id=1, source_target_pairs={{0,112},{16,0},{32,16},{48,32},{64,48},{80,64},{96,80},{112,96},{1... | collective-permute-start | bytes 5111816 | tf_op jit(solution)/shard_map/ppermute | solution.py:89
  160.2 13.9 %collective-permute-start.19 = (bf16[256,1024]{1,0:T(8,128)(2,1)S(1)}, bf16[256,1024]{1,0:T(8,128)(2,1)S(1)}, u32[]{:S(2)}, u32[]{:S(2)}) collective-permute-start(bf16[256,1024]{1,0:T(8,128)(2,1)S(1)} %slice.119), channel_id=1, source_target_pairs={{0,16},{16,32},{32,48},{48,64},{64,80},{80,96},{96,112},{112,0},{1... | collective-permute-start | bytes 1572872 | tf_op jit(solution)/shard_map/ppermute | solution.py:89
  160.3 13.8 %collective-permute-start.20 = (bf16[256,1024]{1,0:T(8,128)(2,1)S(1)}, bf16[256,1024]{1,0:T(8,128)(2,1)S(1)}, u32[]{:S(2)}, u32[]{:S(2)}) collective-permute-start(bf16[256,1024]{1,0:T(8,128)(2,1)S(1)} %slice.120), channel_id=1, source_target_pairs={{0,112},{16,0},{32,16},{48,32},{64,48},{80,64},{96,80},{112,96},{1... | collective-permute-start | bytes 1572872 | tf_op jit(solution)/shard_map/ppermute | solution.py:89
  163.0 18.1 %collective-permute-start.21 = (bf16[256,640]{1,0:T(8,128)(2,1)S(1)}, bf16[256,640]{1,0:T(8,128)(2,1)S(1)}, u32[]{:S(2)}, u32[]{:S(2)}) collective-permute-start(bf16[256,640]{1,0:T(8,128)(2,1)S(1)} %slice.126), channel_id=1, source_target_pairs={{0,16},{16,32},{32,48},{48,64},{64,80},{80,96},{96,112},{112,0},{1... | collective-permute-start | bytes 983048 | tf_op jit(solution)/shard_map/ppermute | solution.py:89
  163.0 18.1 %collective-permute-start.22 = (bf16[256,640]{1,0:T(8,128)(2,1)S(1)}, bf16[256,640]{1,0:T(8,128)(2,1)S(1)}, u32[]{:S(2)}, u32[]{:S(2)}) collective-permute-start(bf16[256,640]{1,0:T(8,128)(2,1)S(1)} %slice.127), channel_id=1, source_target_pairs={{0,112},{16,0},{32,16},{48,32},{64,48},{80,64},{96,80},{112,96},{1... | collective-permute-start | bytes 983048 | tf_op jit(solution)/shard_map/ppermute | solution.py:89
  186.9 19.2 %collective-permute-start.24 = (bf16[376,1024]{1,0:T(8,128)(2,1)S(1)}, bf16[376,1024]{1,0:T(8,128)(2,1)S(1)}, u32[]{:S(2)}, u32[]{:S(2)}) collective-permute-start(bf16[376,1024]{1,0:T(8,128)(2,1)S(1)} %multiply_convert_fusion), channel_id=1, source_target_pairs={{0,0},{1,128},{128,129},{129,1},{2,2},{3,130},{130,131},{131,3},{4... | collective-permute-start | bytes 2310152 | tf_op jit(solution)/shard_map/ppermute | solution.py:122
  189.2 17.0 %collective-permute-start.26 = (bf16[376,640]{1,0:T(8,128)(2,1)S(1)}, bf16[376,640]{1,0:T(8,128)(2,1)S(1)}, u32[]{:S(2)}, u32[]{:S(2)}) collective-permute-start(bf16[376,640]{1,0:T(8,128)(2,1)S(1)} %multiply_convert_fusion.1), channel_id=1, source_target_pairs={{0,0},{1,128},{128,129},{129,1},{2,2},{3,130},{130,131},{131,3},{4... | collective-permute-start | bytes 1443848 | tf_op jit(solution)/shard_map/ppermute | solution.py:122
  (13 other events, 82.9 us)

commit v9 on v8

--- a/solution.py
+++ b/solution.py
@@ -150,10 +150,9 @@
         (up[quarter[0], columns], down[quarter[1], columns])
         for columns in (slice(0, LAST), slice(LAST, None))
     ]
-    (*sent[0], up, down) = together(*sent[0], up, down)
-    early += product(gathered, [(6, up), (10, down)], half)
     ends = [step_along_z(*pair) for pair in sent]
-    up, down, early = together(*ends[0], early)
+    late_up, late_down, up, down = together(up, down, *ends[0])
+    early += product(gathered, [(6, late_up), (10, late_down)], half)
     total = early[:, :LAST] + product(gathered, ((8, up), (9, down)), half)
     total, up, down = together(total, *ends[1])
     first = home(activate(total))

time: 208 us -> 204 us (0.981)
  waiting for transfers between devices: 111 us -> 106 us
    ppermute x12, waiting for transfers between devices: 43.7 us -> 38.7 us  [along_z(): return lax.ppermute(value, 'z', [(i, (i + shift) % 8) for i in range(8)])]
  transfers between devices with their start and end apart: 27 -> 27, of which waited for: 15 -> 15; matrix products, arithmetic and copies ran while one was open for 16% -> 20% of each run, Pallas kernels for 1% -> 1%
where the time goes in v9:
time: 204 us
  waiting for transfers between devices  106 us (52%)
  starting transfers between devices  48.8 us (24%)
  matrix products  29 us (14%)
  local copies, waits for them, and re-layouts  12.7 us (6%)
  other arithmetic  4.45 us (2%)
  Pallas kernels  2.63 us (1%)
    ppermute x12, waiting for transfers between devices, along_z(): return lax.ppermute(value, 'z', [(i, (i + shift) % 8) for i in range(8)])  38.7 us
    dot_general x11, matrix products, product(): total += jnp.dot(features, piece, preferred_element_type=jnp.float32)  29 us
    ppermute x4, waiting for transfers between devices, along_y(): return lax.ppermute(value, 'y', [(i, (i + shift) % 4) for i in range(4)])  24.5 us
    ppermute x12, starting transfers between devices, along_z(): return lax.ppermute(value, 'z', [(i, (i + shift) % 8) for i in range(8)])  18 us
    ppermute x5, waiting for transfers between devices, exchange(): return lax.ppermute(value, axis, [(i, i ^ flip) for i in range(size)])  16.5 us
    ppermute x2, waiting for transfers between devices, home(): return lax.ppermute(out, ('xh', 'core'), HOME)  15 us
    ppermute x2, waiting for transfers between devices, swapped(): turned = lax.ppermute(first, ('xh', 'core'), TURN)  10.8 us
    ppermute x2, starting transfers between devices, swapped(): turned = lax.ppermute(first, ('xh', 'core'), TURN)  8.8 us
  transfers between devices with their start and end apart: 27, of which 15 were waited for; matrix products, arithmetic and copies ran while one was open for 20% of the time, Pallas kernels for 1%

profile of v9, /device:TPU:1, one launch (start us, length us, event | category | flops | bytes accessed | tf_op | source)
XLA Modules:
  0.0 203.6 jit_solution(12051153290725019012)
XLA Ops:
  1.2 3.7 %collective-permute-start = (bf16[256,768]{1,0:T(8,128)(2,1)S(1)}, bf16[256,768]{1,0:T(8,128)(2,1)S(1)}, u32[]{:S(2)}, u32[]{:S(2)}) collective-permute-start(bf16[256,768]{1,0:T(8,128)(2,1)S(1)} %get-tuple-element.69), channel_id=1, source_target_pairs={{0,1},{1,129},{128,0},{129,128},{2,3},{3,131},{130,2},{131,130},{4... | collective-permute-start | bytes 1179656 | tf_op jit(solution)/shard_map/ppermute | solution.py:109
  4.8 4.7 %collective-permute-start.1 = (bf16[256,768]{1,0:T(8,128)(2,1)S(1)}, bf16[256,768]{1,0:T(8,128)(2,1)S(1)}, u32[]{:S(2)}, u32[]{:S(2)}) collective-permute-start(bf16[256,768]{1,0:T(8,128)(2,1)S(1)} %get-tuple-element.70), channel_id=1, source_target_pairs={{0,0},{1,128},{128,1},{129,129},{2,2},{3,130},{130,3},{131,131},{4... | collective-permute-start | bytes 1179656 | tf_op jit(solution)/shard_map/ppermute | solution.py:108
  9.6 7.7 %collective-permute-done.1 = bf16[256,768]{1,0:T(8,128)(2,1)S(1)} collective-permute-done((bf16[256,768]{1,0:T(8,128)(2,1)S(1)}, bf16[256,768]{1,0:T(8,128)(2,1)S(1)}, u32[]{:S(2)}, u32[]{:S(2)}) %collective-permute-start.1) | collective-permute-done | bytes 393248 | tf_op jit(solution)/shard_map/ppermute | solution.py:108
  17.7 3.9 %collective-permute-start.5 = (bf16[512,768]{1,0:T(8,128)(2,1)S(1)}, bf16[512,768]{1,0:T(8,128)(2,1)S(1)}, u32[]{:S(2)}, u32[]{:S(2)}) collective-permute-start(bf16[512,768]{1,0:T(8,128)(2,1)S(1)} %pad_maximum_fusion.3), channel_id=1, source_target_pairs={{0,112},{16,0},{32,16},{48,32},{64,48},{80,64},{96,80},{112,96},{1... | collective-permute-start | bytes 2359304 | tf_op jit(solution)/shard_map/ppermute | solution.py:89
  25.0 4.1 %collective-permute-start.7 = (bf16[256,896]{1,0:T(8,128)(2,1)S(1)}, bf16[256,896]{1,0:T(8,128)(2,1)S(1)}, u32[]{:S(2)}, u32[]{:S(2)}) collective-permute-start(bf16[256,896]{1,0:T(8,128)(2,1)S(1)} %get-tuple-element.74), channel_id=1, source_target_pairs={{0,0},{1,128},{128,1},{129,129},{2,2},{3,130},{130,3},{131,131},{4... | collective-permute-start | bytes 1376264 | tf_op jit(solution)/shard_map/ppermute | solution.py:108
  31.8 7.3 %collective-permute-done.4 = bf16[512,768]{1,0:T(8,128)(2,1)S(1)} collective-permute-done((bf16[512,768]{1,0:T(8,128)(2,1)S(1)}, bf16[512,768]{1,0:T(8,128)(2,1)S(1)}, u32[]{:S(2)}, u32[]{:S(2)}) %collective-permute-start.4) | collective-permute-done | bytes 786464 | tf_op jit(solution)/shard_map/ppermute | solution.py:89
  41.6 3.1 %collective-permute-done.7 = bf16[256,896]{1,0:T(8,128)(2,1)S(1)} collective-permute-done((bf16[256,896]{1,0:T(8,128)(2,1)S(1)}, bf16[256,896]{1,0:T(8,128)(2,1)S(1)}, u32[]{:S(2)}, u32[]{:S(2)}) %collective-permute-start.7) | collective-permute-done | bytes 458784 | tf_op jit(solution)/shard_map/ppermute | solution.py:108
  47.6 12.3 %collective-permute-done.12 = bf16[376,1024]{1,0:T(8,128)(2,1)S(1)} collective-permute-done((bf16[376,1024]{1,0:T(8,128)(2,1)S(1)}, bf16[376,1024]{1,0:T(8,128)(2,1)S(1)}, u32[]{:S(2)}, u32[]{:S(2)}) %collective-permute-start.12) | collective-permute-done | bytes 770080 | tf_op jit(solution)/shard_map/ppermute | solution.py:19
  67.9 3.0 %collective-permute-start.11 = (bf16[512,1664]{1,0:T(8,128)(2,1)}, bf16[512,1664]{1,0:T(8,128)(2,1)}, u32[]{:S(2)}, u32[]{:S(2)}) collective-permute-start(bf16[512,1664]{1,0:T(8,128)(2,1)} %constant_dynamic-update-slice_fusion.2), channel_id=1, source_target_pairs={{0,112},{16,0},{32,16},{48,32},{64,48},{80,64},{96,80},{112,96},{1... | collective-permute-start | bytes 5111816 | tf_op jit(solution)/shard_map/ppermute | solution.py:89
  71.9 23.7 %collective-permute-done.13.up = bf16[2,376,1024]{2,1,0:T(8,128)(2,1)S(1)} collective-permute-done((bf16[2,376,1024]{2,1,0:T(8,128)(2,1)S(1)}, bf16[2,376,1024]{2,1,0:T(8,128)(2,1)S(1)}, u32[]{:S(2)}, u32[]{:S(2)}) %collective-permute-start.13) | collective-permute-done | bytes 1540128 | tf_op jit(solution)/shard_map/ppermute | solution.py:44
  101.3 6.3 %collective-permute-done.11 = bf16[512,1664]{1,0:T(8,128)(2,1)} collective-permute-done((bf16[512,1664]{1,0:T(8,128)(2,1)}, bf16[512,1664]{1,0:T(8,128)(2,1)}, u32[]{:S(2)}, u32[]{:S(2)}) %collective-permute-start.11) | collective-permute-done | bytes 1703968 | tf_op jit(solution)/shard_map/ppermute | solution.py:89
  107.6 4.7 %collective-permute-done.10 = bf16[512,1664]{1,0:T(8,128)(2,1)} collective-permute-done((bf16[512,1664]{1,0:T(8,128)(2,1)}, bf16[512,1664]{1,0:T(8,128)(2,1)}, u32[]{:S(2)}, u32[]{:S(2)}) %collective-permute-start.10) | collective-permute-done | bytes 1703968 | tf_op jit(solution)/shard_map/ppermute | solution.py:89
  119.9 3.0 %fusion.17 = f32[752,1664]{1,0:T(8,128)S(1)} fusion(bf16[512,1664]{1,0:T(8,128)(2,1)} %constant_dynamic-update-slice_fusion, bf16[752,4096]{1,0:T(8,128)(2,1)S(1)} %bitcast.19), kind=kOutput, calls=%fused_computation.27 | convolution fusion | flops 1281359872 | bytes 7479296 | tf_op jit(solution)/shard_map/dot_general | solution.py:100
  122.9 3.1 %fusion.15 = f32[752,1664]{1,0:T(8,128)S(1)} fusion(bf16[512,1664]{1,0:T(8,128)(2,1)} %constant_dynamic-update-slice_fusion.2, bf16[752,4096]{1,0:T(8,128)(2,1)S(1)} %bitcast.20), kind=kOutput, calls=%fused_computation.25 | convolution fusion | flops 1281359872 | bytes 7479296 | tf_op jit(solution)/shard_map/dot_general | solution.py:100
  126.0 3.8 %fusion = f32[752,1664]{1,0:T(8,128)} fusion(bf16[256,896]{1,0:T(8,128)(2,1)S(1)} %copy-done.3, bf16[256,896]{1,0:T(8,128)(2,1)S(1)} %get-tuple-element.71, bf16[512,768]{1,0:T(8,128)(2,1)S(1)} %copy-done.6, bf16[752,4096]{1,0:T(8,128)(2,1)S(1)} %bitcast.21), kind=kOutput, calls=%fused_computation.4 | convolution fusion | flops 1286471680 | bytes 7479296 | tf_op jit(solution)/shard_map/dot_general | solution.py:100
  129.9 3.0 %fusion.13 = f32[752,1664]{1,0:T(8,128)S(1)} fusion(bf16[512,1664]{1,0:T(8,128)(2,1)} %collective-permute-done.10, bf16[752,4096]{1,0:T(8,128)(2,1)S(1)} %bitcast.22), kind=kOutput, calls=%fused_computation.23 | convolution fusion | flops 1281359872 | bytes 7479296 | tf_op jit(solution)/shard_map/dot_general | solution.py:100
  132.9 7.2 %add_add_fusion.1 = f32[752,1664]{1,0:T(8,128)} fusion(f32[752,1664]{1,0:T(8,128)S(1)} %fusion.13, f32[752,1664]{1,0:T(8,128)S(1)} %fusion.15, f32[752,1664]{1,0:T(8,128)} %fusion, f32[752,1664]{1,0:T(8,128)S(1)} %fusion.17, bf16[512,1664]{1,0:T(8,128)(2,1)} %collective-permute-done.11, bf16[752,4096]{1,0:T(8,128)(2,1)S(1)} %bitcast.23), kind=kOutput, calls=%fused_computation.1 | convolution fusion | flops 1286365184 | bytes 27500544 | tf_op jit(solution)/shard_map/dot_general | solution.py:100
  140.1 12.5 %collective-permute-done.17 = bf16[512,1664]{1,0:T(8,128)(2,1)} collective-permute-done((bf16[512,1664]{1,0:T(8,128)(2,1)}, bf16[512,1664]{1,0:T(8,128)(2,1)}, u32[]{:S(2)}, u32[]{:S(2)}) %collective-permute-start.17) | collective-permute-done | bytes 1703968 | tf_op jit(solution)/shard_map/ppermute | solution.py:89
  154.9 2.7 %collective-permute-start.20 = (bf16[256,1024]{1,0:T(8,128)(2,1)S(1)}, bf16[256,1024]{1,0:T(8,128)(2,1)S(1)}, u32[]{:S(2)}, u32[]{:S(2)}) collective-permute-start(bf16[256,1024]{1,0:T(8,128)(2,1)S(1)} %slice.121), channel_id=1, source_target_pairs={{0,112},{16,0},{32,16},{48,32},{64,48},{80,64},{96,80},{112,96},{1... | collective-permute-start | bytes 1572872 | tf_op jit(solution)/shard_map/ppermute | solution.py:89
  162.4 5.2 %collective-permute-done.19 = bf16[256,1024]{1,0:T(8,128)(2,1)S(1)} collective-permute-done((bf16[256,1024]{1,0:T(8,128)(2,1)S(1)}, bf16[256,1024]{1,0:T(8,128)(2,1)S(1)}, u32[]{:S(2)}, u32[]{:S(2)}) %collective-permute-start.19) | collective-permute-done | bytes 524320 | tf_op jit(solution)/shard_map/ppermute | solution.py:89
  168.9 3.3 %fusion.6 = f32[752,1664]{1,0:T(8,128)S(1)} fusion(bf16[512,1664]{1,0:T(8,128)(2,1)} %collective-permute-done.18, bf16[752,4096]{1,0:T(8,128)(2,1)S(1)} %bitcast.25), kind=kOutput, calls=%fused_computation.18 | convolution fusion | flops 1281359872 | bytes 7479296 | tf_op jit(solution)/shard_map/dot_general | solution.py:100
  172.3 3.2 %add_add_fusion = f32[752,1664]{1,0:T(8,128)S(1)} fusion(f32[752,1664]{1,0:T(8,128)S(1)} %bitcast.31, f32[752,1664]{1,0:T(8,128)S(1)} %fusion.6, bf16[512,1664]{1,0:T(8,128)(2,1)} %collective-permute-done.17, bf16[752,4096]{1,0:T(8,128)(2,1)S(1)} %bitcast.26), kind=kOutput, calls=%fused_computation | convolution fusion | flops 1283862528 | bytes 17489920 | tf_op jit(solution)/shard_map/dot_general | solution.py:100
  176.4 3.1 %collective-permute-start.23 = (f32[376,1024]{1,0:T(8,128)S(1)}, f32[376,1024]{1,0:T(8,128)S(1)}, u32[]{:S(2)}, u32[]{:S(2)}) collective-permute-start(f32[376,1024]{1,0:T(8,128)S(1)} %slice_select_fusion), channel_id=1, source_target_pairs={{0,1},{1,0},{2,3},{3,2},{4,5},{5,4},{6,7},{7,6},{8,9},{9,8},{10,11... | collective-permute-start | bytes 4620296 | tf_op jit(solution)/shard_map/ppermute | solution.py:19
  187.5 15.0 %collective-permute-done.26 = bf16[376,640]{1,0:T(8,128)(2,1)S(1)} collective-permute-done((bf16[376,640]{1,0:T(8,128)(2,1)S(1)}, bf16[376,640]{1,0:T(8,128)(2,1)S(1)}, u32[]{:S(2)}, u32[]{:S(2)}) %collective-permute-start.26) | collective-permute-done | bytes 481312 | tf_op jit(solution)/shard_map/ppermute | solution.py:122
  (92 shorter events, 53.6 us)
Async XLA Ops:
  1.2 8.4 %collective-permute-start = (bf16[256,768]{1,0:T(8,128)(2,1)S(1)}, bf16[256,768]{1,0:T(8,128)(2,1)S(1)}, u32[]{:S(2)}, u32[]{:S(2)}) collective-permute-start(bf16[256,768]{1,0:T(8,128)(2,1)S(1)} %get-tuple-element.69), channel_id=1, source_target_pairs={{0,1},{1,129},{128,0},{129,128},{2,3},{3,131},{130,2},{131,130},{4... | collective-permute-start | bytes 1179656 | tf_op jit(solution)/shard_map/ppermute | solution.py:109
  4.8 12.5 %collective-permute-start.1 = (bf16[256,768]{1,0:T(8,128)(2,1)S(1)}, bf16[256,768]{1,0:T(8,128)(2,1)S(1)}, u32[]{:S(2)}, u32[]{:S(2)}) collective-permute-start(bf16[256,768]{1,0:T(8,128)(2,1)S(1)} %get-tuple-element.70), channel_id=1, source_target_pairs={{0,0},{1,128},{128,1},{129,129},{2,2},{3,130},{130,3},{131,131},{4... | collective-permute-start | bytes 1179656 | tf_op jit(solution)/shard_map/ppermute | solution.py:108
  17.6 21.5 %collective-permute-start.4 = (bf16[512,768]{1,0:T(8,128)(2,1)S(1)}, bf16[512,768]{1,0:T(8,128)(2,1)S(1)}, u32[]{:S(2)}, u32[]{:S(2)}) collective-permute-start(bf16[512,768]{1,0:T(8,128)(2,1)S(1)} %pad_maximum_fusion.3), channel_id=1, source_target_pairs={{0,16},{16,32},{32,48},{48,64},{64,80},{80,96},{96,112},{112,0},{1... | collective-permute-start | bytes 2359304 | tf_op jit(solution)/shard_map/ppermute | solution.py:89
  17.7 21.4 %collective-permute-start.5 = (bf16[512,768]{1,0:T(8,128)(2,1)S(1)}, bf16[512,768]{1,0:T(8,128)(2,1)S(1)}, u32[]{:S(2)}, u32[]{:S(2)}) collective-permute-start(bf16[512,768]{1,0:T(8,128)(2,1)S(1)} %pad_maximum_fusion.3), channel_id=1, source_target_pairs={{0,112},{16,0},{32,16},{48,32},{64,48},{80,64},{96,80},{112,96},{1... | collective-permute-start | bytes 2359304 | tf_op jit(solution)/shard_map/ppermute | solution.py:89
  21.7 10.0 %collective-permute-start.3 = (bf16[376,512]{1,0:T(8,128)(2,1)S(1)}, bf16[376,512]{1,0:T(8,128)(2,1)S(1)}, u32[]{:S(2)}, u32[]{:S(2)}) collective-permute-start(bf16[376,512]{1,0:T(8,128)(2,1)S(1)} %pad_maximum_fusion.5), channel_id=1, source_target_pairs={{0,8},{8,0},{1,9},{9,1},{2,10},{10,2},{3,11},{11,3},{4,12},{12,4},... | collective-permute-start | bytes 1155080 | tf_op jit(solution)/shard_map/ppermute | solution.py:19
  23.1 18.5 %collective-permute-start.6 = (bf16[256,896]{1,0:T(8,128)(2,1)S(1)}, bf16[256,896]{1,0:T(8,128)(2,1)S(1)}, u32[]{:S(2)}, u32[]{:S(2)}) collective-permute-start(bf16[256,896]{1,0:T(8,128)(2,1)S(1)} %get-tuple-element.73), channel_id=1, source_target_pairs={{0,1},{1,129},{128,0},{129,128},{2,3},{3,131},{130,2},{131,130},{4... | collective-permute-start | bytes 1376264 | tf_op jit(solution)/shard_map/ppermute | solution.py:109
  25.0 19.6 %collective-permute-start.7 = (bf16[256,896]{1,0:T(8,128)(2,1)S(1)}, bf16[256,896]{1,0:T(8,128)(2,1)S(1)}, u32[]{:S(2)}, u32[]{:S(2)}) collective-permute-start(bf16[256,896]{1,0:T(8,128)(2,1)S(1)} %get-tuple-element.74), channel_id=1, source_target_pairs={{0,0},{1,128},{128,1},{129,129},{2,2},{3,130},{130,3},{131,131},{4... | collective-permute-start | bytes 1376264 | tf_op jit(solution)/shard_map/ppermute | solution.py:108
  39.1 20.8 %collective-permute-start.12 = (bf16[376,1024]{1,0:T(8,128)(2,1)S(1)}, bf16[376,1024]{1,0:T(8,128)(2,1)S(1)}, u32[]{:S(2)}, u32[]{:S(2)}) collective-permute-start(bf16[376,1024]{1,0:T(8,128)(2,1)S(1)} %pad_maximum_fusion.4), channel_id=1, source_target_pairs={{0,128},{128,0},{1,129},{129,1},{2,130},{130,2},{3,131},{131,3},{4... | collective-permute-start | bytes 2310152 | tf_op jit(solution)/shard_map/ppermute | solution.py:19
  44.8 22.0 %collective-permute-start.8 = (bf16[512,896]{1,0:T(8,128)(2,1)S(1)}, bf16[512,896]{1,0:T(8,128)(2,1)S(1)}, u32[]{:S(2)}, u32[]{:S(2)}) collective-permute-start(bf16[512,896]{1,0:T(8,128)(2,1)S(1)} %pad_maximum_fusion.2), channel_id=1, source_target_pairs={{0,16},{16,32},{32,48},{48,64},{64,80},{80,96},{96,112},{112,0},{1... | collective-permute-start | bytes 2752520 | tf_op jit(solution)/shard_map/ppermute | solution.py:89
  44.9 21.9 %collective-permute-start.9 = (bf16[512,896]{1,0:T(8,128)(2,1)S(1)}, bf16[512,896]{1,0:T(8,128)(2,1)S(1)}, u32[]{:S(2)}, u32[]{:S(2)}) collective-permute-start(bf16[512,896]{1,0:T(8,128)(2,1)S(1)} %pad_maximum_fusion.2), channel_id=1, source_target_pairs={{0,112},{16,0},{32,16},{48,32},{64,48},{80,64},{96,80},{112,96},{1... | collective-permute-start | bytes 2752520 | tf_op jit(solution)/shard_map/ppermute | solution.py:89
  60.0 35.5 %collective-permute-start.13 = (bf16[2,376,1024]{2,1,0:T(8,128)(2,1)S(1)}, bf16[2,376,1024]{2,1,0:T(8,128)(2,1)S(1)}, u32[]{:S(2)}, u32[]{:S(2)}) collective-permute-start(bf16[2,376,1024]{2,1,0:T(8,128)(2,1)S(1)} %pad_maximum_fusion.here), channel_id=1, source_target_pairs={{0,2},{2,4},{4,6},{6,0},{1,3},{3,5},{5,7},{7,1},{8,10},{10,12},{12... | collective-permute-start | bytes 4620296 | tf_op jit(solution)/shard_map/ppermute | solution.py:44
  61.4 35.1 %collective-permute-start.14 = (bf16[2,376,1024]{2,1,0:T(8,128)(2,1)S(1)}, bf16[2,376,1024]{2,1,0:T(8,128)(2,1)S(1)}, u32[]{:S(2)}, u32[]{:S(2)}) collective-permute-start(bf16[2,376,1024]{2,1,0:T(8,128)(2,1)S(1)} %pad_maximum_fusion.here), channel_id=1, source_target_pairs={{0,6},{2,0},{4,2},{6,4},{1,7},{3,1},{5,3},{7,5},{8,14},{10,8},{12,... | collective-permute-start | bytes 4620296 | tf_op jit(solution)/shard_map/ppermute | solution.py:44
  67.9 39.7 %collective-permute-start.11 = (bf16[512,1664]{1,0:T(8,128)(2,1)}, bf16[512,1664]{1,0:T(8,128)(2,1)}, u32[]{:S(2)}, u32[]{:S(2)}) collective-permute-start(bf16[512,1664]{1,0:T(8,128)(2,1)} %constant_dynamic-update-slice_fusion.2), channel_id=1, source_target_pairs={{0,112},{16,0},{32,16},{48,32},{64,48},{80,64},{96,80},{112,96},{1... | collective-permute-start | bytes 5111816 | tf_op jit(solution)/shard_map/ppermute | solution.py:89
  71.9 40.4 %collective-permute-start.10 = (bf16[512,1664]{1,0:T(8,128)(2,1)}, bf16[512,1664]{1,0:T(8,128)(2,1)}, u32[]{:S(2)}, u32[]{:S(2)}) collective-permute-start(bf16[512,1664]{1,0:T(8,128)(2,1)} %constant_dynamic-update-slice_fusion), channel_id=1, source_target_pairs={{0,16},{16,32},{32,48},{48,64},{64,80},{80,96},{96,112},{112,0},{1... | collective-permute-start | bytes 5111816 | tf_op jit(solution)/shard_map/ppermute | solution.py:89
  96.5 18.5 %collective-permute-start.15 = (bf16[376,1024]{1,0:T(8,128)(2,1)}, bf16[376,1024]{1,0:T(8,128)(2,1)}, u32[]{:S(2)}, u32[]{:S(2)}) collective-permute-start(bf16[376,1024]{1,0:T(8,128)(2,1)} %slice_bitcast_fusion.1), channel_id=1, source_target_pairs={{0,2},{2,4},{4,6},{6,0},{1,3},{3,5},{5,7},{7,1},{8,10},{10,12},{12... | collective-permute-start | bytes 2310152 | tf_op jit(solution)/shard_map/ppermute | solution.py:44
  98.6 17.3 %collective-permute-start.16 = (bf16[376,1024]{1,0:T(8,128)(2,1)}, bf16[376,1024]{1,0:T(8,128)(2,1)}, u32[]{:S(2)}, u32[]{:S(2)}) collective-permute-start(bf16[376,1024]{1,0:T(8,128)(2,1)} %slice_bitcast_fusion), channel_id=1, source_target_pairs={{0,6},{2,0},{4,2},{6,4},{1,7},{3,1},{5,3},{7,5},{8,14},{10,8},{12,... | collective-permute-start | bytes 2310152 | tf_op jit(solution)/shard_map/ppermute | solution.py:44
  112.3 40.3 %collective-permute-start.17 = (bf16[512,1664]{1,0:T(8,128)(2,1)}, bf16[512,1664]{1,0:T(8,128)(2,1)}, u32[]{:S(2)}, u32[]{:S(2)}) collective-permute-start(bf16[512,1664]{1,0:T(8,128)(2,1)} %collective-permute-done.10), channel_id=1, source_target_pairs={{0,16},{16,32},{32,48},{48,64},{64,80},{80,96},{96,112},{112,0},{1... | collective-permute-start | bytes 5111816 | tf_op jit(solution)/shard_map/ppermute | solution.py:89
  112.3 40.3 %collective-permute-start.18 = (bf16[512,1664]{1,0:T(8,128)(2,1)}, bf16[512,1664]{1,0:T(8,128)(2,1)}, u32[]{:S(2)}, u32[]{:S(2)}) collective-permute-start(bf16[512,1664]{1,0:T(8,128)(2,1)} %collective-permute-done.11), channel_id=1, source_target_pairs={{0,112},{16,0},{32,16},{48,32},{64,48},{80,64},{96,80},{112,96},{1... | collective-permute-start | bytes 5111816 | tf_op jit(solution)/shard_map/ppermute | solution.py:89
  153.7 13.9 %collective-permute-start.19 = (bf16[256,1024]{1,0:T(8,128)(2,1)S(1)}, bf16[256,1024]{1,0:T(8,128)(2,1)S(1)}, u32[]{:S(2)}, u32[]{:S(2)}) collective-permute-start(bf16[256,1024]{1,0:T(8,128)(2,1)S(1)} %slice.120), channel_id=1, source_target_pairs={{0,16},{16,32},{32,48},{48,64},{64,80},{80,96},{96,112},{112,0},{1... | collective-permute-start | bytes 1572872 | tf_op jit(solution)/shard_map/ppermute | solution.py:89
  154.9 13.5 %collective-permute-start.20 = (bf16[256,1024]{1,0:T(8,128)(2,1)S(1)}, bf16[256,1024]{1,0:T(8,128)(2,1)S(1)}, u32[]{:S(2)}, u32[]{:S(2)}) collective-permute-start(bf16[256,1024]{1,0:T(8,128)(2,1)S(1)} %slice.121), channel_id=1, source_target_pairs={{0,112},{16,0},{32,16},{48,32},{64,48},{80,64},{96,80},{112,96},{1... | collective-permute-start | bytes 1572872 | tf_op jit(solution)/shard_map/ppermute | solution.py:89
  159.6 16.5 %collective-permute-start.21 = (bf16[256,640]{1,0:T(8,128)(2,1)S(1)}, bf16[256,640]{1,0:T(8,128)(2,1)S(1)}, u32[]{:S(2)}, u32[]{:S(2)}) collective-permute-start(bf16[256,640]{1,0:T(8,128)(2,1)S(1)} %slice.126), channel_id=1, source_target_pairs={{0,16},{16,32},{32,48},{48,64},{64,80},{80,96},{96,112},{112,0},{1... | collective-permute-start | bytes 983048 | tf_op jit(solution)/shard_map/ppermute | solution.py:89
  159.7 16.4 %collective-permute-start.22 = (bf16[256,640]{1,0:T(8,128)(2,1)S(1)}, bf16[256,640]{1,0:T(8,128)(2,1)S(1)}, u32[]{:S(2)}, u32[]{:S(2)}) collective-permute-start(bf16[256,640]{1,0:T(8,128)(2,1)S(1)} %slice.127), channel_id=1, source_target_pairs={{0,112},{16,0},{32,16},{48,32},{64,48},{80,64},{96,80},{112,96},{1... | collective-permute-start | bytes 983048 | tf_op jit(solution)/shard_map/ppermute | solution.py:89
  183.3 19.2 %collective-permute-start.24 = (bf16[376,1024]{1,0:T(8,128)(2,1)S(1)}, bf16[376,1024]{1,0:T(8,128)(2,1)S(1)}, u32[]{:S(2)}, u32[]{:S(2)}) collective-permute-start(bf16[376,1024]{1,0:T(8,128)(2,1)S(1)} %multiply_convert_fusion), channel_id=1, source_target_pairs={{0,0},{1,128},{128,129},{129,1},{2,2},{3,130},{130,131},{131,3},{4... | collective-permute-start | bytes 2310152 | tf_op jit(solution)/shard_map/ppermute | solution.py:122
  185.5 17.0 %collective-permute-start.26 = (bf16[376,640]{1,0:T(8,128)(2,1)S(1)}, bf16[376,640]{1,0:T(8,128)(2,1)S(1)}, u32[]{:S(2)}, u32[]{:S(2)}) collective-permute-start(bf16[376,640]{1,0:T(8,128)(2,1)S(1)} %multiply_convert_fusion.1), channel_id=1, source_target_pairs={{0,0},{1,128},{128,129},{129,1},{2,2},{3,130},{130,131},{131,3},{4... | collective-permute-start | bytes 1443848 | tf_op jit(solution)/shard_map/ppermute | solution.py:122
  (13 other events, 71.9 us)

commit v10 on v9

--- a/solution.py
+++ b/solution.py
@@ -150,8 +150,9 @@
         (up[quarter[0], columns], down[quarter[1], columns])
         for columns in (slice(0, LAST), slice(LAST, None))
     ]
+    late_up, late_down, *sent[1] = together(up, down, *sent[1])
     ends = [step_along_z(*pair) for pair in sent]
-    late_up, late_down, up, down = together(up, down, *ends[0])
+    up, down = together(*ends[0])
     early += product(gathered, [(6, late_up), (10, late_down)], half)
     total = early[:, :LAST] + product(gathered, ((8, up), (9, down)), half)
     total, up, down = together(total, *ends[1])

time: 204 us -> 205 us (level)
  transfers between devices with their start and end apart: 27 -> 27, of which waited for: 15 -> 15; matrix products, arithmetic and copies ran while one was open for 20% -> 18% of each run, Pallas kernels for 1% -> 1%
where the time goes in v10:
time: 205 us; the launch traced here: 204 us
  waiting for transfers between devices  107 us (52%)
  starting transfers between devices  47.7 us (23%)
  matrix products  28.6 us (14%)
  local copies, waits for them, and re-layouts  13.1 us (6%)
  other arithmetic  4.45 us (2%)
  Pallas kernels  2.63 us (1%)
    ppermute x12, waiting for transfers between devices, along_z(): return lax.ppermute(value, 'z', [(i, (i + shift) % 8) for i in range(8)])  40.4 us
    dot_general x11, matrix products, product(): total += jnp.dot(features, piece, preferred_element_type=jnp.float32)  28.6 us
    ppermute x4, waiting for transfers between devices, along_y(): return lax.ppermute(value, 'y', [(i, (i + shift) % 4) for i in range(4)])  24.5 us
    ppermute x12, starting transfers between devices, along_z(): return lax.ppermute(value, 'z', [(i, (i + shift) % 8) for i in range(8)])  18.1 us
    ppermute x5, waiting for transfers between devices, exchange(): return lax.ppermute(value, axis, [(i, i ^ flip) for i in range(size)])  16.5 us
    ppermute x2, waiting for transfers between devices, home(): return lax.ppermute(out, ('xh', 'core'), HOME)  15 us
    ppermute x2, waiting for transfers between devices, swapped(): turned = lax.ppermute(first, ('xh', 'core'), TURN)  10.8 us
    ppermute x2, starting transfers between devices, swapped(): turned = lax.ppermute(first, ('xh', 'core'), TURN)  8.8 us
  transfers between devices with their start and end apart: 27, of which 15 were waited for; matrix products, arithmetic and copies ran while one was open for 18% of the time, Pallas kernels for 1%

profile of v10, /device:TPU:1, one launch (start us, length us, event | category | flops | bytes accessed | tf_op | source)
XLA Modules:
  0.0 204.2 jit_solution(13925792755449088341)
XLA Ops:
  1.2 3.7 %collective-permute-start = (bf16[256,768]{1,0:T(8,128)(2,1)S(1)}, bf16[256,768]{1,0:T(8,128)(2,1)S(1)}, u32[]{:S(2)}, u32[]{:S(2)}) collective-permute-start(bf16[256,768]{1,0:T(8,128)(2,1)S(1)} %get-tuple-element.73), channel_id=1, source_target_pairs={{0,1},{1,129},{128,0},{129,128},{2,3},{3,131},{130,2},{131,130},{4... | collective-permute-start | bytes 1179656 | tf_op jit(solution)/shard_map/ppermute | solution.py:109
  4.8 4.7 %collective-permute-start.1 = (bf16[256,768]{1,0:T(8,128)(2,1)S(1)}, bf16[256,768]{1,0:T(8,128)(2,1)S(1)}, u32[]{:S(2)}, u32[]{:S(2)}) collective-permute-start(bf16[256,768]{1,0:T(8,128)(2,1)S(1)} %get-tuple-element.74), channel_id=1, source_target_pairs={{0,0},{1,128},{128,1},{129,129},{2,2},{3,130},{130,3},{131,131},{4... | collective-permute-start | bytes 1179656 | tf_op jit(solution)/shard_map/ppermute | solution.py:108
  9.6 7.7 %collective-permute-done.1 = bf16[256,768]{1,0:T(8,128)(2,1)S(1)} collective-permute-done((bf16[256,768]{1,0:T(8,128)(2,1)S(1)}, bf16[256,768]{1,0:T(8,128)(2,1)S(1)}, u32[]{:S(2)}, u32[]{:S(2)}) %collective-permute-start.1) | collective-permute-done | bytes 393248 | tf_op jit(solution)/shard_map/ppermute | solution.py:108
  17.7 3.9 %collective-permute-start.5 = (bf16[512,768]{1,0:T(8,128)(2,1)S(1)}, bf16[512,768]{1,0:T(8,128)(2,1)S(1)}, u32[]{:S(2)}, u32[]{:S(2)}) collective-permute-start(bf16[512,768]{1,0:T(8,128)(2,1)S(1)} %pad_maximum_fusion.3), channel_id=1, source_target_pairs={{0,112},{16,0},{32,16},{48,32},{64,48},{80,64},{96,80},{112,96},{1... | collective-permute-start | bytes 2359304 | tf_op jit(solution)/shard_map/ppermute | solution.py:89
  25.0 4.1 %collective-permute-start.7 = (bf16[256,896]{1,0:T(8,128)(2,1)S(1)}, bf16[256,896]{1,0:T(8,128)(2,1)S(1)}, u32[]{:S(2)}, u32[]{:S(2)}) collective-permute-start(bf16[256,896]{1,0:T(8,128)(2,1)S(1)} %get-tuple-element.78), channel_id=1, source_target_pairs={{0,0},{1,128},{128,1},{129,129},{2,2},{3,130},{130,3},{131,131},{4... | collective-permute-start | bytes 1376264 | tf_op jit(solution)/shard_map/ppermute | solution.py:108
  31.8 7.3 %collective-permute-done.4 = bf16[512,768]{1,0:T(8,128)(2,1)S(1)} collective-permute-done((bf16[512,768]{1,0:T(8,128)(2,1)S(1)}, bf16[512,768]{1,0:T(8,128)(2,1)S(1)}, u32[]{:S(2)}, u32[]{:S(2)}) %collective-permute-start.4) | collective-permute-done | bytes 786464 | tf_op jit(solution)/shard_map/ppermute | solution.py:89
  41.6 3.1 %collective-permute-done.7 = bf16[256,896]{1,0:T(8,128)(2,1)S(1)} collective-permute-done((bf16[256,896]{1,0:T(8,128)(2,1)S(1)}, bf16[256,896]{1,0:T(8,128)(2,1)S(1)}, u32[]{:S(2)}, u32[]{:S(2)}) %collective-permute-start.7) | collective-permute-done | bytes 458784 | tf_op jit(solution)/shard_map/ppermute | solution.py:108
  47.6 12.3 %collective-permute-done.12 = bf16[376,1024]{1,0:T(8,128)(2,1)S(1)} collective-permute-done((bf16[376,1024]{1,0:T(8,128)(2,1)S(1)}, bf16[376,1024]{1,0:T(8,128)(2,1)S(1)}, u32[]{:S(2)}, u32[]{:S(2)}) %collective-permute-start.12) | collective-permute-done | bytes 770080 | tf_op jit(solution)/shard_map/ppermute | solution.py:19
  67.9 3.0 %collective-permute-start.11 = (bf16[512,1664]{1,0:T(8,128)(2,1)}, bf16[512,1664]{1,0:T(8,128)(2,1)}, u32[]{:S(2)}, u32[]{:S(2)}) collective-permute-start(bf16[512,1664]{1,0:T(8,128)(2,1)} %constant_dynamic-update-slice_fusion.2), channel_id=1, source_target_pairs={{0,112},{16,0},{32,16},{48,32},{64,48},{80,64},{96,80},{112,96},{1... | collective-permute-start | bytes 5111816 | tf_op jit(solution)/shard_map/ppermute | solution.py:89
  71.9 23.7 %collective-permute-done.13.up = bf16[2,376,1024]{2,1,0:T(8,128)(2,1)S(1)} collective-permute-done((bf16[2,376,1024]{2,1,0:T(8,128)(2,1)S(1)}, bf16[2,376,1024]{2,1,0:T(8,128)(2,1)S(1)}, u32[]{:S(2)}, u32[]{:S(2)}) %collective-permute-start.13) | collective-permute-done | bytes 1540128 | tf_op jit(solution)/shard_map/ppermute | solution.py:44
  98.6 2.7 %collective-permute-start.16 = (bf16[376,1024]{1,0:T(8,128)(2,1)}, bf16[376,1024]{1,0:T(8,128)(2,1)}, u32[]{:S(2)}, u32[]{:S(2)}) collective-permute-start(bf16[376,1024]{1,0:T(8,128)(2,1)} %slice_bitcast_fusion), channel_id=1, source_target_pairs={{0,6},{2,0},{4,2},{6,4},{1,7},{3,1},{5,3},{7,5},{8,14},{10,8},{12,... | collective-permute-start | bytes 2310152 | tf_op jit(solution)/shard_map/ppermute | solution.py:44
  101.3 6.3 %collective-permute-done.11 = bf16[512,1664]{1,0:T(8,128)(2,1)} collective-permute-done((bf16[512,1664]{1,0:T(8,128)(2,1)}, bf16[512,1664]{1,0:T(8,128)(2,1)}, u32[]{:S(2)}, u32[]{:S(2)}) %collective-permute-start.11) | collective-permute-done | bytes 1703968 | tf_op jit(solution)/shard_map/ppermute | solution.py:89
  107.6 4.7 %collective-permute-done.10 = bf16[512,1664]{1,0:T(8,128)(2,1)} collective-permute-done((bf16[512,1664]{1,0:T(8,128)(2,1)}, bf16[512,1664]{1,0:T(8,128)(2,1)}, u32[]{:S(2)}, u32[]{:S(2)}) %collective-permute-start.10) | collective-permute-done | bytes 1703968 | tf_op jit(solution)/shard_map/ppermute | solution.py:89
  112.3 2.7 %collective-permute-start.18 = (bf16[512,1664]{1,0:T(8,128)(2,1)}, bf16[512,1664]{1,0:T(8,128)(2,1)}, u32[]{:S(2)}, u32[]{:S(2)}) collective-permute-start(bf16[512,1664]{1,0:T(8,128)(2,1)} %collective-permute-done.11), channel_id=1, source_target_pairs={{0,112},{16,0},{32,16},{48,32},{64,48},{80,64},{96,80},{112,96},{1... | collective-permute-start | bytes 5111816 | tf_op jit(solution)/shard_map/ppermute | solution.py:89
  119.9 3.0 %fusion.17 = f32[752,1664]{1,0:T(8,128)S(1)} fusion(bf16[512,1664]{1,0:T(8,128)(2,1)} %constant_dynamic-update-slice_fusion, bf16[752,4096]{1,0:T(8,128)(2,1)S(1)} %bitcast.19), kind=kOutput, calls=%fused_computation.27 | convolution fusion | flops 1281359872 | bytes 7479296 | tf_op jit(solution)/shard_map/dot_general | solution.py:100
  122.9 3.1 %fusion.15 = f32[752,1664]{1,0:T(8,128)S(1)} fusion(bf16[512,1664]{1,0:T(8,128)(2,1)} %constant_dynamic-update-slice_fusion.2, bf16[752,4096]{1,0:T(8,128)(2,1)S(1)} %bitcast.20), kind=kOutput, calls=%fused_computation.25 | convolution fusion | flops 1281359872 | bytes 7479296 | tf_op jit(solution)/shard_map/dot_general | solution.py:100
  126.0 3.8 %fusion = f32[752,1664]{1,0:T(8,128)} fusion(bf16[256,896]{1,0:T(8,128)(2,1)S(1)} %copy-done.3, bf16[256,896]{1,0:T(8,128)(2,1)S(1)} %get-tuple-element.75, bf16[512,768]{1,0:T(8,128)(2,1)S(1)} %copy-done.6, bf16[752,4096]{1,0:T(8,128)(2,1)S(1)} %bitcast.21), kind=kOutput, calls=%fused_computation.4 | convolution fusion | flops 1286471680 | bytes 7479296 | tf_op jit(solution)/shard_map/dot_general | solution.py:100
  129.9 3.0 %fusion.13 = f32[752,1664]{1,0:T(8,128)S(1)} fusion(bf16[512,1664]{1,0:T(8,128)(2,1)} %collective-permute-done.10, bf16[752,4096]{1,0:T(8,128)(2,1)S(1)} %bitcast.22), kind=kOutput, calls=%fused_computation.23 | convolution fusion | flops 1281359872 | bytes 7479296 | tf_op jit(solution)/shard_map/dot_general | solution.py:100
  132.9 7.2 %add_add_fusion.1 = f32[752,1664]{1,0:T(8,128)} fusion(f32[752,1664]{1,0:T(8,128)S(1)} %fusion.13, f32[752,1664]{1,0:T(8,128)S(1)} %fusion.15, f32[752,1664]{1,0:T(8,128)} %fusion, f32[752,1664]{1,0:T(8,128)S(1)} %fusion.17, bf16[512,1664]{1,0:T(8,128)(2,1)} %collective-permute-done.11, bf16[752,4096]{1,0:T(8,128)(2,1)S(1)} %bitcast.23), kind=kOutput, calls=%fused_computation.1 | convolution fusion | flops 1286365184 | bytes 27500544 | tf_op jit(solution)/shard_map/dot_general | solution.py:100
  140.1 12.5 %collective-permute-done.17 = bf16[512,1664]{1,0:T(8,128)(2,1)} collective-permute-done((bf16[512,1664]{1,0:T(8,128)(2,1)}, bf16[512,1664]{1,0:T(8,128)(2,1)}, u32[]{:S(2)}, u32[]{:S(2)}) %collective-permute-start.17) | collective-permute-done | bytes 1703968 | tf_op jit(solution)/shard_map/ppermute | solution.py:89
  159.9 3.0 %fusion.7 = f32[752,1664]{1,0:T(8,128)S(1)} fusion(bf16[512,1664]{1,0:T(8,128)(2,1)} %collective-permute-done.17, bf16[752,4096]{1,0:T(8,128)(2,1)S(1)} %bitcast.24), kind=kOutput, calls=%fused_computation.19 | convolution fusion | flops 1281359872 | bytes 7479296 | tf_op jit(solution)/shard_map/dot_general | solution.py:100
  165.9 3.2 %add_add_fusion = f32[752,1664]{1,0:T(8,128)S(1)} fusion(f32[752,1664]{1,0:T(8,128)S(1)} %bitcast.31, f32[752,1664]{1,0:T(8,128)S(1)} %fusion.7, bf16[512,1664]{1,0:T(8,128)(2,1)} %collective-permute-done.18, bf16[752,4096]{1,0:T(8,128)(2,1)S(1)} %bitcast.25), kind=kOutput, calls=%fused_computation | convolution fusion | flops 1283862528 | bytes 17489920 | tf_op jit(solution)/shard_map/dot_general | solution.py:100
  172.2 5.8 %collective-permute-done.21 = bf16[256,640]{1,0:T(8,128)(2,1)S(1)} collective-permute-done((bf16[256,640]{1,0:T(8,128)(2,1)S(1)}, bf16[256,640]{1,0:T(8,128)(2,1)S(1)}, u32[]{:S(2)}, u32[]{:S(2)}) %collective-permute-start.21) | collective-permute-done | bytes 327712 | tf_op jit(solution)/shard_map/ppermute | solution.py:89
  188.0 15.0 %collective-permute-done.26 = bf16[376,640]{1,0:T(8,128)(2,1)S(1)} collective-permute-done((bf16[376,640]{1,0:T(8,128)(2,1)S(1)}, bf16[376,640]{1,0:T(8,128)(2,1)S(1)}, u32[]{:S(2)}, u32[]{:S(2)}) %collective-permute-start.26) | collective-permute-done | bytes 481312 | tf_op jit(solution)/shard_map/ppermute | solution.py:122
  (92 shorter events, 54.4 us)
Async XLA Ops:
  1.2 8.4 %collective-permute-start = (bf16[256,768]{1,0:T(8,128)(2,1)S(1)}, bf16[256,768]{1,0:T(8,128)(2,1)S(1)}, u32[]{:S(2)}, u32[]{:S(2)}) collective-permute-start(bf16[256,768]{1,0:T(8,128)(2,1)S(1)} %get-tuple-element.73), channel_id=1, source_target_pairs={{0,1},{1,129},{128,0},{129,128},{2,3},{3,131},{130,2},{131,130},{4... | collective-permute-start | bytes 1179656 | tf_op jit(solution)/shard_map/ppermute | solution.py:109
  4.8 12.5 %collective-permute-start.1 = (bf16[256,768]{1,0:T(8,128)(2,1)S(1)}, bf16[256,768]{1,0:T(8,128)(2,1)S(1)}, u32[]{:S(2)}, u32[]{:S(2)}) collective-permute-start(bf16[256,768]{1,0:T(8,128)(2,1)S(1)} %get-tuple-element.74), channel_id=1, source_target_pairs={{0,0},{1,128},{128,1},{129,129},{2,2},{3,130},{130,3},{131,131},{4... | collective-permute-start | bytes 1179656 | tf_op jit(solution)/shard_map/ppermute | solution.py:108
  17.6 21.5 %collective-permute-start.4 = (bf16[512,768]{1,0:T(8,128)(2,1)S(1)}, bf16[512,768]{1,0:T(8,128)(2,1)S(1)}, u32[]{:S(2)}, u32[]{:S(2)}) collective-permute-start(bf16[512,768]{1,0:T(8,128)(2,1)S(1)} %pad_maximum_fusion.3), channel_id=1, source_target_pairs={{0,16},{16,32},{32,48},{48,64},{64,80},{80,96},{96,112},{112,0},{1... | collective-permute-start | bytes 2359304 | tf_op jit(solution)/shard_map/ppermute | solution.py:89
  17.7 21.4 %collective-permute-start.5 = (bf16[512,768]{1,0:T(8,128)(2,1)S(1)}, bf16[512,768]{1,0:T(8,128)(2,1)S(1)}, u32[]{:S(2)}, u32[]{:S(2)}) collective-permute-start(bf16[512,768]{1,0:T(8,128)(2,1)S(1)} %pad_maximum_fusion.3), channel_id=1, source_target_pairs={{0,112},{16,0},{32,16},{48,32},{64,48},{80,64},{96,80},{112,96},{1... | collective-permute-start | bytes 2359304 | tf_op jit(solution)/shard_map/ppermute | solution.py:89
  21.7 10.0 %collective-permute-start.3 = (bf16[376,512]{1,0:T(8,128)(2,1)S(1)}, bf16[376,512]{1,0:T(8,128)(2,1)S(1)}, u32[]{:S(2)}, u32[]{:S(2)}) collective-permute-start(bf16[376,512]{1,0:T(8,128)(2,1)S(1)} %pad_maximum_fusion.5), channel_id=1, source_target_pairs={{0,8},{8,0},{1,9},{9,1},{2,10},{10,2},{3,11},{11,3},{4,12},{12,4},... | collective-permute-start | bytes 1155080 | tf_op jit(solution)/shard_map/ppermute | solution.py:19
  23.1 18.5 %collective-permute-start.6 = (bf16[256,896]{1,0:T(8,128)(2,1)S(1)}, bf16[256,896]{1,0:T(8,128)(2,1)S(1)}, u32[]{:S(2)}, u32[]{:S(2)}) collective-permute-start(bf16[256,896]{1,0:T(8,128)(2,1)S(1)} %get-tuple-element.77), channel_id=1, source_target_pairs={{0,1},{1,129},{128,0},{129,128},{2,3},{3,131},{130,2},{131,130},{4... | collective-permute-start | bytes 1376264 | tf_op jit(solution)/shard_map/ppermute | solution.py:109
  25.0 19.6 %collective-permute-start.7 = (bf16[256,896]{1,0:T(8,128)(2,1)S(1)}, bf16[256,896]{1,0:T(8,128)(2,1)S(1)}, u32[]{:S(2)}, u32[]{:S(2)}) collective-permute-start(bf16[256,896]{1,0:T(8,128)(2,1)S(1)} %get-tuple-element.78), channel_id=1, source_target_pairs={{0,0},{1,128},{128,1},{129,129},{2,2},{3,130},{130,3},{131,131},{4... | collective-permute-start | bytes 1376264 | tf_op jit(solution)/shard_map/ppermute | solution.py:108
  39.1 20.8 %collective-permute-start.12 = (bf16[376,1024]{1,0:T(8,128)(2,1)S(1)}, bf16[376,1024]{1,0:T(8,128)(2,1)S(1)}, u32[]{:S(2)}, u32[]{:S(2)}) collective-permute-start(bf16[376,1024]{1,0:T(8,128)(2,1)S(1)} %pad_maximum_fusion.4), channel_id=1, source_target_pairs={{0,128},{128,0},{1,129},{129,1},{2,130},{130,2},{3,131},{131,3},{4... | collective-permute-start | bytes 2310152 | tf_op jit(solution)/shard_map/ppermute | solution.py:19
  44.8 22.0 %collective-permute-start.8 = (bf16[512,896]{1,0:T(8,128)(2,1)S(1)}, bf16[512,896]{1,0:T(8,128)(2,1)S(1)}, u32[]{:S(2)}, u32[]{:S(2)}) collective-permute-start(bf16[512,896]{1,0:T(8,128)(2,1)S(1)} %pad_maximum_fusion.2), channel_id=1, source_target_pairs={{0,16},{16,32},{32,48},{48,64},{64,80},{80,96},{96,112},{112,0},{1... | collective-permute-start | bytes 2752520 | tf_op jit(solution)/shard_map/ppermute | solution.py:89
  44.9 21.9 %collective-permute-start.9 = (bf16[512,896]{1,0:T(8,128)(2,1)S(1)}, bf16[512,896]{1,0:T(8,128)(2,1)S(1)}, u32[]{:S(2)}, u32[]{:S(2)}) collective-permute-start(bf16[512,896]{1,0:T(8,128)(2,1)S(1)} %pad_maximum_fusion.2), channel_id=1, source_target_pairs={{0,112},{16,0},{32,16},{48,32},{64,48},{80,64},{96,80},{112,96},{1... | collective-permute-start | bytes 2752520 | tf_op jit(solution)/shard_map/ppermute | solution.py:89
  60.0 35.5 %collective-permute-start.13 = (bf16[2,376,1024]{2,1,0:T(8,128)(2,1)S(1)}, bf16[2,376,1024]{2,1,0:T(8,128)(2,1)S(1)}, u32[]{:S(2)}, u32[]{:S(2)}) collective-permute-start(bf16[2,376,1024]{2,1,0:T(8,128)(2,1)S(1)} %pad_maximum_fusion.here), channel_id=1, source_target_pairs={{0,2},{2,4},{4,6},{6,0},{1,3},{3,5},{5,7},{7,1},{8,10},{10,12},{12... | collective-permute-start | bytes 4620296 | tf_op jit(solution)/shard_map/ppermute | solution.py:44
  61.4 35.1 %collective-permute-start.14 = (bf16[2,376,1024]{2,1,0:T(8,128)(2,1)S(1)}, bf16[2,376,1024]{2,1,0:T(8,128)(2,1)S(1)}, u32[]{:S(2)}, u32[]{:S(2)}) collective-permute-start(bf16[2,376,1024]{2,1,0:T(8,128)(2,1)S(1)} %pad_maximum_fusion.here), channel_id=1, source_target_pairs={{0,6},{2,0},{4,2},{6,4},{1,7},{3,1},{5,3},{7,5},{8,14},{10,8},{12,... | collective-permute-start | bytes 4620296 | tf_op jit(solution)/shard_map/ppermute | solution.py:44
  67.9 39.7 %collective-permute-start.11 = (bf16[512,1664]{1,0:T(8,128)(2,1)}, bf16[512,1664]{1,0:T(8,128)(2,1)}, u32[]{:S(2)}, u32[]{:S(2)}) collective-permute-start(bf16[512,1664]{1,0:T(8,128)(2,1)} %constant_dynamic-update-slice_fusion.2), channel_id=1, source_target_pairs={{0,112},{16,0},{32,16},{48,32},{64,48},{80,64},{96,80},{112,96},{1... | collective-permute-start | bytes 5111816 | tf_op jit(solution)/shard_map/ppermute | solution.py:89
  71.9 40.4 %collective-permute-start.10 = (bf16[512,1664]{1,0:T(8,128)(2,1)}, bf16[512,1664]{1,0:T(8,128)(2,1)}, u32[]{:S(2)}, u32[]{:S(2)}) collective-permute-start(bf16[512,1664]{1,0:T(8,128)(2,1)} %constant_dynamic-update-slice_fusion), channel_id=1, source_target_pairs={{0,16},{16,32},{32,48},{48,64},{64,80},{80,96},{96,112},{112,0},{1... | collective-permute-start | bytes 5111816 | tf_op jit(solution)/shard_map/ppermute | solution.py:89
  96.5 18.5 %collective-permute-start.15 = (bf16[376,1024]{1,0:T(8,128)(2,1)}, bf16[376,1024]{1,0:T(8,128)(2,1)}, u32[]{:S(2)}, u32[]{:S(2)}) collective-permute-start(bf16[376,1024]{1,0:T(8,128)(2,1)} %slice_bitcast_fusion.1), channel_id=1, source_target_pairs={{0,2},{2,4},{4,6},{6,0},{1,3},{3,5},{5,7},{7,1},{8,10},{10,12},{12... | collective-permute-start | bytes 2310152 | tf_op jit(solution)/shard_map/ppermute | solution.py:44
  98.6 17.3 %collective-permute-start.16 = (bf16[376,1024]{1,0:T(8,128)(2,1)}, bf16[376,1024]{1,0:T(8,128)(2,1)}, u32[]{:S(2)}, u32[]{:S(2)}) collective-permute-start(bf16[376,1024]{1,0:T(8,128)(2,1)} %slice_bitcast_fusion), channel_id=1, source_target_pairs={{0,6},{2,0},{4,2},{6,4},{1,7},{3,1},{5,3},{7,5},{8,14},{10,8},{12,... | collective-permute-start | bytes 2310152 | tf_op jit(solution)/shard_map/ppermute | solution.py:44
  112.3 40.3 %collective-permute-start.17 = (bf16[512,1664]{1,0:T(8,128)(2,1)}, bf16[512,1664]{1,0:T(8,128)(2,1)}, u32[]{:S(2)}, u32[]{:S(2)}) collective-permute-start(bf16[512,1664]{1,0:T(8,128)(2,1)} %collective-permute-done.10), channel_id=1, source_target_pairs={{0,16},{16,32},{32,48},{48,64},{64,80},{80,96},{96,112},{112,0},{1... | collective-permute-start | bytes 5111816 | tf_op jit(solution)/shard_map/ppermute | solution.py:89
  112.3 40.3 %collective-permute-start.18 = (bf16[512,1664]{1,0:T(8,128)(2,1)}, bf16[512,1664]{1,0:T(8,128)(2,1)}, u32[]{:S(2)}, u32[]{:S(2)}) collective-permute-start(bf16[512,1664]{1,0:T(8,128)(2,1)} %collective-permute-done.11), channel_id=1, source_target_pairs={{0,112},{16,0},{32,16},{48,32},{64,48},{80,64},{96,80},{112,96},{1... | collective-permute-start | bytes 5111816 | tf_op jit(solution)/shard_map/ppermute | solution.py:89
  157.1 13.9 %collective-permute-start.19 = (bf16[256,1024]{1,0:T(8,128)(2,1)S(1)}, bf16[256,1024]{1,0:T(8,128)(2,1)S(1)}, u32[]{:S(2)}, u32[]{:S(2)}) collective-permute-start(bf16[256,1024]{1,0:T(8,128)(2,1)S(1)} %slice.125), channel_id=1, source_target_pairs={{0,16},{16,32},{32,48},{48,64},{64,80},{80,96},{96,112},{112,0},{1... | collective-permute-start | bytes 1572872 | tf_op jit(solution)/shard_map/ppermute | solution.py:89
  157.2 13.8 %collective-permute-start.20 = (bf16[256,1024]{1,0:T(8,128)(2,1)S(1)}, bf16[256,1024]{1,0:T(8,128)(2,1)S(1)}, u32[]{:S(2)}, u32[]{:S(2)}) collective-permute-start(bf16[256,1024]{1,0:T(8,128)(2,1)S(1)} %slice.126), channel_id=1, source_target_pairs={{0,112},{16,0},{32,16},{48,32},{64,48},{80,64},{96,80},{112,96},{1... | collective-permute-start | bytes 1572872 | tf_op jit(solution)/shard_map/ppermute | solution.py:89
  162.9 15.1 %collective-permute-start.21 = (bf16[256,640]{1,0:T(8,128)(2,1)S(1)}, bf16[256,640]{1,0:T(8,128)(2,1)S(1)}, u32[]{:S(2)}, u32[]{:S(2)}) collective-permute-start(bf16[256,640]{1,0:T(8,128)(2,1)S(1)} %slice.120), channel_id=1, source_target_pairs={{0,16},{16,32},{32,48},{48,64},{64,80},{80,96},{96,112},{112,0},{1... | collective-permute-start | bytes 983048 | tf_op jit(solution)/shard_map/ppermute | solution.py:89
  163.2 14.8 %collective-permute-start.22 = (bf16[256,640]{1,0:T(8,128)(2,1)S(1)}, bf16[256,640]{1,0:T(8,128)(2,1)S(1)}, u32[]{:S(2)}, u32[]{:S(2)}) collective-permute-start(bf16[256,640]{1,0:T(8,128)(2,1)S(1)} %slice.121), channel_id=1, source_target_pairs={{0,112},{16,0},{32,16},{48,32},{64,48},{80,64},{96,80},{112,96},{1... | collective-permute-start | bytes 983048 | tf_op jit(solution)/shard_map/ppermute | solution.py:89
  183.8 19.2 %collective-permute-start.24 = (bf16[376,1024]{1,0:T(8,128)(2,1)S(1)}, bf16[376,1024]{1,0:T(8,128)(2,1)S(1)}, u32[]{:S(2)}, u32[]{:S(2)}) collective-permute-start(bf16[376,1024]{1,0:T(8,128)(2,1)S(1)} %multiply_convert_fusion), channel_id=1, source_target_pairs={{0,0},{1,128},{128,129},{129,1},{2,2},{3,130},{130,131},{131,3},{4... | collective-permute-start | bytes 2310152 | tf_op jit(solution)/shard_map/ppermute | solution.py:122
  186.1 17.0 %collective-permute-start.26 = (bf16[376,640]{1,0:T(8,128)(2,1)S(1)}, bf16[376,640]{1,0:T(8,128)(2,1)S(1)}, u32[]{:S(2)}, u32[]{:S(2)}) collective-permute-start(bf16[376,640]{1,0:T(8,128)(2,1)S(1)} %multiply_convert_fusion.1), channel_id=1, source_target_pairs={{0,0},{1,128},{128,129},{129,1},{2,2},{3,130},{130,131},{131,3},{4... | collective-permute-start | bytes 1443848 | tf_op jit(solution)/shard_map/ppermute | solution.py:122
  (13 other events, 83.4 us)

commit v11 on v10

--- a/solution.py
+++ b/solution.py
@@ -7,7 +7,7 @@
 
 AXES = ("xh", "z", "xl", "y", "core")
 SIZES = (2, 8, 2, 4, 2)
-FIRST = 768
+FIRST = 896
 LAST = 1024
 
 TURN = [(h * 2 + c, c * 2 + h) for h in range(2) for c in range(2)]

time: 205 us -> 229 us (1.12)
  waiting for transfers between devices: 107 us -> 131 us
    ppermute x12, waiting for transfers between devices: 40.4 us -> 64 us  [along_z(): return lax.ppermute(value, 'z', [(i, (i + shift) % 8) for i in range(8)])]
    ppermute x2, waiting for transfers between devices: 0.01 us -> 15.8 us  [swapped(): crossed = lax.ppermute(second, ('xh', 'core'), CROSS)]
    ppermute x4, waiting for transfers between devices: 24.5 us -> 12.3 us  [along_y(): return lax.ppermute(value, 'y', [(i, (i + shift) % 4) for i in range(4)])]
    ppermute x5, waiting for transfers between devices: 16.5 us -> 10.4 us  [exchange(): return lax.ppermute(value, axis, [(i, i ^ flip) for i in range(size)])]
    ppermute x2, waiting for transfers between devices: 10.8 us -> 13.6 us  [swapped(): turned = lax.ppermute(first, ('xh', 'core'), TURN)]
  transfers between devices with their start and end apart: 27 -> 27, of which waited for: 15 -> 16; matrix products, arithmetic and copies ran while one was open for 18% -> 16% of each run, Pallas kernels for 1% -> 1%
where the time goes in v11:
time: 229 us; the launch traced here: 228 us
  waiting for transfers between devices  131 us (57%)
  starting transfers between devices  47.9 us (21%)
  matrix products  28.6 us (12%)
  local copies, waits for them, and re-layouts  13 us (6%)
  other arithmetic  4.53 us (2%)
  Pallas kernels  2.63 us (1%)
    ppermute x12, waiting for transfers between devices, along_z(): return lax.ppermute(value, 'z', [(i, (i + shift) % 8) for i in range(8)])  64 us
    dot_general x11, matrix products, product(): total += jnp.dot(features, piece, preferred_element_type=jnp.float32)  28.6 us
    ppermute x12, starting transfers between devices, along_z(): return lax.ppermute(value, 'z', [(i, (i + shift) % 8) for i in range(8)])  18.6 us
    ppermute x2, waiting for transfers between devices, swapped(): crossed = lax.ppermute(second, ('xh', 'core'), CROSS)  15.8 us
    ppermute x2, waiting for transfers between devices, home(): return lax.ppermute(out, ('xh', 'core'), HOME)  15 us
    ppermute x2, waiting for transfers between devices, swapped(): turned = lax.ppermute(first, ('xh', 'core'), TURN)  13.6 us
    ppermute x4, waiting for transfers between devices, along_y(): return lax.ppermute(value, 'y', [(i, (i + shift) % 4) for i in range(4)])  12.3 us
    ppermute x5, waiting for transfers between devices, exchange(): return lax.ppermute(value, axis, [(i, i ^ flip) for i in range(size)])  10.4 us
  transfers between devices with their start and end apart: 27, of which 16 were waited for; matrix products, arithmetic and copies ran while one was open for 16% of the time, Pallas kernels for 1%

profile of v11, /device:TPU:1, one launch (start us, length us, event | category | flops | bytes accessed | tf_op | source)
XLA Modules:
  0.0 228.2 jit_solution(16767334031833291707)
XLA Ops:
  1.2 3.7 %collective-permute-start = (bf16[256,896]{1,0:T(8,128)(2,1)S(1)}, bf16[256,896]{1,0:T(8,128)(2,1)S(1)}, u32[]{:S(2)}, u32[]{:S(2)}) collective-permute-start(bf16[256,896]{1,0:T(8,128)(2,1)S(1)} %get-tuple-element.73), channel_id=1, source_target_pairs={{0,1},{1,129},{128,0},{129,128},{2,3},{3,131},{130,2},{131,130},{4... | collective-permute-start | bytes 1376264 | tf_op jit(solution)/shard_map/ppermute | solution.py:109
  4.9 4.7 %collective-permute-start.1 = (bf16[256,896]{1,0:T(8,128)(2,1)S(1)}, bf16[256,896]{1,0:T(8,128)(2,1)S(1)}, u32[]{:S(2)}, u32[]{:S(2)}) collective-permute-start(bf16[256,896]{1,0:T(8,128)(2,1)S(1)} %get-tuple-element.74), channel_id=1, source_target_pairs={{0,0},{1,128},{128,1},{129,129},{2,2},{3,130},{130,3},{131,131},{4... | collective-permute-start | bytes 1376264 | tf_op jit(solution)/shard_map/ppermute | solution.py:108
  10.3 8.5 %collective-permute-done.1 = bf16[256,896]{1,0:T(8,128)(2,1)S(1)} collective-permute-done((bf16[256,896]{1,0:T(8,128)(2,1)S(1)}, bf16[256,896]{1,0:T(8,128)(2,1)S(1)}, u32[]{:S(2)}, u32[]{:S(2)}) %collective-permute-start.1) | collective-permute-done | bytes 458784 | tf_op jit(solution)/shard_map/ppermute | solution.py:108
  19.2 3.9 %collective-permute-start.5 = (bf16[512,896]{1,0:T(8,128)(2,1)S(1)}, bf16[512,896]{1,0:T(8,128)(2,1)S(1)}, u32[]{:S(2)}, u32[]{:S(2)}) collective-permute-start(bf16[512,896]{1,0:T(8,128)(2,1)S(1)} %pad_maximum_fusion.2), channel_id=1, source_target_pairs={{0,112},{16,0},{32,16},{48,32},{64,48},{80,64},{96,80},{112,96},{1... | collective-permute-start | bytes 2752520 | tf_op jit(solution)/shard_map/ppermute | solution.py:89
  24.6 8.6 %collective-permute-done.3 = bf16[376,512]{1,0:T(8,128)(2,1)S(1)} collective-permute-done((bf16[376,512]{1,0:T(8,128)(2,1)S(1)}, bf16[376,512]{1,0:T(8,128)(2,1)S(1)}, u32[]{:S(2)}, u32[]{:S(2)}) %collective-permute-start.3) | collective-permute-done | bytes 385056 | tf_op jit(solution)/shard_map/ppermute | solution.py:19
  33.3 10.1 %collective-permute-done.4 = bf16[512,896]{1,0:T(8,128)(2,1)S(1)} collective-permute-done((bf16[512,896]{1,0:T(8,128)(2,1)S(1)}, bf16[512,896]{1,0:T(8,128)(2,1)S(1)}, u32[]{:S(2)}, u32[]{:S(2)}) %collective-permute-start.4) | collective-permute-done | bytes 917536 | tf_op jit(solution)/shard_map/ppermute | solution.py:89
  46.5 5.5 %collective-permute-start.7 = (bf16[256,768]{1,0:T(8,128)(2,1)S(1)}, bf16[256,768]{1,0:T(8,128)(2,1)S(1)}, u32[]{:S(2)}, u32[]{:S(2)}) collective-permute-start(bf16[256,768]{1,0:T(8,128)(2,1)S(1)} %get-tuple-element.80), channel_id=1, source_target_pairs={{0,0},{1,128},{128,1},{129,129},{2,2},{3,130},{130,3},{131,131},{4... | collective-permute-start | bytes 1179656 | tf_op jit(solution)/shard_map/ppermute | solution.py:108
  52.0 15.1 %collective-permute-done.6 = bf16[256,768]{1,0:T(8,128)(2,1)S(1)} collective-permute-done((bf16[256,768]{1,0:T(8,128)(2,1)S(1)}, bf16[256,768]{1,0:T(8,128)(2,1)S(1)}, u32[]{:S(2)}, u32[]{:S(2)}) %collective-permute-start.6) | collective-permute-done | bytes 393248 | tf_op jit(solution)/shard_map/ppermute | solution.py:109
  67.1 5.2 %collective-permute-done.7 = bf16[256,768]{1,0:T(8,128)(2,1)S(1)} collective-permute-done((bf16[256,768]{1,0:T(8,128)(2,1)S(1)}, bf16[256,768]{1,0:T(8,128)(2,1)S(1)}, u32[]{:S(2)}, u32[]{:S(2)}) %collective-permute-start.7) | collective-permute-done | bytes 393248 | tf_op jit(solution)/shard_map/ppermute | solution.py:108
  80.6 11.4 %collective-permute-done.8 = bf16[512,768]{1,0:T(8,128)(2,1)S(1)} collective-permute-done((bf16[512,768]{1,0:T(8,128)(2,1)S(1)}, bf16[512,768]{1,0:T(8,128)(2,1)S(1)}, u32[]{:S(2)}, u32[]{:S(2)}) %collective-permute-start.8) | collective-permute-done | bytes 786464 | tf_op jit(solution)/shard_map/ppermute | solution.py:89
  97.0 9.6 %collective-permute-done.13.up = bf16[2,376,1024]{2,1,0:T(8,128)(2,1)S(1)} collective-permute-done((bf16[2,376,1024]{2,1,0:T(8,128)(2,1)S(1)}, bf16[2,376,1024]{2,1,0:T(8,128)(2,1)S(1)}, u32[]{:S(2)}, u32[]{:S(2)}) %collective-permute-start.13) | collective-permute-done | bytes 1540128 | tf_op jit(solution)/shard_map/ppermute | solution.py:44
  115.2 16.4 %collective-permute-done.11 = bf16[512,1664]{1,0:T(8,128)(2,1)} collective-permute-done((bf16[512,1664]{1,0:T(8,128)(2,1)}, bf16[512,1664]{1,0:T(8,128)(2,1)}, u32[]{:S(2)}, u32[]{:S(2)}) %collective-permute-start.11) | collective-permute-done | bytes 1703968 | tf_op jit(solution)/shard_map/ppermute | solution.py:89
  131.6 4.4 %collective-permute-done.10 = bf16[512,1664]{1,0:T(8,128)(2,1)} collective-permute-done((bf16[512,1664]{1,0:T(8,128)(2,1)}, bf16[512,1664]{1,0:T(8,128)(2,1)}, u32[]{:S(2)}, u32[]{:S(2)}) %collective-permute-start.10) | collective-permute-done | bytes 1703968 | tf_op jit(solution)/shard_map/ppermute | solution.py:89
  142.7 3.0 %fusion.17 = f32[752,1664]{1,0:T(8,128)S(1)} fusion(bf16[512,1664]{1,0:T(8,128)(2,1)} %constant_dynamic-update-slice_fusion, bf16[752,4096]{1,0:T(8,128)(2,1)S(1)} %bitcast.19), kind=kOutput, calls=%fused_computation.27 | convolution fusion | flops 1281359872 | bytes 7479296 | tf_op jit(solution)/shard_map/dot_general | solution.py:100
  145.7 3.1 %fusion.15 = f32[752,1664]{1,0:T(8,128)S(1)} fusion(bf16[512,1664]{1,0:T(8,128)(2,1)} %constant_dynamic-update-slice_fusion.2, bf16[752,4096]{1,0:T(8,128)(2,1)S(1)} %bitcast.20), kind=kOutput, calls=%fused_computation.25 | convolution fusion | flops 1281359872 | bytes 7479296 | tf_op jit(solution)/shard_map/dot_general | solution.py:100
  148.9 3.8 %fusion = f32[752,1664]{1,0:T(8,128)} fusion(bf16[256,768]{1,0:T(8,128)(2,1)S(1)} %copy-done.3, bf16[256,768]{1,0:T(8,128)(2,1)S(1)} %get-tuple-element.77, bf16[512,896]{1,0:T(8,128)(2,1)S(1)} %copy-done.6, bf16[752,4096]{1,0:T(8,128)(2,1)S(1)} %bitcast.21), kind=kOutput, calls=%fused_computation.4 | convolution fusion | flops 1286471680 | bytes 7479296 | tf_op jit(solution)/shard_map/dot_general | solution.py:100
  152.7 3.0 %fusion.13 = f32[752,1664]{1,0:T(8,128)S(1)} fusion(bf16[512,1664]{1,0:T(8,128)(2,1)} %collective-permute-done.10, bf16[752,4096]{1,0:T(8,128)(2,1)S(1)} %bitcast.22), kind=kOutput, calls=%fused_computation.23 | convolution fusion | flops 1281359872 | bytes 7479296 | tf_op jit(solution)/shard_map/dot_general | solution.py:100
  155.7 7.2 %add_add_fusion.1 = f32[752,1664]{1,0:T(8,128)} fusion(f32[752,1664]{1,0:T(8,128)S(1)} %fusion.13, f32[752,1664]{1,0:T(8,128)S(1)} %fusion.15, f32[752,1664]{1,0:T(8,128)} %fusion, f32[752,1664]{1,0:T(8,128)S(1)} %fusion.17, bf16[512,1664]{1,0:T(8,128)(2,1)} %collective-permute-done.11, bf16[752,4096]{1,0:T(8,128)(2,1)S(1)} %bitcast.23), kind=kOutput, calls=%fused_computation.1 | convolution fusion | flops 1286365184 | bytes 27500544 | tf_op jit(solution)/shard_map/dot_general | solution.py:100
  163.0 13.2 %collective-permute-done.17 = bf16[512,1664]{1,0:T(8,128)(2,1)} collective-permute-done((bf16[512,1664]{1,0:T(8,128)(2,1)}, bf16[512,1664]{1,0:T(8,128)(2,1)}, u32[]{:S(2)}, u32[]{:S(2)}) %collective-permute-start.17) | collective-permute-done | bytes 1703968 | tf_op jit(solution)/shard_map/ppermute | solution.py:89
  180.7 3.2 %collective-permute-start.20 = (bf16[256,1024]{1,0:T(8,128)(2,1)S(1)}, bf16[256,1024]{1,0:T(8,128)(2,1)S(1)}, u32[]{:S(2)}, u32[]{:S(2)}) collective-permute-start(bf16[256,1024]{1,0:T(8,128)(2,1)S(1)} %slice.126), channel_id=1, source_target_pairs={{0,112},{16,0},{32,16},{48,32},{64,48},{80,64},{96,80},{112,96},{1... | collective-permute-start | bytes 1572872 | tf_op jit(solution)/shard_map/ppermute | solution.py:89
  184.0 3.0 %fusion.7 = f32[752,1664]{1,0:T(8,128)S(1)} fusion(bf16[512,1664]{1,0:T(8,128)(2,1)} %collective-permute-done.17, bf16[752,4096]{1,0:T(8,128)(2,1)S(1)} %bitcast.24), kind=kOutput, calls=%fused_computation.19 | convolution fusion | flops 1281359872 | bytes 7479296 | tf_op jit(solution)/shard_map/dot_general | solution.py:100
  190.0 3.2 %add_add_fusion = f32[752,1664]{1,0:T(8,128)S(1)} fusion(f32[752,1664]{1,0:T(8,128)S(1)} %bitcast.31, f32[752,1664]{1,0:T(8,128)S(1)} %fusion.7, bf16[512,1664]{1,0:T(8,128)(2,1)} %collective-permute-done.18, bf16[752,4096]{1,0:T(8,128)(2,1)S(1)} %bitcast.25), kind=kOutput, calls=%fused_computation | convolution fusion | flops 1283862528 | bytes 17489920 | tf_op jit(solution)/shard_map/dot_general | solution.py:100
  197.1 5.8 %collective-permute-done.21 = bf16[256,640]{1,0:T(8,128)(2,1)S(1)} collective-permute-done((bf16[256,640]{1,0:T(8,128)(2,1)S(1)}, bf16[256,640]{1,0:T(8,128)(2,1)S(1)}, u32[]{:S(2)}, u32[]{:S(2)}) %collective-permute-start.21) | collective-permute-done | bytes 327712 | tf_op jit(solution)/shard_map/ppermute | solution.py:89
  212.0 15.0 %collective-permute-done.26 = bf16[376,640]{1,0:T(8,128)(2,1)S(1)} collective-permute-done((bf16[376,640]{1,0:T(8,128)(2,1)S(1)}, bf16[376,640]{1,0:T(8,128)(2,1)S(1)}, u32[]{:S(2)}, u32[]{:S(2)}) %collective-permute-start.26) | collective-permute-done | bytes 481312 | tf_op jit(solution)/shard_map/ppermute | solution.py:122
  (92 shorter events, 57.3 us)
Async XLA Ops:
  1.2 9.1 %collective-permute-start = (bf16[256,896]{1,0:T(8,128)(2,1)S(1)}, bf16[256,896]{1,0:T(8,128)(2,1)S(1)}, u32[]{:S(2)}, u32[]{:S(2)}) collective-permute-start(bf16[256,896]{1,0:T(8,128)(2,1)S(1)} %get-tuple-element.73), channel_id=1, source_target_pairs={{0,1},{1,129},{128,0},{129,128},{2,3},{3,131},{130,2},{131,130},{4... | collective-permute-start | bytes 1376264 | tf_op jit(solution)/shard_map/ppermute | solution.py:109
  4.9 13.9 %collective-permute-start.1 = (bf16[256,896]{1,0:T(8,128)(2,1)S(1)}, bf16[256,896]{1,0:T(8,128)(2,1)S(1)}, u32[]{:S(2)}, u32[]{:S(2)}) collective-permute-start(bf16[256,896]{1,0:T(8,128)(2,1)S(1)} %get-tuple-element.74), channel_id=1, source_target_pairs={{0,0},{1,128},{128,1},{129,129},{2,2},{3,130},{130,3},{131,131},{4... | collective-permute-start | bytes 1376264 | tf_op jit(solution)/shard_map/ppermute | solution.py:108
  19.1 24.3 %collective-permute-start.4 = (bf16[512,896]{1,0:T(8,128)(2,1)S(1)}, bf16[512,896]{1,0:T(8,128)(2,1)S(1)}, u32[]{:S(2)}, u32[]{:S(2)}) collective-permute-start(bf16[512,896]{1,0:T(8,128)(2,1)S(1)} %pad_maximum_fusion.2), channel_id=1, source_target_pairs={{0,16},{16,32},{32,48},{48,64},{64,80},{80,96},{96,112},{112,0},{1... | collective-permute-start | bytes 2752520 | tf_op jit(solution)/shard_map/ppermute | solution.py:89
  19.2 24.2 %collective-permute-start.5 = (bf16[512,896]{1,0:T(8,128)(2,1)S(1)}, bf16[512,896]{1,0:T(8,128)(2,1)S(1)}, u32[]{:S(2)}, u32[]{:S(2)}) collective-permute-start(bf16[512,896]{1,0:T(8,128)(2,1)S(1)} %pad_maximum_fusion.2), channel_id=1, source_target_pairs={{0,112},{16,0},{32,16},{48,32},{64,48},{80,64},{96,80},{112,96},{1... | collective-permute-start | bytes 2752520 | tf_op jit(solution)/shard_map/ppermute | solution.py:89
  23.2 10.0 %collective-permute-start.3 = (bf16[376,512]{1,0:T(8,128)(2,1)S(1)}, bf16[376,512]{1,0:T(8,128)(2,1)S(1)}, u32[]{:S(2)}, u32[]{:S(2)}) collective-permute-start(bf16[376,512]{1,0:T(8,128)(2,1)S(1)} %pad_maximum_fusion.5), channel_id=1, source_target_pairs={{0,8},{8,0},{1,9},{9,1},{2,10},{10,2},{3,11},{11,3},{4,12},{12,4},... | collective-permute-start | bytes 1155080 | tf_op jit(solution)/shard_map/ppermute | solution.py:19
  43.4 29.0 %collective-permute-start.12 = (bf16[376,1024]{1,0:T(8,128)(2,1)S(1)}, bf16[376,1024]{1,0:T(8,128)(2,1)S(1)}, u32[]{:S(2)}, u32[]{:S(2)}) collective-permute-start(bf16[376,1024]{1,0:T(8,128)(2,1)S(1)} %pad_maximum_fusion.4), channel_id=1, source_target_pairs={{0,128},{128,0},{1,129},{129,1},{2,130},{130,2},{3,131},{131,3},{4... | collective-permute-start | bytes 2310152 | tf_op jit(solution)/shard_map/ppermute | solution.py:19
  45.9 21.2 %collective-permute-start.6 = (bf16[256,768]{1,0:T(8,128)(2,1)S(1)}, bf16[256,768]{1,0:T(8,128)(2,1)S(1)}, u32[]{:S(2)}, u32[]{:S(2)}) collective-permute-start(bf16[256,768]{1,0:T(8,128)(2,1)S(1)} %get-tuple-element.79), channel_id=1, source_target_pairs={{0,1},{1,129},{128,0},{129,128},{2,3},{3,131},{130,2},{131,130},{4... | collective-permute-start | bytes 1179656 | tf_op jit(solution)/shard_map/ppermute | solution.py:109
  46.5 25.7 %collective-permute-start.7 = (bf16[256,768]{1,0:T(8,128)(2,1)S(1)}, bf16[256,768]{1,0:T(8,128)(2,1)S(1)}, u32[]{:S(2)}, u32[]{:S(2)}) collective-permute-start(bf16[256,768]{1,0:T(8,128)(2,1)S(1)} %get-tuple-element.80), channel_id=1, source_target_pairs={{0,0},{1,128},{128,1},{129,129},{2,2},{3,130},{130,3},{131,131},{4... | collective-permute-start | bytes 1179656 | tf_op jit(solution)/shard_map/ppermute | solution.py:108
  72.5 34.0 %collective-permute-start.13 = (bf16[2,376,1024]{2,1,0:T(8,128)(2,1)S(1)}, bf16[2,376,1024]{2,1,0:T(8,128)(2,1)S(1)}, u32[]{:S(2)}, u32[]{:S(2)}) collective-permute-start(bf16[2,376,1024]{2,1,0:T(8,128)(2,1)S(1)} %pad_maximum_fusion.here), channel_id=1, source_target_pairs={{0,2},{2,4},{4,6},{6,0},{1,3},{3,5},{5,7},{7,1},{8,10},{10,12},{12... | collective-permute-start | bytes 4620296 | tf_op jit(solution)/shard_map/ppermute | solution.py:44
  74.0 18.1 %collective-permute-start.8 = (bf16[512,768]{1,0:T(8,128)(2,1)S(1)}, bf16[512,768]{1,0:T(8,128)(2,1)S(1)}, u32[]{:S(2)}, u32[]{:S(2)}) collective-permute-start(bf16[512,768]{1,0:T(8,128)(2,1)S(1)} %pad_maximum_fusion.3), channel_id=1, source_target_pairs={{0,16},{16,32},{32,48},{48,64},{64,80},{80,96},{96,112},{112,0},{1... | collective-permute-start | bytes 2359304 | tf_op jit(solution)/shard_map/ppermute | solution.py:89
  74.1 18.0 %collective-permute-start.9 = (bf16[512,768]{1,0:T(8,128)(2,1)S(1)}, bf16[512,768]{1,0:T(8,128)(2,1)S(1)}, u32[]{:S(2)}, u32[]{:S(2)}) collective-permute-start(bf16[512,768]{1,0:T(8,128)(2,1)S(1)} %pad_maximum_fusion.3), channel_id=1, source_target_pairs={{0,112},{16,0},{32,16},{48,32},{64,48},{80,64},{96,80},{112,96},{1... | collective-permute-start | bytes 2359304 | tf_op jit(solution)/shard_map/ppermute | solution.py:89
  76.7 33.6 %collective-permute-start.14 = (bf16[2,376,1024]{2,1,0:T(8,128)(2,1)S(1)}, bf16[2,376,1024]{2,1,0:T(8,128)(2,1)S(1)}, u32[]{:S(2)}, u32[]{:S(2)}) collective-permute-start(bf16[2,376,1024]{2,1,0:T(8,128)(2,1)S(1)} %pad_maximum_fusion.here), channel_id=1, source_target_pairs={{0,6},{2,0},{4,2},{6,4},{1,7},{3,1},{5,3},{7,5},{8,14},{10,8},{12,... | collective-permute-start | bytes 4620296 | tf_op jit(solution)/shard_map/ppermute | solution.py:44
  93.0 38.6 %collective-permute-start.11 = (bf16[512,1664]{1,0:T(8,128)(2,1)}, bf16[512,1664]{1,0:T(8,128)(2,1)}, u32[]{:S(2)}, u32[]{:S(2)}) collective-permute-start(bf16[512,1664]{1,0:T(8,128)(2,1)} %constant_dynamic-update-slice_fusion.2), channel_id=1, source_target_pairs={{0,112},{16,0},{32,16},{48,32},{64,48},{80,64},{96,80},{112,96},{1... | collective-permute-start | bytes 5111816 | tf_op jit(solution)/shard_map/ppermute | solution.py:89
  97.0 39.0 %collective-permute-start.10 = (bf16[512,1664]{1,0:T(8,128)(2,1)}, bf16[512,1664]{1,0:T(8,128)(2,1)}, u32[]{:S(2)}, u32[]{:S(2)}) collective-permute-start(bf16[512,1664]{1,0:T(8,128)(2,1)} %constant_dynamic-update-slice_fusion), channel_id=1, source_target_pairs={{0,16},{16,32},{32,48},{48,64},{64,80},{80,96},{96,112},{112,0},{1... | collective-permute-start | bytes 5111816 | tf_op jit(solution)/shard_map/ppermute | solution.py:89
  107.5 31.2 %collective-permute-start.15 = (bf16[376,1024]{1,0:T(8,128)(2,1)}, bf16[376,1024]{1,0:T(8,128)(2,1)}, u32[]{:S(2)}, u32[]{:S(2)}) collective-permute-start(bf16[376,1024]{1,0:T(8,128)(2,1)} %slice_bitcast_fusion.1), channel_id=1, source_target_pairs={{0,2},{2,4},{4,6},{6,0},{1,3},{3,5},{5,7},{7,1},{8,10},{10,12},{12... | collective-permute-start | bytes 2310152 | tf_op jit(solution)/shard_map/ppermute | solution.py:44
  112.4 26.2 %collective-permute-start.16 = (bf16[376,1024]{1,0:T(8,128)(2,1)}, bf16[376,1024]{1,0:T(8,128)(2,1)}, u32[]{:S(2)}, u32[]{:S(2)}) collective-permute-start(bf16[376,1024]{1,0:T(8,128)(2,1)} %slice_bitcast_fusion), channel_id=1, source_target_pairs={{0,6},{2,0},{4,2},{6,4},{1,7},{3,1},{5,3},{7,5},{8,14},{10,8},{12,... | collective-permute-start | bytes 2310152 | tf_op jit(solution)/shard_map/ppermute | solution.py:44
  136.0 40.1 %collective-permute-start.17 = (bf16[512,1664]{1,0:T(8,128)(2,1)}, bf16[512,1664]{1,0:T(8,128)(2,1)}, u32[]{:S(2)}, u32[]{:S(2)}) collective-permute-start(bf16[512,1664]{1,0:T(8,128)(2,1)} %collective-permute-done.10), channel_id=1, source_target_pairs={{0,16},{16,32},{32,48},{48,64},{64,80},{80,96},{96,112},{112,0},{1... | collective-permute-start | bytes 5111816 | tf_op jit(solution)/shard_map/ppermute | solution.py:89
  136.0 40.1 %collective-permute-start.18 = (bf16[512,1664]{1,0:T(8,128)(2,1)}, bf16[512,1664]{1,0:T(8,128)(2,1)}, u32[]{:S(2)}, u32[]{:S(2)}) collective-permute-start(bf16[512,1664]{1,0:T(8,128)(2,1)} %collective-permute-done.11), channel_id=1, source_target_pairs={{0,112},{16,0},{32,16},{48,32},{64,48},{80,64},{96,80},{112,96},{1... | collective-permute-start | bytes 5111816 | tf_op jit(solution)/shard_map/ppermute | solution.py:89
  180.7 15.2 %collective-permute-start.19 = (bf16[256,1024]{1,0:T(8,128)(2,1)S(1)}, bf16[256,1024]{1,0:T(8,128)(2,1)S(1)}, u32[]{:S(2)}, u32[]{:S(2)}) collective-permute-start(bf16[256,1024]{1,0:T(8,128)(2,1)S(1)} %slice.125), channel_id=1, source_target_pairs={{0,16},{16,32},{32,48},{48,64},{64,80},{80,96},{96,112},{112,0},{1... | collective-permute-start | bytes 1572872 | tf_op jit(solution)/shard_map/ppermute | solution.py:89
  180.7 15.1 %collective-permute-start.20 = (bf16[256,1024]{1,0:T(8,128)(2,1)S(1)}, bf16[256,1024]{1,0:T(8,128)(2,1)S(1)}, u32[]{:S(2)}, u32[]{:S(2)}) collective-permute-start(bf16[256,1024]{1,0:T(8,128)(2,1)S(1)} %slice.126), channel_id=1, source_target_pairs={{0,112},{16,0},{32,16},{48,32},{64,48},{80,64},{96,80},{112,96},{1... | collective-permute-start | bytes 1572872 | tf_op jit(solution)/shard_map/ppermute | solution.py:89
  187.0 15.9 %collective-permute-start.21 = (bf16[256,640]{1,0:T(8,128)(2,1)S(1)}, bf16[256,640]{1,0:T(8,128)(2,1)S(1)}, u32[]{:S(2)}, u32[]{:S(2)}) collective-permute-start(bf16[256,640]{1,0:T(8,128)(2,1)S(1)} %slice.120), channel_id=1, source_target_pairs={{0,16},{16,32},{32,48},{48,64},{64,80},{80,96},{96,112},{112,0},{1... | collective-permute-start | bytes 983048 | tf_op jit(solution)/shard_map/ppermute | solution.py:89
  187.3 15.6 %collective-permute-start.22 = (bf16[256,640]{1,0:T(8,128)(2,1)S(1)}, bf16[256,640]{1,0:T(8,128)(2,1)S(1)}, u32[]{:S(2)}, u32[]{:S(2)}) collective-permute-start(bf16[256,640]{1,0:T(8,128)(2,1)S(1)} %slice.121), channel_id=1, source_target_pairs={{0,112},{16,0},{32,16},{48,32},{64,48},{80,64},{96,80},{112,96},{1... | collective-permute-start | bytes 983048 | tf_op jit(solution)/shard_map/ppermute | solution.py:89
  207.8 19.2 %collective-permute-start.24 = (bf16[376,1024]{1,0:T(8,128)(2,1)S(1)}, bf16[376,1024]{1,0:T(8,128)(2,1)S(1)}, u32[]{:S(2)}, u32[]{:S(2)}) collective-permute-start(bf16[376,1024]{1,0:T(8,128)(2,1)S(1)} %multiply_convert_fusion), channel_id=1, source_target_pairs={{0,0},{1,128},{128,129},{129,1},{2,2},{3,130},{130,131},{131,3},{4... | collective-permute-start | bytes 2310152 | tf_op jit(solution)/shard_map/ppermute | solution.py:122
  210.1 17.0 %collective-permute-start.26 = (bf16[376,640]{1,0:T(8,128)(2,1)S(1)}, bf16[376,640]{1,0:T(8,128)(2,1)S(1)}, u32[]{:S(2)}, u32[]{:S(2)}) collective-permute-start(bf16[376,640]{1,0:T(8,128)(2,1)S(1)} %multiply_convert_fusion.1), channel_id=1, source_target_pairs={{0,0},{1,128},{128,129},{129,1},{2,2},{3,130},{130,131},{131,3},{4... | collective-permute-start | bytes 1443848 | tf_op jit(solution)/shard_map/ppermute | solution.py:122
  (13 other events, 80.4 us)
